TPU v7x, 32 devices: a whole 2x2x4 slice. The times are simulated.
32 devices in a mesh: grp: 8 (over z, core), exp: 4 (over y, x).
Axes of the slice: x: 2, y: 2, z: 4, core: 2. Of those that a mesh axis runs over, the one named last changes fastest.
Arguments:
- hidden: bfloat16 [8, 16, 7168], P('grp', 'exp'), may hold values from -6 to 6
- norm_gain: float32 [7168], replicated, may hold values from 0.1 to 1.9
- route: int32 [8, 16, 1], P('grp', 'exp'), may hold values from 0 to 1; in each aligned block of 4 rows (0 to 3, 4 to 7, ..., all dimensions but the last counted through in order) at most 3 rows name the same one
- route_weight: float32 [8, 16], P('grp', 'exp'), may hold values from 0.2 to 1
- resident: bfloat16 [2, 2048, 7168], P(None, 'exp'), may hold values from -0.0625 to 0.0625
- sectioned: bfloat16 [8, 512, 7168], P('grp', 'exp'), may hold values from -0.1875 to 0.1875
- owner: int32 [8], replicated, may hold values from 0 to 7, each once
Outputs:
- moe_out: bfloat16 [8, 16, 7168], P('grp', 'exp')
Inputs may be any that keep to these rules, and one draw needn't show every extreme that they name: `route`: each row names one of the 2 experts. Among the 4 rows of one device at most 3 name the same expert, and in every draw some device has exactly 3 rows naming one expert. Every group number appears exactly once, so the 4 buckets have distinct owner groups.
All inputs are finite; a program needn't handle non-finite values.
Results may differ from a plain program's by a relative error of at most 0.0071.
Values may be sent and summed in bfloat16 or wider, within the bound.
No kernel may reach another device: no remote copies, remote signals or barrier semaphores. Data moves between devices by JAX's collectives and lax.ppermute only.
A program may use at most 64 MiB of HBM per device.

v0:
```python
import jax
import jax.numpy as jnp
from jax import lax
from jax.sharding import PartitionSpec as P

E_WIN = 2
BUCKETS = 4
CAP = 3


epsilon = 1e-06


def from_root(value, axis, source):
    kept = jnp.where(lax.axis_index(axis) == source, value, 0).astype(value.dtype)
    return lax.psum(kept, axis)


def activate(slot_rows, gate_up):
    gate_part = lax.dot_general(
        slot_rows, gate_up[0], (((1,), (1,)), ((), ())), preferred_element_type=jnp.float32
    )
    up_part = lax.dot_general(
        slot_rows, gate_up[1], (((1,), (1,)), ((), ())), preferred_element_type=jnp.float32
    )
    return (jax.nn.silu(gate_part) * up_part).astype(jnp.bfloat16)


def per_device(hidden, norm_gain, route, route_weight, resident, sectioned, owner):
    row_data = hidden[0].astype(jnp.float32)
    width = row_data.shape[1]
    row_count = row_data.shape[0]
    scale = lax.rsqrt(jnp.mean(row_data * row_data, axis=1, keepdims=True) + epsilon)
    normed = (row_data * scale * norm_gain[None, :]).astype(jnp.bfloat16)
    devices = lax.axis_size("exp")
    shards = devices // E_WIN
    expert_ids = route[0, :, 0]
    onehot = (expert_ids[:, None] == jnp.arange(E_WIN, dtype=jnp.int32)[None, :]).astype(jnp.int32)
    position = jnp.cumsum(onehot, axis=0) - onehot
    slot_index = jnp.sum(position * onehot, axis=1)
    placing = onehot[:, :, None] * (
        slot_index[:, None, None] == jnp.arange(CAP, dtype=jnp.int32)[None, None, :]
    ).astype(jnp.int32)
    placing = placing.reshape(row_count, E_WIN * CAP)
    packed = jnp.dot(
        placing.astype(jnp.bfloat16).T, normed, preferred_element_type=jnp.float32
    ).astype(jnp.bfloat16)
    packed = packed.reshape(E_WIN, 1, CAP, width)
    outgoing = jnp.broadcast_to(packed, (E_WIN, shards, CAP, width)).reshape(devices, CAP, width)
    piece_rows = sectioned.shape[1]
    arrived = lax.all_to_all(outgoing, "exp", split_axis=0, concat_axis=0, tiled=True)
    flat_slots = arrived.reshape(-1, width)
    activation = activate(flat_slots, resident)
    running_sum = jnp.zeros((flat_slots.shape[0], width), jnp.float32)
    for bucket in range(BUCKETS):
        weight_piece = from_root(sectioned[0], "grp", owner[bucket])
        act_piece = activation[:, bucket * piece_rows : (bucket + 1) * piece_rows]
        running_sum = running_sum + jnp.dot(
            act_piece, weight_piece, preferred_element_type=jnp.float32
        )
    partials = running_sum.astype(jnp.bfloat16).reshape(arrived.shape)
    returned = lax.all_to_all(partials, "exp", split_axis=0, concat_axis=0, tiled=True)
    summed = jnp.sum(returned.astype(jnp.float32).reshape(E_WIN, shards, CAP, width), axis=1)
    summed = summed.reshape(E_WIN * CAP, width)
    combined = jnp.dot(placing.astype(jnp.float32), summed, precision=lax.Precision.HIGHEST)
    result = (combined * route_weight[0][:, None]).astype(jnp.bfloat16)
    return result.reshape(1, row_count, width)


def solution(mesh):
    in_specs = (
        P("grp", "exp", None),
        P(),
        P("grp", "exp", None),
        P("grp", "exp"),
        P(None, "exp", None),
        P("grp", "exp", None),
        P(),
    )
    out_specs = P("grp", "exp", None)
    return jax.shard_map(
        per_device, mesh=mesh, in_specs=in_specs, out_specs=out_specs, check_vma=False
    )
```

profile of v0, /device:TPU:0, one launch (start us, length us, event | category | flops | bytes accessed | tf_op | source)
XLA Modules:
  0.0 195.6 jit_solution(9392328653723648736)
XLA Ops:
  6.5 0.0 all-reduce.3.cloned.1.call-start
  6.5 1.5 fusion.31
  10.5 4.6 %select_bitcast_fusion = (bf16[128,7168]{1,0:T(8,128)(2,1)}, bf16[128,7168]{1,0:T(8,128)(2,1)}, bf16[128,7168]{1,0:T(8,128)(2,1)}, bf16[128,7168]{1,0:T(8,128)(2,1)}) fusion(bf16[1,128,7168]{2,1,0:T(8,128)(2,1)} %param.12, pred[]{:T(512)S(6)} %eq.59, pred[]{:T(512)S(6)} %eq.57, pred[]{:T(512)S(6)} %eq.56, pred[]{:T(512)S(6)} %eq.58), kind=kLoop, calls=%fused_computation.15 | loop fusion | flops 3670016 | bytes 9175044 | tf_op jit(solution)/shard_map/jit(_where)/select_n | solution.py:15
  15.1 0.0 copy-start.4
  15.1 0.0 copy-start.3
  15.1 0.0 copy-start.6
  15.1 0.0 all-reduce.3.cloned.1.call-update
  15.1 0.6 copy-done.4
  15.8 0.1 fusion.29
  15.9 0.2 select_reduce_fusion
  16.1 0.1 fusion.30
  16.1 0.1 multiply_convert_fusion.1
  16.2 0.1 convert_element_type.64
  16.3 0.0 copy-done.3
  16.3 0.2 fusion.16
  16.5 0.0 copy-done.6
  16.5 0.2 convolution_convert_fusion
  16.7 0.1 broadcast_in_dim.20
  16.8 0.1 broadcast_in_dim.21
  16.9 10.6 %all_to_all.10 = bf16[4,3,7168]{2,1,0:T(4,128)(2,1)S(1)} all-to-all(bf16[4,3,7168]{2,1,0:T(4,128)(2,1)S(1)} %bitcast.49), channel_id=1, replica_groups=mesh['grp'=8,'exp'=4] {'exp'}, dimensions={0} | all-to-all | bytes 344064 | tf_op jit(solution)/shard_map/all_to_all | solution.py:51
  27.5 0.2 reshape.122
  27.7 5.2 %fusion.6 = f32[12,512]{1,0:T(8,128)S(1)} fusion(bf16[12,7168]{1,0:T(8,128)(2,1)S(1)} %reshape.122, bf16[2,512,7168]{2,1,0:T(8,128)(2,1)} %param.11), kind=kOutput, calls=%fused_computation.11 | convolution fusion | flops 88080384 | bytes 7536640 | tf_op jit(solution)/shard_map/dot_general | solution.py:20
  32.8 5.2 %fusion.13 = bf16[12,512]{1,0:T(8,128)(2,1)S(1)} fusion(bf16[12,7168]{1,0:T(8,128)(2,1)S(1)} %reshape.122, bf16[2,512,7168]{2,1,0:T(8,128)(2,1)} %param.11, f32[12,512]{1,0:T(8,128)S(1)} %fusion.6), kind=kOutput, calls=%fused_computation.20 | convolution fusion | flops 88117248 | bytes 7548928 | tf_op jit(solution)/shard_map/dot_general | solution.py:23
  38.0 135.8 %all-reduce.3.cloned.1.call-done = (bf16[128,7168]{1,0:T(8,128)(2,1)}, bf16[128,7168]{1,0:T(8,128)(2,1)}, bf16[128,7168]{1,0:T(8,128)(2,1)}, bf16[128,7168]{1,0:T(8,128)(2,1)}) async-done(((bf16[128,7168]{1,0:T(8,128)(2,1)}, bf16[128,7168]{1,0:T(8,128)(2,1)}, bf16[128,7168]{1,0:T(8,128)(2,1)}, bf16[128,7168]{1,0:T(8,128)(2,1)}), (bf16[128,7168]{1,0:T(8,128)(2,1)}, bf16[128,7168]{1,0:T(8,128)(2,1)}, ...) | async-done | bytes 7340048 | tf_op jit(solution)/shard_map/psum | solution.py:16
  173.9 0.0 copy-start.2
  173.9 2.0 %fusion.26 = f32[12,7168]{1,0:T(8,128)S(1)} fusion(bf16[128,7168]{1,0:T(8,128)(2,1)} %get-tuple-element.5, bf16[12,512]{1,0:T(8,128)(2,1)S(1)} %fusion.13), kind=kOutput, calls=%fused_computation.35 | convolution fusion | flops 22020096 | bytes 2183168 | tf_op jit(solution)/shard_map/dot_general | solution.py:58
  175.8 0.0 copy-start.1
  175.8 0.1 copy-done.2
  175.9 0.4 convolution_add_fusion.2
  176.3 0.0 copy-start
  176.3 1.1 copy-done.1
  177.4 0.4 convolution_add_fusion.1
  177.7 0.3 copy-done
  178.0 0.0 copy-start.5
  178.0 0.4 fusion
  178.4 0.1 reshape.123
  178.5 9.1 %all_to_all.11 = bf16[4,3,7168]{2,1,0:T(4,128)(2,1)S(1)} all-to-all(bf16[4,3,7168]{2,1,0:T(4,128)(2,1)S(1)} %reshape.123), channel_id=1, replica_groups=mesh['grp'=8,'exp'=4] {'exp'}, dimensions={0} | all-to-all | bytes 344064 | tf_op jit(solution)/shard_map/all_to_all | solution.py:62
  187.6 0.1 convert_reduce_fusion
  187.7 0.0 copy-done.5
  187.7 1.1 fusion.3
  (2 shorter events, 0.0 us)
Async XLA Ops:
  6.5 167.3 %all-reduce.3.cloned.1.call-start = ((), (), s32[]{:S(2)}) async-start(), calls=%async_computation.2 | async-start | bytes 14680064 | tf_op jit(solution)/shard_map/psum | solution.py:16
  15.1 0.7 copy-start.4
  15.1 1.2 copy-start.3
  15.1 1.4 copy-start.6
  173.9 2.1 %copy-start.2 = (bf16[128,7168]{1,0:T(8,128)(2,1)S(1)}, bf16[128,7168]{1,0:T(8,128)(2,1)}, u32[]{:S(2)}) copy-start(bf16[128,7168]{1,0:T(8,128)(2,1)} %get-tuple-element.6) | copy-start | bytes 5505028
  175.8 1.5 copy-start.1
  176.3 1.7 copy-start
  178.0 9.7 %copy-start.5 = (f32[1,4]{1,0:T(1,128)S(1)}, f32[1,4]{1,0:T(1,128)}, u32[]{:S(2)}) copy-start(f32[1,4]{1,0:T(1,128)} %param.10) | copy-start | bytes 52
Sparse Core Ops, SparseCore 0:
  15.3 158.5 all-reduce.2
where the time goes:
time: 196 us
  waiting for transfers between devices  136 us (69%)
  blocking collectives  19.7 us (10%)
  between operations  15.9 us (8%)
  matrix products  14.7 us (8%)
  other arithmetic  5.38 us (3%)
  local copies, waits for them, and re-layouts  4.03 us (2%)
    psum x1, waiting for transfers between devices, from_root(): return lax.psum(kept, axis)  136 us
    all_to_all x1, blocking collectives, per_device(): lax.all_to_all(outgoing, 'exp', split_axis=0, concat_axis=0, tiled=True)  10.6 us
    all_to_all x1, blocking collectives, per_device(): lax.all_to_all(partials, 'exp', split_axis=0, concat_axis=0, tiled=True)  9.08 us
    dot_general x1, matrix products, activate(): lax.dot_general(slot_rows, gate_up[1], (((1,), (1,)), ((), ())), preferre...  5.18 us
    dot_general x1, matrix products, activate(): lax.dot_general(slot_rows, gate_up[0], (((1,), (1,)), ((), ())), preferre...  5.16 us
    select_n x1, other arithmetic, from_root(): jnp.where(lax.axis_index(axis) == source, value, 0).astype(value.dtype)  4.63 us
  transfers between devices with their start and end apart: 1, of which 1 were waited for; matrix products, arithmetic and copies ran while one was open for 6% of the time, Pallas kernels for 0%

commit v1 on v0

--- a/solution.py
+++ b/solution.py
@@ -6,6 +6,7 @@
 E_WIN = 2
 BUCKETS = 4
 CAP = 3
+PAIR = 2
 
 
 epsilon = 1e-06
@@ -26,12 +27,15 @@
     return (jax.nn.silu(gate_part) * up_part).astype(jnp.bfloat16)
 
 
-def per_device(hidden, norm_gain, route, route_weight, resident, sectioned, owner):
-    row_data = hidden[0].astype(jnp.float32)
-    width = row_data.shape[1]
-    row_count = row_data.shape[0]
+def normalize(rows, norm_gain):
+    row_data = rows.astype(jnp.float32)
     scale = lax.rsqrt(jnp.mean(row_data * row_data, axis=1, keepdims=True) + epsilon)
-    normed = (row_data * scale * norm_gain[None, :]).astype(jnp.bfloat16)
+    return (row_data * scale * norm_gain[None, :]).astype(jnp.bfloat16)
+
+
+def move_weights(hidden, norm_gain, route, route_weight, resident, sectioned, owner):
+    normed = normalize(hidden[0], norm_gain)
+    row_count, width = normed.shape
     devices = lax.axis_size("exp")
     shards = devices // E_WIN
     expert_ids = route[0, :, 0]
@@ -67,6 +71,55 @@
     return result.reshape(1, row_count, width)
 
 
+def swap(value, axis, bits):
+    size = lax.axis_size(axis)
+    return lax.ppermute(value, axis, [(i, i ^ bits) for i in range(size)])
+
+
+def move_rows(hidden, norm_gain, route, route_weight, resident, sectioned, owner):
+    rows = hidden[0]
+    row_count, width = rows.shape
+    devices = lax.axis_size("exp")
+    chips = lax.axis_size("grp") // PAIR
+    shards = devices // E_WIN
+    me, group = lax.axis_index("exp"), lax.axis_index("grp")
+    piece = sectioned.shape[1]
+    own_piece = sectioned[0]
+    other_piece = swap(own_piece, "grp", 1)
+    arrived = []
+    for bits in range(devices):
+        expert = (me ^ bits) // shards
+        kept = jnp.where(route[0] == expert, rows, 0).astype(rows.dtype)
+        arrived.append(swap(kept, "exp", bits) if bits else kept)
+    normed = normalize(jnp.concatenate(arrived, axis=0), norm_gain)
+    activation = activate(normed, resident)
+    along = [activation] + [swap(activation, "grp", PAIR * hop) for hop in range(1, chips)]
+    acts = jnp.stack(along).reshape(chips, devices, row_count, BUCKETS, piece)
+    acts = jnp.transpose(acts, (1, 0, 2, 3, 4)).reshape(-1, BUCKETS, piece)
+    partial = 0.0
+    for held_by, weights in ((group, own_piece), (group ^ 1, other_piece)):
+        mine = (owner[:BUCKETS] == held_by)[None, :, None]
+        picked = jnp.sum(jnp.where(mine, acts, 0).astype(jnp.float32), axis=1).astype(jnp.bfloat16)
+        partial = partial + jnp.dot(picked, weights, preferred_element_type=jnp.float32)
+    partial = partial.astype(jnp.bfloat16).reshape(devices, chips * row_count, width)
+    total = partial[0].astype(jnp.float32)
+    for bits in range(1, devices):
+        total = total + swap(partial[bits], "exp", bits).astype(jnp.float32)
+    total = total.astype(jnp.bfloat16).reshape(chips, row_count, width)
+    combined = total[0].astype(jnp.float32)
+    for hop in range(1, chips):
+        combined = combined + swap(total[hop], "grp", PAIR * hop).astype(jnp.float32)
+    result = (combined * route_weight[0][:, None]).astype(jnp.bfloat16)
+    return result.reshape(1, row_count, width)
+
+
+def per_device(hidden, norm_gain, route, route_weight, resident, sectioned, owner):
+    weight_rows = BUCKETS * sectioned.shape[1]
+    partial_rows = lax.axis_size("exp") * lax.axis_size("grp") // PAIR * hidden.shape[1]
+    plan = move_rows if partial_rows < weight_rows else move_weights
+    return plan(hidden, norm_gain, route, route_weight, resident, sectioned, owner)
+
+
 def solution(mesh):
     in_specs = (
         P("grp", "exp", None),

time: 196 us -> 53.3 us (0.27)
  waiting for transfers between devices: 136 us -> 20.2 us
  blocking collectives: 19.7 us -> 0 us
  starting transfers between devices: 0.01 us -> 16.1 us
  between operations: 15.9 us -> 0.13 us
  local copies, waits for them, and re-layouts: 4.03 us -> 0.25 us
  matrix products: 14.7 us -> 12.7 us
    psum x1 -> x0, waiting for transfers between devices: 136 us -> none  [from_root(): return lax.psum(kept, axis)]
    ppermute x0 -> x13, waiting for transfers between devices: none -> 20.2 us  [swap(): return lax.ppermute(value, axis, [(i, i ^ bits) for i in range(size)])]
    all_to_all x2 -> x0, blocking collectives: 19.7 us -> none  [the longest x1 10.6 us: per_device(): lax.all_to_all(outgoing, 'exp', split_axis=0, concat_axis=0, tiled=True)]
    ppermute x0 -> x13, starting transfers between devices: none -> 16.1 us  [swap(): return lax.ppermute(value, axis, [(i, i ^ bits) for i in range(size)])]
    select_n x1, other arithmetic: 4.63 us -> 0.97 us  [move_rows(): kept = jnp.where(route[0] == expert, rows, 0).astype(rows.dtype)]
    dot_general x6 -> x2, matrix products: 4.37 us -> 2.34 us  [move_rows(): jnp.dot(picked, weights, preferred_element_type=jnp.float32)]
    unnamed x14 -> x9, local copies, waits for them, and re-layouts: 2.09 us -> 0.05 us
  transfers between devices with their start and end apart: 1 -> 13, of which waited for: 1 -> 10; matrix products, arithmetic and copies ran while one was open for 6% -> 23% of each run, Pallas kernels for 0% -> 0%
where the time goes in v1:
time: 53.3 us; the launch traced here: 53.1 us
  waiting for transfers between devices  20.2 us (38%)
  starting transfers between devices  16.1 us (30%)
  matrix products  12.7 us (24%)
  other arithmetic  3.65 us (7%)
    ppermute x13, waiting for transfers between devices, swap(): return lax.ppermute(value, axis, [(i, i ^ bits) for i in range(size)])  20.2 us
    ppermute x13, starting transfers between devices, swap(): return lax.ppermute(value, axis, [(i, i ^ bits) for i in range(size)])  16.1 us
    dot_general x1, matrix products, activate(): lax.dot_general(slot_rows, gate_up[1], (((1,), (1,)), ((), ())), preferre...  5.24 us
    dot_general x1, matrix products, activate(): lax.dot_general(slot_rows, gate_up[0], (((1,), (1,)), ((), ())), preferre...  5.11 us
    dot_general x2, matrix products, move_rows(): jnp.dot(picked, weights, preferred_element_type=jnp.float32)  2.34 us
  transfers between devices with their start and end apart: 13, of which 10 were waited for; matrix products, arithmetic and copies ran while one was open for 23% of the time, Pallas kernels for 0%

profile of v1, /device:TPU:0, one launch (start us, length us, event | category | flops | bytes accessed | tf_op | source)
XLA Modules:
  0.0 53.1 jit_solution(17695495339691110607)
XLA Ops:
  0.0 0.7 %compare_bitcast_fusion.3 = (pred[4]{0:T(512)(128)(4,1)S(1)}, pred[4]{0:T(512)(128)(4,1)S(1)}, pred[4]{0:T(512)(128)(4,1)S(1)}, pred[4]{0:T(512)(128)(4,1)S(1)}) fusion(s32[1,4,1]{1,2,0:T(1,128)} %param.9, s32[]{:T(128)S(6)} %select_n.38, s32[]{:T(128)S(6)} %select_n.40, s32[]{:T(128)S(6)} %select_n.44, s32[]{:T(128)S(6)} %select_n.42), kind=kLoop, calls=%fused_computation.32 | loop fusion | flops 16 | bytes 48 | tf_op jit(solution)/shard_map/eq | solution.py:92
  0.7 1.0 %bitcast_select_fusion.3 = (bf16[4,7168]{1,0:T(4,128)(2,1)S(1)}, bf16[4,7168]{1,0:T(4,128)(2,1)S(1)}, bf16[4,7168]{1,0:T(4,128)(2,1)S(1)}, bf16[4,7168]{1,0:T(4,128)(2,1)S(1)}) fusion(bf16[1,4,7168]{2,1,0:T(4,128)(2,1)} %param.7, pred[4]{0:T(512)(128)(4,1)S(1)} %get-tuple-element.19, pred[4]{0:T(512)(128)(4,1)S(1)} %get-tuple-element.20, ...), kind=kLoop, calls=%fused_computation.24 | loop fusion | flops 114688 | bytes 286736 | tf_op jit(solution)/shard_map/jit(_where)/select_n | solution.py:92
  1.6 3.0 %collective-permute-start = (bf16[4,7168]{1,0:T(4,128)(2,1)S(1)}, bf16[4,7168]{1,0:T(4,128)(2,1)S(1)}, u32[]{:S(2)}, u32[]{:S(2)}) collective-permute-start(bf16[4,7168]{1,0:T(4,128)(2,1)S(1)} %get-tuple-element.14), channel_id=1, source_target_pairs={{0,1},{1,0},{2,3},{3,2},{4,5},{5,4},{6,7},{7,6},{8,9},{9,8},{10,11... | collective-permute-start | bytes 172040 | tf_op jit(solution)/shard_map/ppermute | solution.py:76
  4.7 1.5 %collective-permute-start.1 = (bf16[4,7168]{1,0:T(4,128)(2,1)S(1)}, bf16[4,7168]{1,0:T(4,128)(2,1)S(1)}, u32[]{:S(2)}, u32[]{:S(2)}) collective-permute-start(bf16[4,7168]{1,0:T(4,128)(2,1)S(1)} %get-tuple-element.15), channel_id=1, source_target_pairs={{0,2},{1,3},{2,0},{3,1},{4,6},{5,7},{6,4},{7,5},{8,10},{9,11},{10,... | collective-permute-start | bytes 172040 | tf_op jit(solution)/shard_map/ppermute | solution.py:76
  6.2 0.0 collective-permute-start.2
  6.2 0.0 collective-permute-start.6
  6.2 0.7 %slice_compare_fusion.1 = (pred[4]{0:T(512)(128)(4,1)S(1)}, pred[4]{0:T(512)(128)(4,1)S(1)}) fusion(s32[8]{0:T(128)} %param.13, s32[]{:T(128)S(6)} %axis_index.23, s32[]{:T(128)S(6)} %xor.15), kind=kLoop, calls=%fused_computation.35 | loop fusion | flops 8 | bytes 32 | tf_op jit(solution)/shard_map/eq | solution.py:101
  6.9 0.0 collective-permute-done
  6.9 2.0 %collective-permute-done.1 = bf16[4,7168]{1,0:T(4,128)(2,1)S(1)} collective-permute-done((bf16[4,7168]{1,0:T(4,128)(2,1)S(1)}, bf16[4,7168]{1,0:T(4,128)(2,1)S(1)}, u32[]{:S(2)}, u32[]{:S(2)}) %collective-permute-start.1) | collective-permute-done | bytes 57376 | tf_op jit(solution)/shard_map/ppermute | solution.py:76
  8.8 2.4 %collective-permute-done.2 = bf16[4,7168]{1,0:T(4,128)(2,1)S(1)} collective-permute-done((bf16[4,7168]{1,0:T(4,128)(2,1)S(1)}, bf16[4,7168]{1,0:T(4,128)(2,1)S(1)}, u32[]{:S(2)}, u32[]{:S(2)}) %collective-permute-start.2) | collective-permute-done | bytes 57376 | tf_op jit(solution)/shard_map/ppermute | solution.py:76
  11.3 0.3 fusion.13
  11.5 0.0 copy-start.2
  11.5 5.1 %fusion.3 = f32[16,512]{1,0:T(8,128)S(1)} fusion(bf16[2,512,7168]{2,1,0:T(8,128)(2,1)} %param.11, f32[7168]{0:T(1024)} %param.8, f32[16]{0:T(128)S(1)} %add_rsqrt_fusion, bf16[4,7168]{1,0:T(4,128)(2,1)S(1)} %collective-permute-done.2, bf16[4,7168]{1,0:T(4,128)(2,1)S(1)} %collective-permute-done.1, bf16[4,7168]{1,0:T(4,128)(2,1)S(1)} %collective-permute-done, ...), kind=kOutput, calls=%fused_computation.4 | convolution fusion | flops 118702080 | bytes 7630912 | tf_op jit(solution)/shard_map/dot_general | solution.py:21
  16.7 0.0 copy-done.2
  16.7 0.0 copy-start
  16.7 5.2 %fusion.10 = bf16[16,512]{1,0:T(8,128)(2,1)S(1)} fusion(bf16[2,512,7168]{2,1,0:T(8,128)(2,1)} %param.11, f32[7168]{0:T(1024)S(1)} %copy-done.2, f32[16]{0:T(128)S(1)} %add_rsqrt_fusion, f32[16,512]{1,0:T(8,128)S(1)} %fusion.3, bf16[4,7168]{1,0:T(4,128)(2,1)S(1)} %collective-permute-done.2, bf16[4,7168]{1,0:T(4,128)(2,1)S(1)} %collective-permute-done.1, ...), kind=kOutput, calls=%fused_computation.9 | convolution fusion | flops 118751232 | bytes 7647296 | tf_op jit(solution)/shard_map/dot_general | solution.py:24
  21.9 3.7 %collective-permute-start.5 = (bf16[16,512]{1,0:T(8,128)(2,1)S(1)}, bf16[16,512]{1,0:T(8,128)(2,1)S(1)}, u32[]{:S(2)}, u32[]{:S(2)}) collective-permute-start(bf16[16,512]{1,0:T(8,128)(2,1)S(1)} %fusion.10), channel_id=1, source_target_pairs={{0,24},{4,28},{8,16},{12,20},{16,8},{20,12},{24,0},{28,4},{1,25},{... | collective-permute-start | bytes 49160 | tf_op jit(solution)/shard_map/ppermute | solution.py:76
  25.6 0.0 collective-permute-start.4
  25.6 0.8 %collective-permute-start.3 = (bf16[16,512]{1,0:T(8,128)(2,1)S(1)}, bf16[16,512]{1,0:T(8,128)(2,1)S(1)}, u32[]{:S(2)}, u32[]{:S(2)}) collective-permute-start(bf16[16,512]{1,0:T(8,128)(2,1)S(1)} %fusion.10), channel_id=1, source_target_pairs={{0,8},{4,12},{8,0},{12,4},{16,24},{20,28},{24,16},{28,20},{1,9},{5... | collective-permute-start | bytes 49160 | tf_op jit(solution)/shard_map/ppermute | solution.py:76
  26.4 1.1 %collective-permute-done.5 = bf16[16,512]{1,0:T(8,128)(2,1)S(1)} collective-permute-done((bf16[16,512]{1,0:T(8,128)(2,1)S(1)}, bf16[16,512]{1,0:T(8,128)(2,1)S(1)}, u32[]{:S(2)}, u32[]{:S(2)}) %collective-permute-start.5) | collective-permute-done | bytes 16416 | tf_op jit(solution)/shard_map/ppermute | solution.py:76
  27.5 2.7 %collective-permute-done.4 = bf16[16,512]{1,0:T(8,128)(2,1)S(1)} collective-permute-done((bf16[16,512]{1,0:T(8,128)(2,1)S(1)}, bf16[16,512]{1,0:T(8,128)(2,1)S(1)}, u32[]{:S(2)}, u32[]{:S(2)}) %collective-permute-start.4) | collective-permute-done | bytes 16416 | tf_op jit(solution)/shard_map/ppermute | solution.py:76
  30.2 0.0 collective-permute-done.3
  30.3 0.3 select_reduce_fusion
  30.6 0.0 copy-done
  30.6 0.4 fusion.19
  31.0 0.0 collective-permute-done.6
  31.0 1.9 %fusion = bf16[64,7168]{1,0:T(8,128)(2,1)S(1)} fusion(f32[64,7168]{1,0:T(8,128)S(1)} %fusion.19, bf16[64,128]{1,0:T(8,128)(2,1)S(1)} %bitcast.37, bf16[128,7168]{1,0:T(8,128)(2,1)} %collective-permute-done.6), kind=kOutput, calls=%fused_computation.1 | convolution fusion | flops 118358016 | bytes 4603904 | tf_op jit(solution)/shard_map/dot_general | solution.py:103
  33.0 0.0 copy-start.1
  33.1 0.6 %collective-permute-start.7 = (bf16[16,7168]{1,0:T(8,128)(2,1)S(1)}, bf16[16,7168]{1,0:T(8,128)(2,1)S(1)}, u32[]{:S(2)}, u32[]{:S(2)}) collective-permute-start(bf16[16,7168]{1,0:T(8,128)(2,1)S(1)} %get-tuple-element.7), channel_id=1, source_target_pairs={{0,1},{1,0},{2,3},{3,2},{4,5},{5,4},{6,7},{7,6},{8,9},{9,8},{10,11... | collective-permute-start | bytes 688136 | tf_op jit(solution)/shard_map/ppermute | solution.py:76
  33.7 1.4 %collective-permute-start.9 = (bf16[16,7168]{1,0:T(8,128)(2,1)S(1)}, bf16[16,7168]{1,0:T(8,128)(2,1)S(1)}, u32[]{:S(2)}, u32[]{:S(2)}) collective-permute-start(bf16[16,7168]{1,0:T(8,128)(2,1)S(1)} %get-tuple-element.8), channel_id=1, source_target_pairs={{0,3},{1,2},{2,1},{3,0},{4,7},{5,6},{6,5},{7,4},{8,11},{9,10},{10,... | collective-permute-start | bytes 688136 | tf_op jit(solution)/shard_map/ppermute | solution.py:76
  35.1 1.5 %collective-permute-start.8 = (bf16[16,7168]{1,0:T(8,128)(2,1)S(1)}, bf16[16,7168]{1,0:T(8,128)(2,1)S(1)}, u32[]{:S(2)}, u32[]{:S(2)}) collective-permute-start(bf16[16,7168]{1,0:T(8,128)(2,1)S(1)} %get-tuple-element.9), channel_id=1, source_target_pairs={{0,2},{1,3},{2,0},{3,1},{4,6},{5,7},{6,4},{7,5},{8,10},{9,11},{10,... | collective-permute-start | bytes 688136 | tf_op jit(solution)/shard_map/ppermute | solution.py:76
  36.6 3.5 %collective-permute-done.7 = bf16[16,7168]{1,0:T(8,128)(2,1)S(1)} collective-permute-done((bf16[16,7168]{1,0:T(8,128)(2,1)S(1)}, bf16[16,7168]{1,0:T(8,128)(2,1)S(1)}, u32[]{:S(2)}, u32[]{:S(2)}) %collective-permute-start.7) | collective-permute-done | bytes 229408 | tf_op jit(solution)/shard_map/ppermute | solution.py:76
  40.1 2.5 %collective-permute-done.9 = bf16[16,7168]{1,0:T(8,128)(2,1)S(1)} collective-permute-done((bf16[16,7168]{1,0:T(8,128)(2,1)S(1)}, bf16[16,7168]{1,0:T(8,128)(2,1)S(1)}, u32[]{:S(2)}, u32[]{:S(2)}) %collective-permute-start.9) | collective-permute-done | bytes 229408 | tf_op jit(solution)/shard_map/ppermute | solution.py:76
  42.7 1.3 %collective-permute-done.8 = bf16[16,7168]{1,0:T(8,128)(2,1)S(1)} collective-permute-done((bf16[16,7168]{1,0:T(8,128)(2,1)S(1)}, bf16[16,7168]{1,0:T(8,128)(2,1)S(1)}, u32[]{:S(2)}, u32[]{:S(2)}) %collective-permute-start.8) | collective-permute-done | bytes 229408 | tf_op jit(solution)/shard_map/ppermute | solution.py:76
  44.0 0.1 add_convert_fusion
  44.1 0.1 fusion.22
  44.2 0.1 collective-permute-start.10
  44.3 3.0 %collective-permute-start.12 = (bf16[4,7168]{1,0:T(4,128)(2,1)S(1)}, bf16[4,7168]{1,0:T(4,128)(2,1)S(1)}, u32[]{:S(2)}, u32[]{:S(2)}) collective-permute-start(bf16[4,7168]{1,0:T(4,128)(2,1)S(1)} %get-tuple-element.11), channel_id=1, source_target_pairs={{0,24},{4,28},{8,16},{12,20},{16,8},{20,12},{24,0},{28,4},{1,25},{... | collective-permute-start | bytes 172040 | tf_op jit(solution)/shard_map/ppermute | solution.py:76
  47.3 0.4 collective-permute-start.11
  47.7 0.7 %collective-permute-done.10 = bf16[4,7168]{1,0:T(4,128)(2,1)S(1)} collective-permute-done((bf16[4,7168]{1,0:T(4,128)(2,1)S(1)}, bf16[4,7168]{1,0:T(4,128)(2,1)S(1)}, u32[]{:S(2)}, u32[]{:S(2)}) %collective-permute-start.10) | collective-permute-done | bytes 57376 | tf_op jit(solution)/shard_map/ppermute | solution.py:76
  48.4 2.0 %collective-permute-done.12 = bf16[4,7168]{1,0:T(4,128)(2,1)S(1)} collective-permute-done((bf16[4,7168]{1,0:T(4,128)(2,1)S(1)}, bf16[4,7168]{1,0:T(4,128)(2,1)S(1)}, u32[]{:S(2)}, u32[]{:S(2)}) %collective-permute-start.12) | collective-permute-done | bytes 57376 | tf_op jit(solution)/shard_map/ppermute | solution.py:76
  50.4 2.0 %collective-permute-done.11 = bf16[4,7168]{1,0:T(4,128)(2,1)S(1)} collective-permute-done((bf16[4,7168]{1,0:T(4,128)(2,1)S(1)}, bf16[4,7168]{1,0:T(4,128)(2,1)S(1)}, u32[]{:S(2)}, u32[]{:S(2)}) %collective-permute-start.11) | collective-permute-done | bytes 57376 | tf_op jit(solution)/shard_map/ppermute | solution.py:76
  52.4 0.0 copy-done.1
  52.4 0.7 %fusion.16 = bf16[1,4,7168]{2,1,0:T(4,128)(2,1)} fusion(bf16[4,7168]{1,0:T(4,128)(2,1)S(1)} %collective-permute-done.12, bf16[4,7168]{1,0:T(4,128)(2,1)S(1)} %collective-permute-done.11, bf16[4,7168]{1,0:T(4,128)(2,1)S(1)} %collective-permute-done.10, bf16[16,7168]{1,0:T(8,128)(2,1)S(1)} %add_convert_fusion, f32[4]{0:T(128)S(1)} %bitcast.41), kind=kLoop, calls=%fused_computation.20 | loop fusion | flops 258048 | bytes 286736 | tf_op jit(solution)/shard_map/reshape | solution.py:113
  (12 shorter events, 0.2 us)
Async XLA Ops:
  1.6 5.2 %collective-permute-start = (bf16[4,7168]{1,0:T(4,128)(2,1)S(1)}, bf16[4,7168]{1,0:T(4,128)(2,1)S(1)}, u32[]{:S(2)}, u32[]{:S(2)}) collective-permute-start(bf16[4,7168]{1,0:T(4,128)(2,1)S(1)} %get-tuple-element.14), channel_id=1, source_target_pairs={{0,1},{1,0},{2,3},{3,2},{4,5},{5,4},{6,7},{7,6},{8,9},{9,8},{10,11... | collective-permute-start | bytes 172040 | tf_op jit(solution)/shard_map/ppermute | solution.py:76
  4.7 4.2 %collective-permute-start.1 = (bf16[4,7168]{1,0:T(4,128)(2,1)S(1)}, bf16[4,7168]{1,0:T(4,128)(2,1)S(1)}, u32[]{:S(2)}, u32[]{:S(2)}) collective-permute-start(bf16[4,7168]{1,0:T(4,128)(2,1)S(1)} %get-tuple-element.15), channel_id=1, source_target_pairs={{0,2},{1,3},{2,0},{3,1},{4,6},{5,7},{6,4},{7,5},{8,10},{9,11},{10,... | collective-permute-start | bytes 172040 | tf_op jit(solution)/shard_map/ppermute | solution.py:76
  6.2 5.1 %collective-permute-start.2 = (bf16[4,7168]{1,0:T(4,128)(2,1)S(1)}, bf16[4,7168]{1,0:T(4,128)(2,1)S(1)}, u32[]{:S(2)}, u32[]{:S(2)}) collective-permute-start(bf16[4,7168]{1,0:T(4,128)(2,1)S(1)} %get-tuple-element.16), channel_id=1, source_target_pairs={{0,3},{1,2},{2,1},{3,0},{4,7},{5,6},{6,5},{7,4},{8,11},{9,10},{10,... | collective-permute-start | bytes 172040 | tf_op jit(solution)/shard_map/ppermute | solution.py:76
  6.2 24.8 %collective-permute-start.6 = (bf16[128,7168]{1,0:T(8,128)(2,1)}, bf16[128,7168]{1,0:T(8,128)(2,1)}, u32[]{:S(2)}, u32[]{:S(2)}) collective-permute-start(bf16[128,7168]{1,0:T(8,128)(2,1)} %bitcast.36), channel_id=1, source_target_pairs={{0,4},{4,0},{8,12},{12,8},{16,20},{20,16},{24,28},{28,24},{1,5},{5... | collective-permute-start | bytes 5505032 | tf_op jit(solution)/shard_map/ppermute | solution.py:76
  11.5 5.1 %copy-start.2 = (f32[7168]{0:T(1024)S(1)}, f32[7168]{0:T(1024)}, u32[]{:S(2)}) copy-start(f32[7168]{0:T(1024)} %param.8) | copy-start | bytes 86020
  16.7 14.0 %copy-start = (bf16[1,128,7168]{2,1,0:T(8,128)(2,1)S(1)}, bf16[1,128,7168]{2,1,0:T(8,128)(2,1)}, u32[]{:S(2)}) copy-start(bf16[1,128,7168]{2,1,0:T(8,128)(2,1)} %param.12) | copy-start | bytes 5505028
  21.9 5.6 %collective-permute-start.5 = (bf16[16,512]{1,0:T(8,128)(2,1)S(1)}, bf16[16,512]{1,0:T(8,128)(2,1)S(1)}, u32[]{:S(2)}, u32[]{:S(2)}) collective-permute-start(bf16[16,512]{1,0:T(8,128)(2,1)S(1)} %fusion.10), channel_id=1, source_target_pairs={{0,24},{4,28},{8,16},{12,20},{16,8},{20,12},{24,0},{28,4},{1,25},{... | collective-permute-start | bytes 49160 | tf_op jit(solution)/shard_map/ppermute | solution.py:76
  25.6 4.6 %collective-permute-start.4 = (bf16[16,512]{1,0:T(8,128)(2,1)S(1)}, bf16[16,512]{1,0:T(8,128)(2,1)S(1)}, u32[]{:S(2)}, u32[]{:S(2)}) collective-permute-start(bf16[16,512]{1,0:T(8,128)(2,1)S(1)} %fusion.10), channel_id=1, source_target_pairs={{0,16},{4,20},{8,24},{12,28},{16,0},{20,4},{24,8},{28,12},{1,17},{... | collective-permute-start | bytes 49160 | tf_op jit(solution)/shard_map/ppermute | solution.py:76
  25.6 4.7 %collective-permute-start.3 = (bf16[16,512]{1,0:T(8,128)(2,1)S(1)}, bf16[16,512]{1,0:T(8,128)(2,1)S(1)}, u32[]{:S(2)}, u32[]{:S(2)}) collective-permute-start(bf16[16,512]{1,0:T(8,128)(2,1)S(1)} %fusion.10), channel_id=1, source_target_pairs={{0,8},{4,12},{8,0},{12,4},{16,24},{20,28},{24,16},{28,20},{1,9},{5... | collective-permute-start | bytes 49160 | tf_op jit(solution)/shard_map/ppermute | solution.py:76
  33.0 19.4 %copy-start.1 = (f32[1,4]{1,0:T(1,128)S(1)}, f32[1,4]{1,0:T(1,128)}, u32[]{:S(2)}) copy-start(f32[1,4]{1,0:T(1,128)} %param.10) | copy-start | bytes 52
  33.1 7.1 %collective-permute-start.7 = (bf16[16,7168]{1,0:T(8,128)(2,1)S(1)}, bf16[16,7168]{1,0:T(8,128)(2,1)S(1)}, u32[]{:S(2)}, u32[]{:S(2)}) collective-permute-start(bf16[16,7168]{1,0:T(8,128)(2,1)S(1)} %get-tuple-element.7), channel_id=1, source_target_pairs={{0,1},{1,0},{2,3},{3,2},{4,5},{5,4},{6,7},{7,6},{8,9},{9,8},{10,11... | collective-permute-start | bytes 688136 | tf_op jit(solution)/shard_map/ppermute | solution.py:76
  33.7 9.0 %collective-permute-start.9 = (bf16[16,7168]{1,0:T(8,128)(2,1)S(1)}, bf16[16,7168]{1,0:T(8,128)(2,1)S(1)}, u32[]{:S(2)}, u32[]{:S(2)}) collective-permute-start(bf16[16,7168]{1,0:T(8,128)(2,1)S(1)} %get-tuple-element.8), channel_id=1, source_target_pairs={{0,3},{1,2},{2,1},{3,0},{4,7},{5,6},{6,5},{7,4},{8,11},{9,10},{10,... | collective-permute-start | bytes 688136 | tf_op jit(solution)/shard_map/ppermute | solution.py:76
  35.1 8.9 %collective-permute-start.8 = (bf16[16,7168]{1,0:T(8,128)(2,1)S(1)}, bf16[16,7168]{1,0:T(8,128)(2,1)S(1)}, u32[]{:S(2)}, u32[]{:S(2)}) collective-permute-start(bf16[16,7168]{1,0:T(8,128)(2,1)S(1)} %get-tuple-element.9), channel_id=1, source_target_pairs={{0,2},{1,3},{2,0},{3,1},{4,6},{5,7},{6,4},{7,5},{8,10},{9,11},{10,... | collective-permute-start | bytes 688136 | tf_op jit(solution)/shard_map/ppermute | solution.py:76
  44.2 4.2 %collective-permute-start.10 = (bf16[4,7168]{1,0:T(4,128)(2,1)S(1)}, bf16[4,7168]{1,0:T(4,128)(2,1)S(1)}, u32[]{:S(2)}, u32[]{:S(2)}) collective-permute-start(bf16[4,7168]{1,0:T(4,128)(2,1)S(1)} %get-tuple-element.10), channel_id=1, source_target_pairs={{0,8},{4,12},{8,0},{12,4},{16,24},{20,28},{24,16},{28,20},{1,9},{5... | collective-permute-start | bytes 172040 | tf_op jit(solution)/shard_map/ppermute | solution.py:76
  44.3 6.1 %collective-permute-start.12 = (bf16[4,7168]{1,0:T(4,128)(2,1)S(1)}, bf16[4,7168]{1,0:T(4,128)(2,1)S(1)}, u32[]{:S(2)}, u32[]{:S(2)}) collective-permute-start(bf16[4,7168]{1,0:T(4,128)(2,1)S(1)} %get-tuple-element.11), channel_id=1, source_target_pairs={{0,24},{4,28},{8,16},{12,20},{16,8},{20,12},{24,0},{28,4},{1,25},{... | collective-permute-start | bytes 172040 | tf_op jit(solution)/shard_map/ppermute | solution.py:76
  47.3 5.1 %collective-permute-start.11 = (bf16[4,7168]{1,0:T(4,128)(2,1)S(1)}, bf16[4,7168]{1,0:T(4,128)(2,1)S(1)}, u32[]{:S(2)}, u32[]{:S(2)}) collective-permute-start(bf16[4,7168]{1,0:T(4,128)(2,1)S(1)} %get-tuple-element.12), channel_id=1, source_target_pairs={{0,16},{4,20},{8,24},{12,28},{16,0},{20,4},{24,8},{28,12},{1,17},{... | collective-permute-start | bytes 172040 | tf_op jit(solution)/shard_map/ppermute | solution.py:76

commit v2 on v1

--- a/solution.py
+++ b/solution.py
@@ -1,6 +1,10 @@
+import functools
+
 import jax
 import jax.numpy as jnp
 from jax import lax
+from jax.experimental import pallas as pl
+from jax.experimental.pallas import tpu as pltpu
 from jax.sharding import PartitionSpec as P
 
 E_WIN = 2
@@ -76,39 +80,205 @@
     return lax.ppermute(value, axis, [(i, i ^ bits) for i in range(size)])
 
 
+NT = (((1,), (1,)), ((), ()))
+VMEM = pl.BlockSpec(memory_space=pltpu.VMEM)
+SMEM = pl.BlockSpec(memory_space=pltpu.SMEM)
+ANY = pl.BlockSpec(memory_space=pl.ANY)
+
+
+def pack_body(chips, shards, gain_ref, *refs):
+    rows, routes, blocks, line = refs[:chips], refs[chips : 2 * chips], refs[2 * chips : -1], refs[-1]
+    row_count, width = rows[0].shape
+    half = width // 2
+    block = 2 * CAP * chips
+    height = E_WIN * block
+    mine = lax.axis_index("exp") // shards
+    at = lax.broadcasted_iota(jnp.int32, (height, row_count), 0)
+    at_expert, at_slot = at // block, (at % block) // (2 * chips)
+    at_half, at_chip = (at % (2 * chips)) // chips, at % chips
+    total = jnp.zeros((height, half), jnp.float32)
+    for chip in range(chips):
+        line[...] = jnp.full(line.shape, -1, jnp.int32)
+        line[0:1, 0:row_count] = routes[chip][...]
+        named = line[...]
+        position = jnp.zeros(named.shape, jnp.int32)
+        for back in range(1, row_count):
+            position = position + (named == pltpu.roll(named, back, 1)).astype(jnp.int32)
+        named, position = named[0:1, 0:row_count], position[0:1, 0:row_count]
+        wanted = (at_chip == chip) & (at_slot == position) & ((mine ^ at_expert) == named)
+        for part in range(2):
+            placing = jnp.where(wanted & (at_half == part), 1.0, 0.0).astype(jnp.bfloat16)
+            total = total + jnp.dot(
+                placing,
+                rows[chip][:, part * half : (part + 1) * half],
+                preferred_element_type=jnp.float32,
+            )
+    squares = jnp.broadcast_to(jnp.sum(total * total, axis=1, keepdims=True), (height, 128))
+    first = (lax.broadcasted_iota(jnp.int32, (height, 128), 0) % (2 * chips)) < chips
+    partner = jnp.where(first, pltpu.roll(squares, height - chips, 0), pltpu.roll(squares, chips, 0))
+    scale = lax.rsqrt((squares + partner) * (1.0 / width) + epsilon)[:, 0:1]
+    upper = (lax.broadcasted_iota(jnp.int32, (height, half), 0) % (2 * chips)) < chips
+    gain = jnp.where(upper, gain_ref[:, :half], gain_ref[:, half:])
+    normed = total * scale * gain
+    for expert in range(E_WIN):
+        blocks[expert][...] = normed[expert * block : (expert + 1) * block].astype(jnp.bfloat16)
+
+
+def fetch_body(piece, owner_ref, resident, own, other, after, both, down, held, sems):
+    group = lax.axis_index("grp")
+    copies = []
+    for which, holder in enumerate((group, group ^ 1)):
+        bucket, has = jnp.int32(0), jnp.int32(0)
+        for index in range(BUCKETS):
+            hit = owner_ref[index] == holder
+            bucket, has = jnp.where(hit, index, bucket), jnp.where(hit, 1, has)
+        here = pl.ds(which * piece, piece)
+        for part in range(2):
+            copies.append(
+                pltpu.make_async_copy(
+                    resident.at[part, pl.ds(pl.multiple_of(bucket * piece, piece), piece)],
+                    both.at[part, here],
+                    sems.at[3 * which + part],
+                )
+            )
+        copies.append(
+            pltpu.make_async_copy((own, other)[which], down.at[here], sems.at[3 * which + 2])
+        )
+        held[here, :] = jnp.broadcast_to(has.astype(jnp.float32), (piece, held.shape[1]))
+    for copy in copies:
+        copy.start()
+    for copy in copies:
+        copy.wait()
+
+
+def expert_body(devices, chips, lanes, both, down, held, *refs):
+    blocks, partials, stacked = refs[:devices], refs[devices : 2 * devices], refs[-1]
+    block, half = blocks[0].shape
+    used = devices * block
+    for index in range(devices):
+        stacked[index * block : (index + 1) * block, :] = blocks[index][...]
+    if lanes > used:
+        stacked[used:, :] = jnp.zeros((lanes - used, half), jnp.bfloat16)
+    sums = []
+    for part in range(2):
+        upper = lax.dot_general(
+            both[part, :, :half], stacked[...], NT, preferred_element_type=jnp.float32
+        )
+        lower = lax.dot_general(
+            both[part, :, half:], stacked[...], NT, preferred_element_type=jnp.float32
+        )
+        sums.append(upper + pltpu.roll(lower, lanes - chips, 1))
+    column = lax.broadcasted_iota(jnp.int32, sums[0].shape, 1)
+    valid = ((column % (2 * chips)) < chips) & (column < used)
+    act = sums[0] * jax.nn.sigmoid(sums[0]) * sums[1]
+    act = jnp.where(valid & (held[...] > 0.5), act, 0.0)
+    above = act.T.astype(jnp.bfloat16)[:used]
+    below = pltpu.roll(act, chips, 1).T.astype(jnp.bfloat16)[:used]
+    step = half // 7 if half % (7 * 128) == 0 else half
+    for start in range(0, half, step):
+        out = jnp.dot(above, down[:, start : start + step], preferred_element_type=jnp.float32)
+        out = out + jnp.dot(
+            below, down[:, half + start : half + start + step], preferred_element_type=jnp.float32
+        )
+        for index in range(devices):
+            partials[index][:, start : start + step] = out[
+                index * block : (index + 1) * block
+            ].astype(jnp.bfloat16)
+
+
+def combine_body(devices, chips, shards, placing, *refs):
+    blocks, outs = refs[:devices], refs[devices:]
+    half = blocks[0].shape[1]
+    row_count = outs[0].shape[0]
+    for part in range(2):
+        total = 0.0
+        for index in range(devices):
+            total = total + jnp.dot(
+                placing[2 * (index // shards) + part],
+                blocks[index][...],
+                preferred_element_type=jnp.float32,
+            )
+        for chip in range(chips):
+            outs[chip][:, part * half : (part + 1) * half] = total[
+                chip * row_count : (chip + 1) * row_count
+            ].astype(outs[chip].dtype)
+
+
 def move_rows(hidden, norm_gain, route, route_weight, resident, sectioned, owner):
     rows = hidden[0]
     row_count, width = rows.shape
     devices = lax.axis_size("exp")
     chips = lax.axis_size("grp") // PAIR
     shards = devices // E_WIN
-    me, group = lax.axis_index("exp"), lax.axis_index("grp")
+    half, block = width // 2, 2 * CAP * chips
     piece = sectioned.shape[1]
-    own_piece = sectioned[0]
-    other_piece = swap(own_piece, "grp", 1)
-    arrived = []
-    for bits in range(devices):
-        expert = (me ^ bits) // shards
-        kept = jnp.where(route[0] == expert, rows, 0).astype(rows.dtype)
-        arrived.append(swap(kept, "exp", bits) if bits else kept)
-    normed = normalize(jnp.concatenate(arrived, axis=0), norm_gain)
-    activation = activate(normed, resident)
-    along = [activation] + [swap(activation, "grp", PAIR * hop) for hop in range(1, chips)]
-    acts = jnp.stack(along).reshape(chips, devices, row_count, BUCKETS, piece)
-    acts = jnp.transpose(acts, (1, 0, 2, 3, 4)).reshape(-1, BUCKETS, piece)
-    partial = 0.0
-    for held_by, weights in ((group, own_piece), (group ^ 1, other_piece)):
-        mine = (owner[:BUCKETS] == held_by)[None, :, None]
-        picked = jnp.sum(jnp.where(mine, acts, 0).astype(jnp.float32), axis=1).astype(jnp.bfloat16)
-        partial = partial + jnp.dot(picked, weights, preferred_element_type=jnp.float32)
-    partial = partial.astype(jnp.bfloat16).reshape(devices, chips * row_count, width)
-    total = partial[0].astype(jnp.float32)
-    for bits in range(1, devices):
-        total = total + swap(partial[bits], "exp", bits).astype(jnp.float32)
-    total = total.astype(jnp.bfloat16).reshape(chips, row_count, width)
-    combined = total[0].astype(jnp.float32)
+    mine = lax.axis_index("exp") // shards
+    routes = [route[0].reshape(1, row_count)]
+    gathered = [rows]
     for hop in range(1, chips):
-        combined = combined + swap(total[hop], "grp", PAIR * hop).astype(jnp.float32)
+        gathered.append(swap(rows, "grp", PAIR * hop))
+    for hop in range(1, chips):
+        routes.append(swap(routes[0], "grp", PAIR * hop))
+    other_piece = swap(sectioned[0], "grp", 1)
+    half_block = jax.ShapeDtypeStruct((block, half), jnp.bfloat16)
+    packed = pl.pallas_call(
+        functools.partial(pack_body, chips, shards),
+        out_shape=[half_block] * E_WIN,
+        in_specs=[VMEM] * (1 + 2 * chips),
+        out_specs=[VMEM] * E_WIN,
+        scratch_shapes=[pltpu.VMEM((8, 128), jnp.int32)],
+        name="pack",
+    )(norm_gain.reshape(1, width), *gathered, *routes)
+    blocks = [packed[bits // shards] for bits in range(devices)]
+    blocks = [blocks[0]] + [swap(blocks[bits], "exp", bits) for bits in range(1, devices)]
+    both, down, held = pl.pallas_call(
+        functools.partial(fetch_body, piece),
+        out_shape=[
+            jax.ShapeDtypeStruct((2, PAIR * piece, width), jnp.bfloat16),
+            jax.ShapeDtypeStruct((PAIR * piece, width), jnp.bfloat16),
+            jax.ShapeDtypeStruct((PAIR * piece, 128), jnp.float32),
+        ],
+        in_specs=[SMEM, ANY, ANY, ANY, ANY],
+        out_specs=[VMEM] * 3,
+        scratch_shapes=[pltpu.SemaphoreType.DMA((3 * PAIR,))],
+        name="fetch",
+    )(owner, resident, sectioned[0], other_piece, packed[0])
+    named = jnp.concatenate(routes, axis=0)
+    seen = [
+        sum([(named[:, r] == named[:, b]).astype(jnp.int32) for b in range(r)], jnp.zeros((chips,), jnp.int32))
+        for r in range(row_count)
+    ]
+    position = jnp.stack(seen, axis=1)
+    chip_of = jnp.arange(chips, dtype=jnp.int32)[:, None]
+    column = jnp.arange(block, dtype=jnp.int32)[None, None, :]
+    placing = []
+    for expert in range(E_WIN):
+        for part in range(2):
+            target = (position * 2 + part) * chips + chip_of
+            chosen = (named == (mine ^ expert))[:, :, None] & (column == target[:, :, None])
+            placing.append(chosen.astype(jnp.bfloat16).reshape(chips * row_count, block))
+    placing = jnp.stack(placing)
+    lanes = -(-devices * block // 128) * 128
+    partials = pl.pallas_call(
+        functools.partial(expert_body, devices, chips, lanes),
+        out_shape=[half_block] * devices,
+        in_specs=[VMEM] * (3 + devices),
+        out_specs=[VMEM] * devices,
+        scratch_shapes=[pltpu.VMEM((lanes, half), jnp.bfloat16)],
+        name="expert",
+    )(both, down, held, *blocks)
+    returned = [partials[0]] + [swap(partials[bits], "exp", bits) for bits in range(1, devices)]
+    home = jax.ShapeDtypeStruct((row_count, width), jnp.bfloat16)
+    sums = pl.pallas_call(
+        functools.partial(combine_body, devices, chips, shards),
+        out_shape=[home] * chips,
+        in_specs=[VMEM] * (1 + devices),
+        out_specs=[VMEM] * chips,
+        name="combine",
+    )(placing, *returned)
+    combined = sums[0].astype(jnp.float32)
+    for hop in range(1, chips):
+        combined = combined + swap(sums[hop], "grp", PAIR * hop).astype(jnp.float32)
     result = (combined * route_weight[0][:, None]).astype(jnp.bfloat16)
     return result.reshape(1, row_count, width)
 

time: 53.3 us -> 64.5 us (1.21)
  Pallas kernels: 0 us -> 22.2 us
  matrix products: 12.7 us -> 0 us
  waiting for transfers between devices: 20.2 us -> 12.9 us
  starting transfers between devices: 16.1 us -> 21.4 us
  local copies, waits for them, and re-layouts: 0.25 us -> 3.76 us
    pallas_call x0 -> x4, Pallas kernels: none -> 22.2 us  [the longest x1 9.01 us: move_rows(): pl.pallas_call(functools.partial(fetch_body, piece), out_shape=[jax.Shape...]
    dot_general x4 -> x0, matrix products: 12.7 us -> none  [the longest x1 5.24 us: activate(): lax.dot_general(slot_rows, gate_up[1], (((1,), (1,)), ((), ())), preferre...]
    ppermute x13 -> x16, waiting for transfers between devices: 20.2 us -> 12.9 us  [swap(): return lax.ppermute(value, axis, [(i, i ^ bits) for i in range(size)])]
    ppermute x13 -> x16, starting transfers between devices: 16.1 us -> 21.4 us  [swap(): return lax.ppermute(value, axis, [(i, i ^ bits) for i in range(size)])]
    unnamed x9 -> x28, local copies, waits for them, and re-layouts: 0.05 us -> 3.33 us
    select_n x1 -> x0, other arithmetic: 0.97 us -> none  [move_rows(): kept = jnp.where(route[0] == expert, rows, 0).astype(rows.dtype)]
    reshape x1, other arithmetic: 0.71 us -> 1.53 us  [move_rows(): return result.reshape(1, row_count, width)]
    another operation x0 -> x3, other arithmetic: none -> 0.76 us  [the longest x1 0.61 us: move_rows(): placing = jnp.stack(placing)]
  transfers between devices with their start and end apart: 13 -> 16, of which waited for: 10 -> 8; matrix products, arithmetic and copies ran while one was open for 23% -> 4% of each run, Pallas kernels for 0% -> 18%
where the time goes in v2:
time: 64.5 us; the launch traced here: 64.2 us
  Pallas kernels  22.2 us (34%)
  starting transfers between devices  21.4 us (33%)
  waiting for transfers between devices  12.9 us (20%)
  other arithmetic  3.81 us (6%)
  local copies, waits for them, and re-layouts  3.76 us (6%)
    ppermute x16, starting transfers between devices, swap(): return lax.ppermute(value, axis, [(i, i ^ bits) for i in range(size)])  21.4 us
    ppermute x16, waiting for transfers between devices, swap(): return lax.ppermute(value, axis, [(i, i ^ bits) for i in range(size)])  12.9 us
    pallas_call x1, Pallas kernels, move_rows(): pl.pallas_call(functools.partial(fetch_body, piece), out_shape=[jax.Shape...  9.01 us
    pallas_call x1, Pallas kernels, move_rows(): pl.pallas_call(functools.partial(expert_body, devices, chips, lanes), out...  8.09 us
    unnamed x28, local copies, waits for them, and re-layouts  3.33 us
    pallas_call x1, Pallas kernels, move_rows(): pl.pallas_call(functools.partial(pack_body, chips, shards), out_shape=[ha...  2.83 us
    pallas_call x1, Pallas kernels, move_rows(): pl.pallas_call(functools.partial(combine_body, devices, chips, shards), o...  2.27 us
    reshape x1, other arithmetic, move_rows(): return result.reshape(1, row_count, width)  1.53 us
  transfers between devices with their start and end apart: 16, of which 8 were waited for; matrix products, arithmetic and copies ran while one was open for 4% of the time, Pallas kernels for 18%

profile of v2, /device:TPU:0, one launch (start us, length us, event | category | flops | bytes accessed | tf_op | source)
XLA Modules:
  0.0 64.2 jit_solution(14144849975908651528)
XLA Ops:
  0.0 0.5 collective-permute-start.3
  0.5 2.6 %collective-permute-start = (s32[1,4]{1,0:T(1,128)}, s32[1,4]{1,0:T(1,128)S(1)}, u32[]{:S(2)}, u32[]{:S(2)}) collective-permute-start(s32[1,4]{1,0:T(1,128)} %bitcast.28), channel_id=1, source_target_pairs={{0,8},{4,12},{8,0},{12,4},{16,24},{20,28},{24,16},{28,20},{1,9},{5... | collective-permute-start | bytes 56 | tf_op jit(solution)/shard_map/ppermute | solution.py:80
  3.1 2.6 %collective-permute-start.1 = (s32[1,4]{1,0:T(1,128)}, s32[1,4]{1,0:T(1,128)S(1)}, u32[]{:S(2)}, u32[]{:S(2)}) collective-permute-start(s32[1,4]{1,0:T(1,128)} %bitcast.29), channel_id=1, source_target_pairs={{0,16},{4,20},{8,24},{12,28},{16,0},{20,4},{24,8},{28,12},{1,17},{... | collective-permute-start | bytes 56 | tf_op jit(solution)/shard_map/ppermute | solution.py:80
  5.6 0.0 collective-permute-start.2
  5.6 0.9 %collective-permute-start.4 = (bf16[4,7168]{1,0:T(4,128)(2,1)}, bf16[4,7168]{1,0:T(4,128)(2,1)S(1)}, u32[]{:S(2)}, u32[]{:S(2)}) collective-permute-start(bf16[4,7168]{1,0:T(4,128)(2,1)} %bitcast.23), channel_id=1, source_target_pairs={{0,8},{4,12},{8,0},{12,4},{16,24},{20,28},{24,16},{28,20},{1,9},{5... | collective-permute-start | bytes 172040 | tf_op jit(solution)/shard_map/ppermute | solution.py:80
  6.6 0.1 add.71
  6.6 0.0 collective-permute-done.refs_5_
  6.6 3.5 %collective-permute-start.5 = (bf16[4,7168]{1,0:T(4,128)(2,1)}, bf16[4,7168]{1,0:T(4,128)(2,1)S(1)}, u32[]{:S(2)}, u32[]{:S(2)}) collective-permute-start(bf16[4,7168]{1,0:T(4,128)(2,1)} %bitcast.24), channel_id=1, source_target_pairs={{0,16},{4,20},{8,24},{12,28},{16,0},{20,4},{24,8},{28,12},{1,17},{... | collective-permute-start | bytes 172040 | tf_op jit(solution)/shard_map/ppermute | solution.py:80
  10.2 0.0 collective-permute-done.1.refs_6_
  10.2 0.0 collective-permute-start.6
  10.2 1.1 %collective-permute-done.2.refs_7_ = s32[1,4]{1,0:T(1,128)S(1)} collective-permute-done((s32[1,4]{1,0:T(1,128)}, s32[1,4]{1,0:T(1,128)S(1)}, u32[]{:S(2)}, u32[]{:S(2)}) %collective-permute-start.2) | collective-permute-done | bytes 48 | tf_op jit(solution)/shard_map/ppermute | solution.py:80
  11.3 0.7 %pad_add_fusion.1 = s32[4,4]{1,0:T(4,128)S(1)} fusion(s32[1,4]{1,0:T(1,128)S(1)} %collective-permute-done.2.refs_7_, s32[1,4]{1,0:T(1,128)S(1)} %collective-permute-done.1.refs_6_, s32[1,4]{1,0:T(1,128)S(1)} %collective-permute-done.refs_5_, s32[1,4]{1,0:T(1,128)} %bitcast.31), kind=kLoop, calls=%fused_computation.12 | loop fusion | flops 48 | bytes 128 | tf_op jit(solution)/shard_map/concatenate | solution.py:246
  11.9 0.1 convert_bitcast_fusion
  12.0 0.1 add_bitcast_fusion.1
  12.1 0.1 broadcast_multiply_fusion
  12.2 0.7 %compare_reduce_fusion.1 = (pred[4,4]{1,0:T(4,128)(4,1)S(1)}, pred[4,4]{1,0:T(4,128)(4,1)S(1)}) fusion(s32[]{:T(128)S(6)} %select_n.5, s32[]{:T(128)S(6)} %xor.4, s32[1,4,1]{1,2,0:T(1,128)S(1)} %bitcast.35, s32[1,4,1]{1,2,0:T(1,128)S(1)} %bitcast.34, s32[1,4,1]{1,2,0:T(1,128)S(1)} %bitcast.33, s32[1,4,1]{1,2,0:T(1,128)} %param.9), kind=kLoop, calls=%fused_computation.10 | loop fusion | flops 80 | bytes 104 | tf_op jit(solution)/shard_map/eq | solution.py:258
  12.8 0.1 eq.118
  12.9 0.1 eq.133
  13.0 0.1 mul.50
  13.1 0.1 mul.47
  13.2 0.0 collective-permute-done.4.refs_1_
  13.2 0.5 collective-permute-done.5.refs_2_
  13.7 2.7 %collective-permute-done.6.refs_3_ = bf16[4,7168]{1,0:T(4,128)(2,1)S(1)} collective-permute-done((bf16[4,7168]{1,0:T(4,128)(2,1)}, bf16[4,7168]{1,0:T(4,128)(2,1)S(1)}, u32[]{:S(2)}, u32[]{:S(2)}) %collective-permute-start.6) | collective-permute-done | bytes 57376 | tf_op jit(solution)/shard_map/ppermute | solution.py:80
  16.4 0.0 copy-done.10
  16.4 0.0 copy-done.11
  16.4 0.0 copy-done.12
  16.4 0.0 copy-done.7
  16.4 0.0 copy-done.8
  16.4 0.6 copy-done.9
  17.0 2.8 %pack.1 = (bf16[24,3584]{1,0:T(8,128)(2,1)}, bf16[24,3584]{1,0:T(8,128)(2,1)}) custom-call(f32[1,7168]{1,0:T(1,128)} %bitcast.27, bf16[4,7168]{1,0:T(4,128)(2,1)} %bitcast.26, bf16[4,7168]{1,0:T(4,128)(2,1)} %copy-done.7, bf16[4,7168]{1,0:T(4,128)(2,1)} %copy-done.8, bf16[4,7168]{1,0:T(4,128)(2,1)} %copy-done.9, s32[1,4]{1,0:T(1,128)} %bitcast.32, ...), custom_call_target="tpu_custom_call" | custom-call | tf_op jit(solution)/shard_map/pack/pallas_call | solution.py:224
  19.8 1.5 %collective-permute-start.8 = (bf16[24,3584]{1,0:T(8,128)(2,1)}, bf16[24,3584]{1,0:T(8,128)(2,1)S(1)}, u32[]{:S(2)}, u32[]{:S(2)}) collective-permute-start(bf16[24,3584]{1,0:T(8,128)(2,1)} %get-tuple-element.22), channel_id=1, source_target_pairs={{0,2},{1,3},{2,0},{3,1},{4,6},{5,7},{6,4},{7,5},{8,10},{9,11},{10,... | collective-permute-start | bytes 516104 | tf_op jit(solution)/shard_map/ppermute | solution.py:80
  21.3 1.4 %collective-permute-start.9 = (bf16[24,3584]{1,0:T(8,128)(2,1)}, bf16[24,3584]{1,0:T(8,128)(2,1)S(1)}, u32[]{:S(2)}, u32[]{:S(2)}) collective-permute-start(bf16[24,3584]{1,0:T(8,128)(2,1)} %get-tuple-element.22), channel_id=1, source_target_pairs={{0,3},{1,2},{2,1},{3,0},{4,7},{5,6},{6,5},{7,4},{8,11},{9,10},{10,... | collective-permute-start | bytes 516104 | tf_op jit(solution)/shard_map/ppermute | solution.py:80
  22.8 0.5 collective-permute-start.7
  23.3 0.0 collective-permute-done.3.other
  23.3 1.3 %copy-done = bf16[128,7168]{1,0:T(8,128)(2,1)} copy-done((bf16[128,7168]{1,0:T(8,128)(2,1)}, bf16[128,7168]{1,0:T(8,128)(2,1)S(1)}, u32[]{:S(2)}) %copy-start) | copy-done | bytes 1835032
  24.6 9.0 %fetch.1 = (bf16[2,256,7168]{2,1,0:T(8,128)(2,1)}, bf16[256,7168]{1,0:T(8,128)(2,1)}, f32[256,128]{1,0:T(8,128)}) custom-call(s32[8]{0:T(128)} %owner_ref.1, bf16[2,512,7168]{2,1,0:T(8,128)(2,1)} %resident.1, bf16[128,7168]{1,0:T(8,128)(2,1)} %bitcast.22, bf16[128,7168]{1,0:T(8,128)(2,1)} %copy-done, bf16[24,3584]{1,0:T(8,128)(2,1)} %get-tuple-element.18.after.refs_0_), custom_call_target="tpu_custom_call" | custom-call | tf_op jit(solution)/shard_map/fetch/pallas_call | solution.py:234
  33.6 0.0 collective-permute-done.7.refs_1_
  33.7 0.0 copy-start.6
  33.7 0.0 collective-permute-done.8.refs_2_
  33.7 0.0 copy-start.4
  33.7 0.0 collective-permute-done.9.refs_3_
  33.7 0.0 copy-start.5
  33.7 0.6 copy-done.6
  34.3 0.1 copy-done.4
  34.4 0.1 copy-done.5
  34.5 8.1 %expert.1 = (bf16[24,3584]{1,0:T(8,128)(2,1)}, bf16[24,3584]{1,0:T(8,128)(2,1)}, bf16[24,3584]{1,0:T(8,128)(2,1)}, bf16[24,3584]{1,0:T(8,128)(2,1)}) custom-call(bf16[2,256,7168]{2,1,0:T(8,128)(2,1)} %get-tuple-element.19.both, bf16[256,7168]{1,0:T(8,128)(2,1)} %get-tuple-element.20.down, f32[256,128]{1,0:T(8,128)} %get-tuple-element.21.held, ...), custom_call_target="tpu_custom_call" | custom-call | tf_op jit(solution)/shard_map/expert/pallas_call | solution.py:262
  42.5 1.5 %collective-permute-start.10 = (bf16[24,3584]{1,0:T(8,128)(2,1)}, bf16[24,3584]{1,0:T(8,128)(2,1)S(1)}, u32[]{:S(2)}, u32[]{:S(2)}) collective-permute-start(bf16[24,3584]{1,0:T(8,128)(2,1)} %get-tuple-element.24), channel_id=1, source_target_pairs={{0,1},{1,0},{2,3},{3,2},{4,5},{5,4},{6,7},{7,6},{8,9},{9,8},{10,11... | collective-permute-start | bytes 516104 | tf_op jit(solution)/shard_map/ppermute | solution.py:80
  44.0 1.5 %collective-permute-start.11 = (bf16[24,3584]{1,0:T(8,128)(2,1)}, bf16[24,3584]{1,0:T(8,128)(2,1)S(1)}, u32[]{:S(2)}, u32[]{:S(2)}) collective-permute-start(bf16[24,3584]{1,0:T(8,128)(2,1)} %get-tuple-element.25), channel_id=1, source_target_pairs={{0,2},{1,3},{2,0},{3,1},{4,6},{5,7},{6,4},{7,5},{8,10},{9,11},{10,... | collective-permute-start | bytes 516104 | tf_op jit(solution)/shard_map/ppermute | solution.py:80
  45.5 0.5 collective-permute-start.12
  46.0 0.1 fusion.4
  46.1 0.6 add_convert_fusion.placing
  46.7 2.0 %collective-permute-done.10.refs_1_ = bf16[24,3584]{1,0:T(8,128)(2,1)S(1)} collective-permute-done((bf16[24,3584]{1,0:T(8,128)(2,1)}, bf16[24,3584]{1,0:T(8,128)(2,1)S(1)}, u32[]{:S(2)}, u32[]{:S(2)}) %collective-permute-start.10) | collective-permute-done | bytes 172064 | tf_op jit(solution)/shard_map/ppermute | solution.py:80
  48.7 2.0 %collective-permute-done.11.refs_2_ = bf16[24,3584]{1,0:T(8,128)(2,1)S(1)} collective-permute-done((bf16[24,3584]{1,0:T(8,128)(2,1)}, bf16[24,3584]{1,0:T(8,128)(2,1)S(1)}, u32[]{:S(2)}, u32[]{:S(2)}) %collective-permute-start.11) | collective-permute-done | bytes 172064 | tf_op jit(solution)/shard_map/ppermute | solution.py:80
  50.7 1.4 %collective-permute-done.12.refs_3_ = bf16[24,3584]{1,0:T(8,128)(2,1)S(1)} collective-permute-done((bf16[24,3584]{1,0:T(8,128)(2,1)}, bf16[24,3584]{1,0:T(8,128)(2,1)S(1)}, u32[]{:S(2)}, u32[]{:S(2)}) %collective-permute-start.12) | collective-permute-done | bytes 172064 | tf_op jit(solution)/shard_map/ppermute | solution.py:80
  52.1 0.0 copy-done.1
  52.1 0.7 %copy-done.3 = bf16[24,3584]{1,0:T(8,128)(2,1)} copy-done((bf16[24,3584]{1,0:T(8,128)(2,1)}, bf16[24,3584]{1,0:T(8,128)(2,1)S(1)}, u32[]{:S(2)}) %copy-start.3) | copy-done | bytes 172056
  52.7 2.3 %combine.1 = (bf16[4,7168]{1,0:T(4,128)(2,1)}, bf16[4,7168]{1,0:T(4,128)(2,1)}, bf16[4,7168]{1,0:T(4,128)(2,1)}, bf16[4,7168]{1,0:T(4,128)(2,1)}) custom-call(bf16[4,16,24]{2,1,0:T(8,128)(2,1)} %add_convert_fusion.placing, bf16[24,3584]{1,0:T(8,128)(2,1)} %get-tuple-element.23.refs_0_, bf16[24,3584]{1,0:T(8,128)(2,1)} %copy-done.1, ...), custom_call_target="tpu_custom_call" | custom-call | tf_op jit(solution)/shard_map/combine/pallas_call | solution.py:272
  55.0 0.0 collective-permute-start.13
  55.0 1.5 %collective-permute-start.14 = (bf16[4,7168]{1,0:T(4,128)(2,1)}, bf16[4,7168]{1,0:T(4,128)(2,1)S(1)}, u32[]{:S(2)}, u32[]{:S(2)}) collective-permute-start(bf16[4,7168]{1,0:T(4,128)(2,1)} %get-tuple-element.29), channel_id=1, source_target_pairs={{0,16},{4,20},{8,24},{12,28},{16,0},{20,4},{24,8},{28,12},{1,17},{... | collective-permute-start | bytes 172040 | tf_op jit(solution)/shard_map/ppermute | solution.py:80
  56.5 2.9 %collective-permute-start.15 = (bf16[4,7168]{1,0:T(4,128)(2,1)}, bf16[4,7168]{1,0:T(4,128)(2,1)S(1)}, u32[]{:S(2)}, u32[]{:S(2)}) collective-permute-start(bf16[4,7168]{1,0:T(4,128)(2,1)} %get-tuple-element.30), channel_id=1, source_target_pairs={{0,24},{4,28},{8,16},{12,20},{16,8},{20,12},{24,0},{28,4},{1,25},{... | collective-permute-start | bytes 172040 | tf_op jit(solution)/shard_map/ppermute | solution.py:80
  59.4 0.0 collective-permute-done.13
  59.4 0.9 %collective-permute-done.14 = bf16[4,7168]{1,0:T(4,128)(2,1)S(1)} collective-permute-done((bf16[4,7168]{1,0:T(4,128)(2,1)}, bf16[4,7168]{1,0:T(4,128)(2,1)S(1)}, u32[]{:S(2)}, u32[]{:S(2)}) %collective-permute-start.14) | collective-permute-done | bytes 57376 | tf_op jit(solution)/shard_map/ppermute | solution.py:80
  60.3 2.4 %collective-permute-done.15 = bf16[4,7168]{1,0:T(4,128)(2,1)S(1)} collective-permute-done((bf16[4,7168]{1,0:T(4,128)(2,1)}, bf16[4,7168]{1,0:T(4,128)(2,1)S(1)}, u32[]{:S(2)}, u32[]{:S(2)}) %collective-permute-start.15) | collective-permute-done | bytes 57376 | tf_op jit(solution)/shard_map/ppermute | solution.py:80
  62.7 1.5 %fusion = bf16[1,4,7168]{2,1,0:T(4,128)(2,1)} fusion(bf16[4,7168]{1,0:T(4,128)(2,1)S(1)} %collective-permute-done.15, bf16[4,7168]{1,0:T(4,128)(2,1)S(1)} %collective-permute-done.14, bf16[4,7168]{1,0:T(4,128)(2,1)S(1)} %collective-permute-done.13, bf16[4,7168]{1,0:T(4,128)(2,1)} %get-tuple-element.27, f32[4]{0:T(128)S(1)} %bitcast.36), kind=kLoop, calls=%fused_computation.1 | loop fusion | flops 258048 | bytes 286736 | tf_op jit(solution)/shard_map/reshape | solution.py:283
  (17 shorter events, 0.0 us)
Async XLA Ops:
  0.0 23.3 %collective-permute-start.3 = (bf16[128,7168]{1,0:T(8,128)(2,1)}, bf16[128,7168]{1,0:T(8,128)(2,1)S(1)}, u32[]{:S(2)}, u32[]{:S(2)}) collective-permute-start(bf16[128,7168]{1,0:T(8,128)(2,1)} %bitcast.21), channel_id=1, source_target_pairs={{0,4},{4,0},{8,12},{12,8},{16,20},{20,16},{24,28},{28,24},{1,5},{5... | collective-permute-start | bytes 5505032 | tf_op jit(solution)/shard_map/ppermute | solution.py:80
  0.5 6.1 %collective-permute-start = (s32[1,4]{1,0:T(1,128)}, s32[1,4]{1,0:T(1,128)S(1)}, u32[]{:S(2)}, u32[]{:S(2)}) collective-permute-start(s32[1,4]{1,0:T(1,128)} %bitcast.28), channel_id=1, source_target_pairs={{0,8},{4,12},{8,0},{12,4},{16,24},{20,28},{24,16},{28,20},{1,9},{5... | collective-permute-start | bytes 56 | tf_op jit(solution)/shard_map/ppermute | solution.py:80
  3.1 7.1 %collective-permute-start.1 = (s32[1,4]{1,0:T(1,128)}, s32[1,4]{1,0:T(1,128)S(1)}, u32[]{:S(2)}, u32[]{:S(2)}) collective-permute-start(s32[1,4]{1,0:T(1,128)} %bitcast.29), channel_id=1, source_target_pairs={{0,16},{4,20},{8,24},{12,28},{16,0},{20,4},{24,8},{28,12},{1,17},{... | collective-permute-start | bytes 56 | tf_op jit(solution)/shard_map/ppermute | solution.py:80
  5.6 5.6 %collective-permute-start.2 = (s32[1,4]{1,0:T(1,128)}, s32[1,4]{1,0:T(1,128)S(1)}, u32[]{:S(2)}, u32[]{:S(2)}) collective-permute-start(s32[1,4]{1,0:T(1,128)} %bitcast.30), channel_id=1, source_target_pairs={{0,24},{4,28},{8,16},{12,20},{16,8},{20,12},{24,0},{28,4},{1,25},{... | collective-permute-start | bytes 56 | tf_op jit(solution)/shard_map/ppermute | solution.py:80
  5.6 7.5 %collective-permute-start.4 = (bf16[4,7168]{1,0:T(4,128)(2,1)}, bf16[4,7168]{1,0:T(4,128)(2,1)S(1)}, u32[]{:S(2)}, u32[]{:S(2)}) collective-permute-start(bf16[4,7168]{1,0:T(4,128)(2,1)} %bitcast.23), channel_id=1, source_target_pairs={{0,8},{4,12},{8,0},{12,4},{16,24},{20,28},{24,16},{28,20},{1,9},{5... | collective-permute-start | bytes 172040 | tf_op jit(solution)/shard_map/ppermute | solution.py:80
  6.6 9.7 %copy-start.10 = (s32[1,4]{1,0:T(1,128)}, s32[1,4]{1,0:T(1,128)S(1)}, u32[]{:S(2)}) copy-start(s32[1,4]{1,0:T(1,128)S(1)} %collective-permute-done.refs_5_) | copy-start | bytes 52
  6.6 7.1 %collective-permute-start.5 = (bf16[4,7168]{1,0:T(4,128)(2,1)}, bf16[4,7168]{1,0:T(4,128)(2,1)S(1)}, u32[]{:S(2)}, u32[]{:S(2)}) collective-permute-start(bf16[4,7168]{1,0:T(4,128)(2,1)} %bitcast.24), channel_id=1, source_target_pairs={{0,16},{4,20},{8,24},{12,28},{16,0},{20,4},{24,8},{28,12},{1,17},{... | collective-permute-start | bytes 172040 | tf_op jit(solution)/shard_map/ppermute | solution.py:80
  10.2 6.2 %copy-start.11 = (s32[1,4]{1,0:T(1,128)}, s32[1,4]{1,0:T(1,128)S(1)}, u32[]{:S(2)}) copy-start(s32[1,4]{1,0:T(1,128)S(1)} %collective-permute-done.1.refs_6_) | copy-start | bytes 52
  10.2 6.2 %collective-permute-start.6 = (bf16[4,7168]{1,0:T(4,128)(2,1)}, bf16[4,7168]{1,0:T(4,128)(2,1)S(1)}, u32[]{:S(2)}, u32[]{:S(2)}) collective-permute-start(bf16[4,7168]{1,0:T(4,128)(2,1)} %bitcast.25), channel_id=1, source_target_pairs={{0,24},{4,28},{8,16},{12,20},{16,8},{20,12},{24,0},{28,4},{1,25},{... | collective-permute-start | bytes 172040 | tf_op jit(solution)/shard_map/ppermute | solution.py:80
  11.2 5.1 %copy-start.12 = (s32[1,4]{1,0:T(1,128)}, s32[1,4]{1,0:T(1,128)S(1)}, u32[]{:S(2)}) copy-start(s32[1,4]{1,0:T(1,128)S(1)} %collective-permute-done.2.refs_7_) | copy-start | bytes 52
  13.2 3.2 %copy-start.7 = (bf16[4,7168]{1,0:T(4,128)(2,1)}, bf16[4,7168]{1,0:T(4,128)(2,1)S(1)}, u32[]{:S(2)}) copy-start(bf16[4,7168]{1,0:T(4,128)(2,1)S(1)} %collective-permute-done.4.refs_1_) | copy-start | bytes 172036
  13.7 2.7 %copy-start.8 = (bf16[4,7168]{1,0:T(4,128)(2,1)}, bf16[4,7168]{1,0:T(4,128)(2,1)S(1)}, u32[]{:S(2)}) copy-start(bf16[4,7168]{1,0:T(4,128)(2,1)S(1)} %collective-permute-done.5.refs_2_) | copy-start | bytes 172036
  16.4 0.6 copy-start.9
  19.8 13.9 %collective-permute-start.8 = (bf16[24,3584]{1,0:T(8,128)(2,1)}, bf16[24,3584]{1,0:T(8,128)(2,1)S(1)}, u32[]{:S(2)}, u32[]{:S(2)}) collective-permute-start(bf16[24,3584]{1,0:T(8,128)(2,1)} %get-tuple-element.22), channel_id=1, source_target_pairs={{0,2},{1,3},{2,0},{3,1},{4,6},{5,7},{6,4},{7,5},{8,10},{9,11},{10,... | collective-permute-start | bytes 516104 | tf_op jit(solution)/shard_map/ppermute | solution.py:80
  21.3 12.4 %collective-permute-start.9 = (bf16[24,3584]{1,0:T(8,128)(2,1)}, bf16[24,3584]{1,0:T(8,128)(2,1)S(1)}, u32[]{:S(2)}, u32[]{:S(2)}) collective-permute-start(bf16[24,3584]{1,0:T(8,128)(2,1)} %get-tuple-element.22), channel_id=1, source_target_pairs={{0,3},{1,2},{2,1},{3,0},{4,7},{5,6},{6,5},{7,4},{8,11},{9,10},{10,... | collective-permute-start | bytes 516104 | tf_op jit(solution)/shard_map/ppermute | solution.py:80
  22.8 10.9 %collective-permute-start.7 = (bf16[24,3584]{1,0:T(8,128)(2,1)}, bf16[24,3584]{1,0:T(8,128)(2,1)S(1)}, u32[]{:S(2)}, u32[]{:S(2)}) collective-permute-start(bf16[24,3584]{1,0:T(8,128)(2,1)} %get-tuple-element.18.after.refs_0_), channel_id=1, source_target_pairs={{0,1},{1,0},{2,3},{3,2},{4,5},{5,4},{6,7},{7,6},{8,9},{9,8},{10,11... | collective-permute-start | bytes 516104 | tf_op jit(solution)/shard_map/ppermute | solution.py:80
  23.3 1.3 %copy-start = (bf16[128,7168]{1,0:T(8,128)(2,1)}, bf16[128,7168]{1,0:T(8,128)(2,1)S(1)}, u32[]{:S(2)}) copy-start(bf16[128,7168]{1,0:T(8,128)(2,1)S(1)} %collective-permute-done.3.other) | copy-start | bytes 5505028
  33.7 0.7 %copy-start.6 = (bf16[24,3584]{1,0:T(8,128)(2,1)}, bf16[24,3584]{1,0:T(8,128)(2,1)S(1)}, u32[]{:S(2)}) copy-start(bf16[24,3584]{1,0:T(8,128)(2,1)S(1)} %collective-permute-done.7.refs_1_) | copy-start | bytes 516100
  33.7 0.7 %copy-start.4 = (bf16[24,3584]{1,0:T(8,128)(2,1)}, bf16[24,3584]{1,0:T(8,128)(2,1)S(1)}, u32[]{:S(2)}) copy-start(bf16[24,3584]{1,0:T(8,128)(2,1)S(1)} %collective-permute-done.8.refs_2_) | copy-start | bytes 516100
  33.7 0.7 %copy-start.5 = (bf16[24,3584]{1,0:T(8,128)(2,1)}, bf16[24,3584]{1,0:T(8,128)(2,1)S(1)}, u32[]{:S(2)}) copy-start(bf16[24,3584]{1,0:T(8,128)(2,1)S(1)} %collective-permute-done.9.refs_3_) | copy-start | bytes 516100
  34.5 28.2 %copy-start.13 = (f32[1,4]{1,0:T(1,128)S(1)}, f32[1,4]{1,0:T(1,128)}, u32[]{:S(2)}) copy-start(f32[1,4]{1,0:T(1,128)} %param.10) | copy-start | bytes 52
  42.5 6.1 %collective-permute-start.10 = (bf16[24,3584]{1,0:T(8,128)(2,1)}, bf16[24,3584]{1,0:T(8,128)(2,1)S(1)}, u32[]{:S(2)}, u32[]{:S(2)}) collective-permute-start(bf16[24,3584]{1,0:T(8,128)(2,1)} %get-tuple-element.24), channel_id=1, source_target_pairs={{0,1},{1,0},{2,3},{3,2},{4,5},{5,4},{6,7},{7,6},{8,9},{9,8},{10,11... | collective-permute-start | bytes 516104 | tf_op jit(solution)/shard_map/ppermute | solution.py:80
  44.0 6.6 %collective-permute-start.11 = (bf16[24,3584]{1,0:T(8,128)(2,1)}, bf16[24,3584]{1,0:T(8,128)(2,1)S(1)}, u32[]{:S(2)}, u32[]{:S(2)}) collective-permute-start(bf16[24,3584]{1,0:T(8,128)(2,1)} %get-tuple-element.25), channel_id=1, source_target_pairs={{0,2},{1,3},{2,0},{3,1},{4,6},{5,7},{6,4},{7,5},{8,10},{9,11},{10,... | collective-permute-start | bytes 516104 | tf_op jit(solution)/shard_map/ppermute | solution.py:80
  45.5 6.5 %collective-permute-start.12 = (bf16[24,3584]{1,0:T(8,128)(2,1)}, bf16[24,3584]{1,0:T(8,128)(2,1)S(1)}, u32[]{:S(2)}, u32[]{:S(2)}) collective-permute-start(bf16[24,3584]{1,0:T(8,128)(2,1)} %get-tuple-element.26), channel_id=1, source_target_pairs={{0,3},{1,2},{2,1},{3,0},{4,7},{5,6},{6,5},{7,4},{8,11},{9,10},{10,... | collective-permute-start | bytes 516104 | tf_op jit(solution)/shard_map/ppermute | solution.py:80
  48.7 3.4 %copy-start.1 = (bf16[24,3584]{1,0:T(8,128)(2,1)}, bf16[24,3584]{1,0:T(8,128)(2,1)S(1)}, u32[]{:S(2)}) copy-start(bf16[24,3584]{1,0:T(8,128)(2,1)S(1)} %collective-permute-done.10.refs_1_) | copy-start | bytes 516100
  50.7 1.4 %copy-start.2 = (bf16[24,3584]{1,0:T(8,128)(2,1)}, bf16[24,3584]{1,0:T(8,128)(2,1)S(1)}, u32[]{:S(2)}) copy-start(bf16[24,3584]{1,0:T(8,128)(2,1)S(1)} %collective-permute-done.11.refs_2_) | copy-start | bytes 516100
  52.1 0.7 %copy-start.3 = (bf16[24,3584]{1,0:T(8,128)(2,1)}, bf16[24,3584]{1,0:T(8,128)(2,1)S(1)}, u32[]{:S(2)}) copy-start(bf16[24,3584]{1,0:T(8,128)(2,1)S(1)} %collective-permute-done.12.refs_3_) | copy-start | bytes 516100
  55.0 4.4 %collective-permute-start.13 = (bf16[4,7168]{1,0:T(4,128)(2,1)}, bf16[4,7168]{1,0:T(4,128)(2,1)S(1)}, u32[]{:S(2)}, u32[]{:S(2)}) collective-permute-start(bf16[4,7168]{1,0:T(4,128)(2,1)} %get-tuple-element.28), channel_id=1, source_target_pairs={{0,8},{4,12},{8,0},{12,4},{16,24},{20,28},{24,16},{28,20},{1,9},{5... | collective-permute-start | bytes 172040 | tf_op jit(solution)/shard_map/ppermute | solution.py:80
  55.0 5.3 %collective-permute-start.14 = (bf16[4,7168]{1,0:T(4,128)(2,1)}, bf16[4,7168]{1,0:T(4,128)(2,1)S(1)}, u32[]{:S(2)}, u32[]{:S(2)}) collective-permute-start(bf16[4,7168]{1,0:T(4,128)(2,1)} %get-tuple-element.29), channel_id=1, source_target_pairs={{0,16},{4,20},{8,24},{12,28},{16,0},{20,4},{24,8},{28,12},{1,17},{... | collective-permute-start | bytes 172040 | tf_op jit(solution)/shard_map/ppermute | solution.py:80
  56.5 6.2 %collective-permute-start.15 = (bf16[4,7168]{1,0:T(4,128)(2,1)}, bf16[4,7168]{1,0:T(4,128)(2,1)S(1)}, u32[]{:S(2)}, u32[]{:S(2)}) collective-permute-start(bf16[4,7168]{1,0:T(4,128)(2,1)} %get-tuple-element.30), channel_id=1, source_target_pairs={{0,24},{4,28},{8,16},{12,20},{16,8},{20,12},{24,0},{28,4},{1,25},{... | collective-permute-start | bytes 172040 | tf_op jit(solution)/shard_map/ppermute | solution.py:80

commit v3 on v2

--- a/solution.py
+++ b/solution.py
@@ -84,47 +84,64 @@
 VMEM = pl.BlockSpec(memory_space=pltpu.VMEM)
 SMEM = pl.BlockSpec(memory_space=pltpu.SMEM)
 ANY = pl.BlockSpec(memory_space=pl.ANY)
-
-
-def pack_body(chips, shards, gain_ref, *refs):
-    rows, routes, blocks, line = refs[:chips], refs[chips : 2 * chips], refs[2 * chips : -1], refs[-1]
-    row_count, width = rows[0].shape
-    half = width // 2
+HBM = pl.BlockSpec(memory_space=pltpu.HBM)
+CODE = 128
+MIB = 1 << 20
+
+
+def held(*values):
+    return [pltpu.with_memory_space_constraint(value, pltpu.VMEM) for value in values]
+
+
+def limit(mib):
+    return pltpu.CompilerParams(vmem_limit_bytes=mib * MIB)
+
+
+def prepare_body(route_ref, rows_ref, gain_ref, out_ref):
+    row_count, width = rows_ref.shape
+    rows = rows_ref[...].astype(jnp.float32)
+    scale = lax.rsqrt(jnp.sum(rows * rows, axis=1, keepdims=True) * (1.0 / width) + epsilon)
+    out_ref[:, :width] = (rows * scale * gain_ref[...]).astype(jnp.bfloat16)
+    named = [route_ref[row] for row in range(row_count)]
+    at = lax.broadcasted_iota(jnp.int32, (row_count, CODE), 0)
+    code = jnp.zeros((row_count, CODE), jnp.int32)
+    for row in range(row_count):
+        slot = jnp.int32(0)
+        for before in range(row):
+            slot = slot + jnp.where(named[before] == named[row], 1, 0)
+        code = jnp.where(at == row, named[row] * row_count + slot, code)
+    out_ref[:, width:] = code.astype(jnp.float32).astype(jnp.bfloat16)
+
+
+def pack_body(chips, shards, *refs):
+    rows, blocks = refs[:chips], refs[chips:]
+    row_count, half = rows[0].shape[0], (rows[0].shape[1] - CODE) // 2
     block = 2 * CAP * chips
     height = E_WIN * block
     mine = lax.axis_index("exp") // shards
-    at = lax.broadcasted_iota(jnp.int32, (height, row_count), 0)
-    at_expert, at_slot = at // block, (at % block) // (2 * chips)
-    at_half, at_chip = (at % (2 * chips)) // chips, at % chips
+    at = lax.broadcasted_iota(jnp.int32, (height, CODE), 0)
+    at_slot, at_part, at_chip = (at % block) // (2 * chips), (at % (2 * chips)) // chips, at % chips
+    wanted = ((mine ^ (at // block)) * row_count + at_slot).astype(jnp.float32)
+    diagonal = lax.broadcasted_iota(jnp.int32, (row_count, CODE), 0) == lax.broadcasted_iota(
+        jnp.int32, (row_count, CODE), 1
+    )
     total = jnp.zeros((height, half), jnp.float32)
     for chip in range(chips):
-        line[...] = jnp.full(line.shape, -1, jnp.int32)
-        line[0:1, 0:row_count] = routes[chip][...]
-        named = line[...]
-        position = jnp.zeros(named.shape, jnp.int32)
-        for back in range(1, row_count):
-            position = position + (named == pltpu.roll(named, back, 1)).astype(jnp.int32)
-        named, position = named[0:1, 0:row_count], position[0:1, 0:row_count]
-        wanted = (at_chip == chip) & (at_slot == position) & ((mine ^ at_expert) == named)
+        code = rows[chip][:, 2 * half :].astype(jnp.float32)
+        code = jnp.sum(jnp.where(diagonal, code, 0.0), axis=0, keepdims=True)
         for part in range(2):
-            placing = jnp.where(wanted & (at_half == part), 1.0, 0.0).astype(jnp.bfloat16)
+            chosen = (wanted == code) & (at_chip == chip) & (at_part == part)
+            placing = jnp.where(chosen, 1.0, 0.0).astype(jnp.bfloat16)[:, :row_count]
             total = total + jnp.dot(
                 placing,
                 rows[chip][:, part * half : (part + 1) * half],
                 preferred_element_type=jnp.float32,
             )
-    squares = jnp.broadcast_to(jnp.sum(total * total, axis=1, keepdims=True), (height, 128))
-    first = (lax.broadcasted_iota(jnp.int32, (height, 128), 0) % (2 * chips)) < chips
-    partner = jnp.where(first, pltpu.roll(squares, height - chips, 0), pltpu.roll(squares, chips, 0))
-    scale = lax.rsqrt((squares + partner) * (1.0 / width) + epsilon)[:, 0:1]
-    upper = (lax.broadcasted_iota(jnp.int32, (height, half), 0) % (2 * chips)) < chips
-    gain = jnp.where(upper, gain_ref[:, :half], gain_ref[:, half:])
-    normed = total * scale * gain
     for expert in range(E_WIN):
-        blocks[expert][...] = normed[expert * block : (expert + 1) * block].astype(jnp.bfloat16)
-
-
-def fetch_body(piece, owner_ref, resident, own, other, after, both, down, held, sems):
+        blocks[expert][...] = total[expert * block : (expert + 1) * block].astype(jnp.bfloat16)
+
+
+def fetch_body(piece, owner_ref, resident, own, other, after, both, down, has_ref, sems):
     group = lax.axis_index("grp")
     copies = []
     for which, holder in enumerate((group, group ^ 1)):
@@ -144,14 +161,14 @@
         copies.append(
             pltpu.make_async_copy((own, other)[which], down.at[here], sems.at[3 * which + 2])
         )
-        held[here, :] = jnp.broadcast_to(has.astype(jnp.float32), (piece, held.shape[1]))
+        has_ref[here, :] = jnp.broadcast_to(has.astype(jnp.float32), (piece, has_ref.shape[1]))
     for copy in copies:
         copy.start()
     for copy in copies:
         copy.wait()
 
 
-def expert_body(devices, chips, lanes, both, down, held, *refs):
+def expert_body(devices, chips, lanes, both, down, has_ref, *refs):
     blocks, partials, stacked = refs[:devices], refs[devices : 2 * devices], refs[-1]
     block, half = blocks[0].shape
     used = devices * block
@@ -171,7 +188,7 @@
     column = lax.broadcasted_iota(jnp.int32, sums[0].shape, 1)
     valid = ((column % (2 * chips)) < chips) & (column < used)
     act = sums[0] * jax.nn.sigmoid(sums[0]) * sums[1]
-    act = jnp.where(valid & (held[...] > 0.5), act, 0.0)
+    act = jnp.where(valid & (has_ref[...] > 0.5), act, 0.0)
     above = act.T.astype(jnp.bfloat16)[:used]
     below = pltpu.roll(act, chips, 1).T.astype(jnp.bfloat16)[:used]
     step = half // 7 if half % (7 * 128) == 0 else half
@@ -186,15 +203,35 @@
             ].astype(jnp.bfloat16)
 
 
-def combine_body(devices, chips, shards, placing, *refs):
-    blocks, outs = refs[:devices], refs[devices:]
-    half = blocks[0].shape[1]
+def combine_body(devices, chips, shards, *refs):
+    rows, blocks = refs[:chips], refs[chips : chips + devices]
+    outs, codes = refs[chips + devices : -1], refs[-1]
+    block, half = blocks[0].shape
     row_count = outs[0].shape[0]
+    mine = lax.axis_index("exp") // shards
+    for chip in range(chips):
+        codes[chip * row_count : (chip + 1) * row_count, :] = rows[chip][:, 2 * half :].astype(
+            jnp.float32
+        )
+    code = codes[...]
+    home = lax.broadcasted_iota(jnp.int32, code.shape, 0) // row_count
+    at = lax.broadcasted_iota(jnp.int32, code.shape, 1)
+    at_slot, at_part, at_chip = at // (2 * chips), (at % (2 * chips)) // chips, at % chips
+    placing = []
+    for expert in range(E_WIN):
+        wanted = ((mine ^ expert) * row_count + at_slot).astype(jnp.float32)
+        chosen = (wanted == code) & (at_chip == home) & (at < block)
+        placing.append(
+            [
+                jnp.where(chosen & (at_part == part), 1.0, 0.0).astype(jnp.bfloat16)[:, :block]
+                for part in range(2)
+            ]
+        )
     for part in range(2):
         total = 0.0
         for index in range(devices):
             total = total + jnp.dot(
-                placing[2 * (index // shards) + part],
+                placing[index // shards][part],
                 blocks[index][...],
                 preferred_element_type=jnp.float32,
             )
@@ -212,52 +249,41 @@
     shards = devices // E_WIN
     half, block = width // 2, 2 * CAP * chips
     piece = sectioned.shape[1]
-    mine = lax.axis_index("exp") // shards
-    routes = [route[0].reshape(1, row_count)]
-    gathered = [rows]
-    for hop in range(1, chips):
-        gathered.append(swap(rows, "grp", PAIR * hop))
-    for hop in range(1, chips):
-        routes.append(swap(routes[0], "grp", PAIR * hop))
-    other_piece = swap(sectioned[0], "grp", 1)
-    half_block = jax.ShapeDtypeStruct((block, half), jnp.bfloat16)
+    payload = pl.pallas_call(
+        prepare_body,
+        out_shape=pltpu.VMEM((row_count, width + CODE), jnp.bfloat16),
+        in_specs=[SMEM, VMEM, VMEM],
+        out_specs=VMEM,
+        compiler_params=limit(4),
+        name="prepare",
+    )(route.reshape(row_count), rows, norm_gain.reshape(1, width))
+    gathered = [payload] + [swap(payload, "grp", PAIR * hop) for hop in range(1, chips)]
+    own_piece, payload = lax.optimization_barrier((sectioned[0], payload))
+    other_piece = swap(own_piece, "grp", 1)
+    half_block = pltpu.VMEM((block, half), jnp.bfloat16)
     packed = pl.pallas_call(
         functools.partial(pack_body, chips, shards),
         out_shape=[half_block] * E_WIN,
-        in_specs=[VMEM] * (1 + 2 * chips),
+        in_specs=[VMEM] * chips,
         out_specs=[VMEM] * E_WIN,
-        scratch_shapes=[pltpu.VMEM((8, 128), jnp.int32)],
+        compiler_params=limit(8),
         name="pack",
-    )(norm_gain.reshape(1, width), *gathered, *routes)
+    )(*held(*gathered))
     blocks = [packed[bits // shards] for bits in range(devices)]
     blocks = [blocks[0]] + [swap(blocks[bits], "exp", bits) for bits in range(1, devices)]
-    both, down, held = pl.pallas_call(
+    both, down, has = pl.pallas_call(
         functools.partial(fetch_body, piece),
         out_shape=[
-            jax.ShapeDtypeStruct((2, PAIR * piece, width), jnp.bfloat16),
-            jax.ShapeDtypeStruct((PAIR * piece, width), jnp.bfloat16),
-            jax.ShapeDtypeStruct((PAIR * piece, 128), jnp.float32),
+            pltpu.VMEM((2, PAIR * piece, width), jnp.bfloat16),
+            pltpu.VMEM((PAIR * piece, width), jnp.bfloat16),
+            pltpu.VMEM((PAIR * piece, 128), jnp.float32),
         ],
-        in_specs=[SMEM, ANY, ANY, ANY, ANY],
+        in_specs=[SMEM, HBM, HBM, ANY, ANY],
         out_specs=[VMEM] * 3,
         scratch_shapes=[pltpu.SemaphoreType.DMA((3 * PAIR,))],
+        compiler_params=limit(2),
         name="fetch",
     )(owner, resident, sectioned[0], other_piece, packed[0])
-    named = jnp.concatenate(routes, axis=0)
-    seen = [
-        sum([(named[:, r] == named[:, b]).astype(jnp.int32) for b in range(r)], jnp.zeros((chips,), jnp.int32))
-        for r in range(row_count)
-    ]
-    position = jnp.stack(seen, axis=1)
-    chip_of = jnp.arange(chips, dtype=jnp.int32)[:, None]
-    column = jnp.arange(block, dtype=jnp.int32)[None, None, :]
-    placing = []
-    for expert in range(E_WIN):
-        for part in range(2):
-            target = (position * 2 + part) * chips + chip_of
-            chosen = (named == (mine ^ expert))[:, :, None] & (column == target[:, :, None])
-            placing.append(chosen.astype(jnp.bfloat16).reshape(chips * row_count, block))
-    placing = jnp.stack(placing)
     lanes = -(-devices * block // 128) * 128
     partials = pl.pallas_call(
         functools.partial(expert_body, devices, chips, lanes),
@@ -265,17 +291,20 @@
         in_specs=[VMEM] * (3 + devices),
         out_specs=[VMEM] * devices,
         scratch_shapes=[pltpu.VMEM((lanes, half), jnp.bfloat16)],
+        compiler_params=limit(12),
         name="expert",
-    )(both, down, held, *blocks)
+    )(*held(both, down, has, *blocks))
     returned = [partials[0]] + [swap(partials[bits], "exp", bits) for bits in range(1, devices)]
-    home = jax.ShapeDtypeStruct((row_count, width), jnp.bfloat16)
+    home = pltpu.VMEM((row_count, width), jnp.bfloat16)
     sums = pl.pallas_call(
         functools.partial(combine_body, devices, chips, shards),
         out_shape=[home] * chips,
-        in_specs=[VMEM] * (1 + devices),
+        in_specs=[VMEM] * (chips + devices),
         out_specs=[VMEM] * chips,
+        scratch_shapes=[pltpu.VMEM((chips * row_count, CODE), jnp.float32)],
+        compiler_params=limit(8),
         name="combine",
-    )(placing, *returned)
+    )(*held(*gathered, *returned))
     combined = sums[0].astype(jnp.float32)
     for hop in range(1, chips):
         combined = combined + swap(sums[hop], "grp", PAIR * hop).astype(jnp.float32)

time: 64.5 us -> 50.2 us (0.78)
  Pallas kernels: 22.2 us -> 6.29 us
  local copies, waits for them, and re-layouts: 3.76 us -> 9.55 us
  starting transfers between devices: 21.4 us -> 17.3 us
  other arithmetic: 3.81 us -> 0.71 us
  waiting for transfers between devices: 12.9 us -> 15.9 us
    pallas_call x1 -> x2, Pallas kernels: 9.01 us -> 2.07 us  [the longest x1 1.36 us: move_rows(): pl.pallas_call(functools.partial(fetch_body, piece), out_shape=[pltpu.VME...]
    unnamed x28 -> x14, local copies, waits for them, and re-layouts: 3.33 us -> 9.55 us
    pallas_call x1, Pallas kernels: 8.09 us -> 2.94 us  [move_rows(): pl.pallas_call(functools.partial(expert_body, devices, chips, lanes), out...]
    ppermute x16 -> x13, starting transfers between devices: 21.4 us -> 17.3 us  [swap(): return lax.ppermute(value, axis, [(i, i ^ bits) for i in range(size)])]
    ppermute x16 -> x13, waiting for transfers between devices: 12.9 us -> 15.9 us  [swap(): return lax.ppermute(value, axis, [(i, i ^ bits) for i in range(size)])]
    pallas_call x1, Pallas kernels: 2.83 us -> 0.87 us  [move_rows(): pl.pallas_call(functools.partial(pack_body, chips, shards), out_shape=[ha...]
    pallas_call x1, Pallas kernels: 2.27 us -> 0.4 us  [move_rows(): pl.pallas_call(functools.partial(combine_body, devices, chips, shards), o...]
    reshape x1, other arithmetic: 1.53 us -> 0.71 us  [move_rows(): return result.reshape(1, row_count, width)]
  transfers between devices with their start and end apart: 16 -> 13, of which waited for: 8 -> 7; matrix products, arithmetic and copies ran while one was open for 4% -> 0% of each run, Pallas kernels for 18% -> 4%
where the time goes in v3:
time: 50.2 us; the launch traced here: 49.9 us
  starting transfers between devices  17.3 us (34%)
  waiting for transfers between devices  15.9 us (32%)
  local copies, waits for them, and re-layouts  9.55 us (19%)
  Pallas kernels  6.29 us (13%)
  other arithmetic  0.71 us (1%)
    ppermute x13, starting transfers between devices, swap(): return lax.ppermute(value, axis, [(i, i ^ bits) for i in range(size)])  17.3 us
    ppermute x13, waiting for transfers between devices, swap(): return lax.ppermute(value, axis, [(i, i ^ bits) for i in range(size)])  15.9 us
    unnamed x14, local copies, waits for them, and re-layouts  9.55 us
    pallas_call x1, Pallas kernels, move_rows(): pl.pallas_call(functools.partial(expert_body, devices, chips, lanes), out...  2.94 us
    pallas_call x1, Pallas kernels, move_rows(): pl.pallas_call(functools.partial(fetch_body, piece), out_shape=[pltpu.VME...  1.36 us
  transfers between devices with their start and end apart: 13, of which 7 were waited for; matrix products, arithmetic and copies ran while one was open for 0% of the time, Pallas kernels for 4%

profile of v3, /device:TPU:0, one launch (start us, length us, event | category | flops | bytes accessed | tf_op | source)
XLA Modules:
  0.0 49.9 jit_solution(3184004469104677762)
XLA Ops:
  0.0 0.0 copy-start.2
  0.0 0.8 %copy-done.2 = bf16[1,4,7168]{2,1,0:T(4,128)(2,1)S(1)} copy-done((bf16[1,4,7168]{2,1,0:T(4,128)(2,1)S(1)}, bf16[1,4,7168]{2,1,0:T(4,128)(2,1)}, u32[]{:S(2)}) %copy-start.2) | copy-done | bytes 57368
  0.8 0.0 copy-start.3
  0.8 0.7 %copy-done.3 = f32[7168]{0:T(1024)S(1)} copy-done((f32[7168]{0:T(1024)S(1)}, f32[7168]{0:T(1024)}, u32[]{:S(2)}) %copy-start.3) | copy-done | bytes 28696
  1.6 0.0 copy-start.5
  1.6 0.7 %copy-done.5 = s32[1,4,1]{1,2,0:T(1,128)S(1)} copy-done((s32[1,4,1]{1,2,0:T(1,128)S(1)}, s32[1,4,1]{1,2,0:T(1,128)}, u32[]{:S(2)}) %copy-start.5) | copy-done | bytes 40
  2.2 0.7 %prepare.1.refs_0_ = bf16[4,7296]{1,0:T(4,128)(2,1)S(1)} custom-call(s32[4]{0:T(128)S(1)} %bitcast.11, bf16[4,7168]{1,0:T(4,128)(2,1)S(1)} %bitcast.9, f32[1,7168]{1,0:T(1,128)S(1)} %bitcast.10), custom_call_target="tpu_custom_call" | custom-call | tf_op jit(solution)/shard_map/prepare/pallas_call | solution.py:252
  2.9 0.6 %collective-permute-start.3 = (bf16[128,7168]{1,0:T(8,128)(2,1)}, bf16[128,7168]{1,0:T(8,128)(2,1)S(1)}, u32[]{:S(2)}, u32[]{:S(2)}) collective-permute-start(bf16[128,7168]{1,0:T(8,128)(2,1)} %bitcast.7), channel_id=1, source_target_pairs={{0,4},{4,0},{8,12},{12,8},{16,20},{20,16},{24,28},{28,24},{1,5},{5... | collective-permute-start | bytes 5505032 | tf_op jit(solution)/shard_map/ppermute | solution.py:80
  3.5 2.6 %collective-permute-start = (bf16[4,7296]{1,0:T(4,128)(2,1)S(1)}, bf16[4,7296]{1,0:T(4,128)(2,1)S(1)}, u32[]{:S(2)}, u32[]{:S(2)}) collective-permute-start(bf16[4,7296]{1,0:T(4,128)(2,1)S(1)} %prepare.1.refs_0_), channel_id=1, source_target_pairs={{0,8},{4,12},{8,0},{12,4},{16,24},{20,28},{24,16},{28,20},{1,9},{5... | collective-permute-start | bytes 175112 | tf_op jit(solution)/shard_map/ppermute | solution.py:80
  6.1 2.6 %collective-permute-start.1 = (bf16[4,7296]{1,0:T(4,128)(2,1)S(1)}, bf16[4,7296]{1,0:T(4,128)(2,1)S(1)}, u32[]{:S(2)}, u32[]{:S(2)}) collective-permute-start(bf16[4,7296]{1,0:T(4,128)(2,1)S(1)} %prepare.1.refs_0_), channel_id=1, source_target_pairs={{0,16},{4,20},{8,24},{12,28},{16,0},{20,4},{24,8},{28,12},{1,17},{... | collective-permute-start | bytes 175112 | tf_op jit(solution)/shard_map/ppermute | solution.py:80
  8.7 0.0 collective-permute-start.2
  8.7 0.0 collective-permute-done.refs_1_
  8.7 4.0 %collective-permute-done.1.refs_2_ = bf16[4,7296]{1,0:T(4,128)(2,1)S(1)} collective-permute-done((bf16[4,7296]{1,0:T(4,128)(2,1)S(1)}, bf16[4,7296]{1,0:T(4,128)(2,1)S(1)}, u32[]{:S(2)}, u32[]{:S(2)}) %collective-permute-start.1) | collective-permute-done | bytes 58400 | tf_op jit(solution)/shard_map/ppermute | solution.py:80
  12.7 2.0 %collective-permute-done.2.refs_3_ = bf16[4,7296]{1,0:T(4,128)(2,1)S(1)} collective-permute-done((bf16[4,7296]{1,0:T(4,128)(2,1)S(1)}, bf16[4,7296]{1,0:T(4,128)(2,1)S(1)}, u32[]{:S(2)}, u32[]{:S(2)}) %collective-permute-start.2) | collective-permute-done | bytes 58400 | tf_op jit(solution)/shard_map/ppermute | solution.py:80
  14.7 0.9 %pack.1 = (bf16[24,3584]{1,0:T(8,128)(2,1)S(1)}, bf16[24,3584]{1,0:T(8,128)(2,1)S(1)}) custom-call(bf16[4,7296]{1,0:T(4,128)(2,1)S(1)} %prepare.1.refs_0_, bf16[4,7296]{1,0:T(4,128)(2,1)S(1)} %collective-permute-done.refs_1_, bf16[4,7296]{1,0:T(4,128)(2,1)S(1)} %collective-permute-done.1.refs_2_, bf16[4,7296]{1,0:T(4,128)(2,1)S(1)} %collective-permute-done.2.refs_3_), custom_call_target="tpu_custom_call" | custom-call | tf_op jit(solution)/shard_map/pack/pallas_call | solution.py:264
  15.6 1.6 %collective-permute-start.4 = (bf16[24,3584]{1,0:T(8,128)(2,1)S(1)}, bf16[24,3584]{1,0:T(8,128)(2,1)S(1)}, u32[]{:S(2)}, u32[]{:S(2)}) collective-permute-start(bf16[24,3584]{1,0:T(8,128)(2,1)S(1)} %get-tuple-element.20.after.refs_0_), channel_id=1, source_target_pairs={{0,1},{1,0},{2,3},{3,2},{4,5},{5,4},{6,7},{7,6},{8,9},{9,8},{10,11... | collective-permute-start | bytes 516104 | tf_op jit(solution)/shard_map/ppermute | solution.py:80
  17.2 1.5 %collective-permute-start.5 = (bf16[24,3584]{1,0:T(8,128)(2,1)S(1)}, bf16[24,3584]{1,0:T(8,128)(2,1)S(1)}, u32[]{:S(2)}, u32[]{:S(2)}) collective-permute-start(bf16[24,3584]{1,0:T(8,128)(2,1)S(1)} %get-tuple-element.24), channel_id=1, source_target_pairs={{0,2},{1,3},{2,0},{3,1},{4,6},{5,7},{6,4},{7,5},{8,10},{9,11},{10,... | collective-permute-start | bytes 516104 | tf_op jit(solution)/shard_map/ppermute | solution.py:80
  18.7 0.5 collective-permute-start.6
  19.2 0.0 collective-permute-done.3.other
  19.2 0.0 copy-start
  19.2 5.2 %copy-done = bf16[2,512,7168]{2,1,0:T(8,128)(2,1)S(1)} copy-done((bf16[2,512,7168]{2,1,0:T(8,128)(2,1)S(1)}, bf16[2,512,7168]{2,1,0:T(8,128)(2,1)}, u32[]{:S(2)}) %copy-start) | copy-done | bytes 14680088
  24.3 0.0 copy-start.1
  24.3 1.5 %copy-done.1 = bf16[1,128,7168]{2,1,0:T(8,128)(2,1)S(1)} copy-done((bf16[1,128,7168]{2,1,0:T(8,128)(2,1)S(1)}, bf16[1,128,7168]{2,1,0:T(8,128)(2,1)}, u32[]{:S(2)}) %copy-start.1) | copy-done | bytes 1835032
  25.8 0.0 copy-start.4
  25.8 0.7 %copy-done.4 = s32[8]{0:T(128)S(1)} copy-done((s32[8]{0:T(128)S(1)}, s32[8]{0:T(128)}, u32[]{:S(2)}) %copy-start.4) | copy-done | bytes 56
  26.5 1.4 %fetch.1 = (bf16[2,256,7168]{2,1,0:T(8,128)(2,1)S(1)}, bf16[256,7168]{1,0:T(8,128)(2,1)S(1)}, f32[256,128]{1,0:T(8,128)S(1)}) custom-call(s32[8]{0:T(128)S(1)} %copy-done.4, bf16[2,512,7168]{2,1,0:T(8,128)(2,1)S(1)} %copy-done, bf16[128,7168]{1,0:T(8,128)(2,1)S(1)} %bitcast.8, bf16[128,7168]{1,0:T(8,128)(2,1)S(1)} %collective-permute-done.3.other, ...), custom_call_target="tpu_custom_call" | custom-call | tf_op jit(solution)/shard_map/fetch/pallas_call | solution.py:274
  27.9 0.0 collective-permute-done.4.refs_1_
  27.9 0.0 collective-permute-done.5.refs_2_
  27.9 0.0 collective-permute-done.6.refs_3_
  27.9 0.0 copy-start.6
  27.9 2.9 %expert.1 = (bf16[24,3584]{1,0:T(8,128)(2,1)S(1)}, bf16[24,3584]{1,0:T(8,128)(2,1)S(1)}, bf16[24,3584]{1,0:T(8,128)(2,1)S(1)}, bf16[24,3584]{1,0:T(8,128)(2,1)S(1)}) custom-call(bf16[2,256,7168]{2,1,0:T(8,128)(2,1)S(1)} %get-tuple-element.21.both, bf16[256,7168]{1,0:T(8,128)(2,1)S(1)} %get-tuple-element.22.down, f32[256,128]{1,0:T(8,128)S(1)} %get-tuple-element.23.has_ref, ...), custom_call_target="tpu_custom_call" | custom-call | tf_op jit(solution)/shard_map/expert/pallas_call | solution.py:288
  30.8 1.5 %collective-permute-start.7 = (bf16[24,3584]{1,0:T(8,128)(2,1)S(1)}, bf16[24,3584]{1,0:T(8,128)(2,1)S(1)}, u32[]{:S(2)}, u32[]{:S(2)}) collective-permute-start(bf16[24,3584]{1,0:T(8,128)(2,1)S(1)} %get-tuple-element.26), channel_id=1, source_target_pairs={{0,1},{1,0},{2,3},{3,2},{4,5},{5,4},{6,7},{7,6},{8,9},{9,8},{10,11... | collective-permute-start | bytes 516104 | tf_op jit(solution)/shard_map/ppermute | solution.py:80
  32.4 1.5 %collective-permute-start.8 = (bf16[24,3584]{1,0:T(8,128)(2,1)S(1)}, bf16[24,3584]{1,0:T(8,128)(2,1)S(1)}, u32[]{:S(2)}, u32[]{:S(2)}) collective-permute-start(bf16[24,3584]{1,0:T(8,128)(2,1)S(1)} %get-tuple-element.27), channel_id=1, source_target_pairs={{0,2},{1,3},{2,0},{3,1},{4,6},{5,7},{6,4},{7,5},{8,10},{9,11},{10,... | collective-permute-start | bytes 516104 | tf_op jit(solution)/shard_map/ppermute | solution.py:80
  33.9 0.5 collective-permute-start.9
  34.4 3.2 %collective-permute-done.7.refs_5_ = bf16[24,3584]{1,0:T(8,128)(2,1)S(1)} collective-permute-done((bf16[24,3584]{1,0:T(8,128)(2,1)S(1)}, bf16[24,3584]{1,0:T(8,128)(2,1)S(1)}, u32[]{:S(2)}, u32[]{:S(2)}) %collective-permute-start.7) | collective-permute-done | bytes 172064 | tf_op jit(solution)/shard_map/ppermute | solution.py:80
  37.6 3.1 %collective-permute-done.8.refs_6_ = bf16[24,3584]{1,0:T(8,128)(2,1)S(1)} collective-permute-done((bf16[24,3584]{1,0:T(8,128)(2,1)S(1)}, bf16[24,3584]{1,0:T(8,128)(2,1)S(1)}, u32[]{:S(2)}, u32[]{:S(2)}) %collective-permute-start.8) | collective-permute-done | bytes 172064 | tf_op jit(solution)/shard_map/ppermute | solution.py:80
  40.6 0.0 collective-permute-done.9.refs_7_
  40.6 0.4 combine.1
  41.0 1.0 %collective-permute-start.10 = (bf16[4,7168]{1,0:T(4,128)(2,1)S(1)}, bf16[4,7168]{1,0:T(4,128)(2,1)S(1)}, u32[]{:S(2)}, u32[]{:S(2)}) collective-permute-start(bf16[4,7168]{1,0:T(4,128)(2,1)S(1)} %get-tuple-element.30), channel_id=1, source_target_pairs={{0,8},{4,12},{8,0},{12,4},{16,24},{20,28},{24,16},{28,20},{1,9},{5... | collective-permute-start | bytes 172040 | tf_op jit(solution)/shard_map/ppermute | solution.py:80
  42.1 1.1 %collective-permute-start.11 = (bf16[4,7168]{1,0:T(4,128)(2,1)S(1)}, bf16[4,7168]{1,0:T(4,128)(2,1)S(1)}, u32[]{:S(2)}, u32[]{:S(2)}) collective-permute-start(bf16[4,7168]{1,0:T(4,128)(2,1)S(1)} %get-tuple-element.31), channel_id=1, source_target_pairs={{0,16},{4,20},{8,24},{12,28},{16,0},{20,4},{24,8},{28,12},{1,17},{... | collective-permute-start | bytes 172040 | tf_op jit(solution)/shard_map/ppermute | solution.py:80
  43.2 2.3 %collective-permute-start.12 = (bf16[4,7168]{1,0:T(4,128)(2,1)S(1)}, bf16[4,7168]{1,0:T(4,128)(2,1)S(1)}, u32[]{:S(2)}, u32[]{:S(2)}) collective-permute-start(bf16[4,7168]{1,0:T(4,128)(2,1)S(1)} %get-tuple-element.32), channel_id=1, source_target_pairs={{0,24},{4,28},{8,16},{12,20},{16,8},{20,12},{24,0},{28,4},{1,25},{... | collective-permute-start | bytes 172040 | tf_op jit(solution)/shard_map/ppermute | solution.py:80
  45.5 0.3 collective-permute-done.10
  45.7 2.0 %collective-permute-done.11 = bf16[4,7168]{1,0:T(4,128)(2,1)S(1)} collective-permute-done((bf16[4,7168]{1,0:T(4,128)(2,1)S(1)}, bf16[4,7168]{1,0:T(4,128)(2,1)S(1)}, u32[]{:S(2)}, u32[]{:S(2)}) %collective-permute-start.11) | collective-permute-done | bytes 57376 | tf_op jit(solution)/shard_map/ppermute | solution.py:80
  47.8 1.4 %collective-permute-done.12 = bf16[4,7168]{1,0:T(4,128)(2,1)S(1)} collective-permute-done((bf16[4,7168]{1,0:T(4,128)(2,1)S(1)}, bf16[4,7168]{1,0:T(4,128)(2,1)S(1)}, u32[]{:S(2)}, u32[]{:S(2)}) %collective-permute-start.12) | collective-permute-done | bytes 57376 | tf_op jit(solution)/shard_map/ppermute | solution.py:80
  49.2 0.0 copy-done.6
  49.2 0.7 %fusion = bf16[1,4,7168]{2,1,0:T(4,128)(2,1)} fusion(bf16[4,7168]{1,0:T(4,128)(2,1)S(1)} %collective-permute-done.12, bf16[4,7168]{1,0:T(4,128)(2,1)S(1)} %collective-permute-done.11, bf16[4,7168]{1,0:T(4,128)(2,1)S(1)} %collective-permute-done.10, bf16[4,7168]{1,0:T(4,128)(2,1)S(1)} %get-tuple-element.29, f32[4]{0:T(128)S(1)} %bitcast.12), kind=kLoop, calls=%fused_computation.1 | loop fusion | flops 258048 | bytes 286736 | tf_op jit(solution)/shard_map/reshape | solution.py:312
Async XLA Ops:
  0.0 0.8 %copy-start.2 = (bf16[1,4,7168]{2,1,0:T(4,128)(2,1)S(1)}, bf16[1,4,7168]{2,1,0:T(4,128)(2,1)}, u32[]{:S(2)}) copy-start(bf16[1,4,7168]{2,1,0:T(4,128)(2,1)} %param.7) | copy-start | bytes 172036
  0.8 0.7 %copy-start.3 = (f32[7168]{0:T(1024)S(1)}, f32[7168]{0:T(1024)}, u32[]{:S(2)}) copy-start(f32[7168]{0:T(1024)} %param.8) | copy-start | bytes 86020
  1.6 0.7 %copy-start.5 = (s32[1,4,1]{1,2,0:T(1,128)S(1)}, s32[1,4,1]{1,2,0:T(1,128)}, u32[]{:S(2)}) copy-start(s32[1,4,1]{1,2,0:T(1,128)} %param.9) | copy-start | bytes 52
  2.9 16.2 %collective-permute-start.3 = (bf16[128,7168]{1,0:T(8,128)(2,1)}, bf16[128,7168]{1,0:T(8,128)(2,1)S(1)}, u32[]{:S(2)}, u32[]{:S(2)}) collective-permute-start(bf16[128,7168]{1,0:T(8,128)(2,1)} %bitcast.7), channel_id=1, source_target_pairs={{0,4},{4,0},{8,12},{12,8},{16,20},{20,16},{24,28},{28,24},{1,5},{5... | collective-permute-start | bytes 5505032 | tf_op jit(solution)/shard_map/ppermute | solution.py:80
  3.5 5.2 %collective-permute-start = (bf16[4,7296]{1,0:T(4,128)(2,1)S(1)}, bf16[4,7296]{1,0:T(4,128)(2,1)S(1)}, u32[]{:S(2)}, u32[]{:S(2)}) collective-permute-start(bf16[4,7296]{1,0:T(4,128)(2,1)S(1)} %prepare.1.refs_0_), channel_id=1, source_target_pairs={{0,8},{4,12},{8,0},{12,4},{16,24},{20,28},{24,16},{28,20},{1,9},{5... | collective-permute-start | bytes 175112 | tf_op jit(solution)/shard_map/ppermute | solution.py:80
  6.1 6.6 %collective-permute-start.1 = (bf16[4,7296]{1,0:T(4,128)(2,1)S(1)}, bf16[4,7296]{1,0:T(4,128)(2,1)S(1)}, u32[]{:S(2)}, u32[]{:S(2)}) collective-permute-start(bf16[4,7296]{1,0:T(4,128)(2,1)S(1)} %prepare.1.refs_0_), channel_id=1, source_target_pairs={{0,16},{4,20},{8,24},{12,28},{16,0},{20,4},{24,8},{28,12},{1,17},{... | collective-permute-start | bytes 175112 | tf_op jit(solution)/shard_map/ppermute | solution.py:80
  8.7 6.0 %collective-permute-start.2 = (bf16[4,7296]{1,0:T(4,128)(2,1)S(1)}, bf16[4,7296]{1,0:T(4,128)(2,1)S(1)}, u32[]{:S(2)}, u32[]{:S(2)}) collective-permute-start(bf16[4,7296]{1,0:T(4,128)(2,1)S(1)} %prepare.1.refs_0_), channel_id=1, source_target_pairs={{0,24},{4,28},{8,16},{12,20},{16,8},{20,12},{24,0},{28,4},{1,25},{... | collective-permute-start | bytes 175112 | tf_op jit(solution)/shard_map/ppermute | solution.py:80
  15.6 12.3 %collective-permute-start.4 = (bf16[24,3584]{1,0:T(8,128)(2,1)S(1)}, bf16[24,3584]{1,0:T(8,128)(2,1)S(1)}, u32[]{:S(2)}, u32[]{:S(2)}) collective-permute-start(bf16[24,3584]{1,0:T(8,128)(2,1)S(1)} %get-tuple-element.20.after.refs_0_), channel_id=1, source_target_pairs={{0,1},{1,0},{2,3},{3,2},{4,5},{5,4},{6,7},{7,6},{8,9},{9,8},{10,11... | collective-permute-start | bytes 516104 | tf_op jit(solution)/shard_map/ppermute | solution.py:80
  17.2 10.7 %collective-permute-start.5 = (bf16[24,3584]{1,0:T(8,128)(2,1)S(1)}, bf16[24,3584]{1,0:T(8,128)(2,1)S(1)}, u32[]{:S(2)}, u32[]{:S(2)}) collective-permute-start(bf16[24,3584]{1,0:T(8,128)(2,1)S(1)} %get-tuple-element.24), channel_id=1, source_target_pairs={{0,2},{1,3},{2,0},{3,1},{4,6},{5,7},{6,4},{7,5},{8,10},{9,11},{10,... | collective-permute-start | bytes 516104 | tf_op jit(solution)/shard_map/ppermute | solution.py:80
  18.7 9.2 %collective-permute-start.6 = (bf16[24,3584]{1,0:T(8,128)(2,1)S(1)}, bf16[24,3584]{1,0:T(8,128)(2,1)S(1)}, u32[]{:S(2)}, u32[]{:S(2)}) collective-permute-start(bf16[24,3584]{1,0:T(8,128)(2,1)S(1)} %get-tuple-element.24), channel_id=1, source_target_pairs={{0,3},{1,2},{2,1},{3,0},{4,7},{5,6},{6,5},{7,4},{8,11},{9,10},{10,... | collective-permute-start | bytes 516104 | tf_op jit(solution)/shard_map/ppermute | solution.py:80
  19.2 5.2 %copy-start = (bf16[2,512,7168]{2,1,0:T(8,128)(2,1)S(1)}, bf16[2,512,7168]{2,1,0:T(8,128)(2,1)}, u32[]{:S(2)}) copy-start(bf16[2,512,7168]{2,1,0:T(8,128)(2,1)} %resident.1) | copy-start | bytes 44040196
  24.3 1.5 %copy-start.1 = (bf16[1,128,7168]{2,1,0:T(8,128)(2,1)S(1)}, bf16[1,128,7168]{2,1,0:T(8,128)(2,1)}, u32[]{:S(2)}) copy-start(bf16[1,128,7168]{2,1,0:T(8,128)(2,1)} %param.12) | copy-start | bytes 5505028
  25.8 0.7 %copy-start.4 = (s32[8]{0:T(128)S(1)}, s32[8]{0:T(128)}, u32[]{:S(2)}) copy-start(s32[8]{0:T(128)} %owner_ref.1) | copy-start | bytes 100
  27.9 21.3 %copy-start.6 = (f32[1,4]{1,0:T(1,128)S(1)}, f32[1,4]{1,0:T(1,128)}, u32[]{:S(2)}) copy-start(f32[1,4]{1,0:T(1,128)} %param.10) | copy-start | bytes 52
  30.8 6.7 %collective-permute-start.7 = (bf16[24,3584]{1,0:T(8,128)(2,1)S(1)}, bf16[24,3584]{1,0:T(8,128)(2,1)S(1)}, u32[]{:S(2)}, u32[]{:S(2)}) collective-permute-start(bf16[24,3584]{1,0:T(8,128)(2,1)S(1)} %get-tuple-element.26), channel_id=1, source_target_pairs={{0,1},{1,0},{2,3},{3,2},{4,5},{5,4},{6,7},{7,6},{8,9},{9,8},{10,11... | collective-permute-start | bytes 516104 | tf_op jit(solution)/shard_map/ppermute | solution.py:80
  32.4 8.2 %collective-permute-start.8 = (bf16[24,3584]{1,0:T(8,128)(2,1)S(1)}, bf16[24,3584]{1,0:T(8,128)(2,1)S(1)}, u32[]{:S(2)}, u32[]{:S(2)}) collective-permute-start(bf16[24,3584]{1,0:T(8,128)(2,1)S(1)} %get-tuple-element.27), channel_id=1, source_target_pairs={{0,2},{1,3},{2,0},{3,1},{4,6},{5,7},{6,4},{7,5},{8,10},{9,11},{10,... | collective-permute-start | bytes 516104 | tf_op jit(solution)/shard_map/ppermute | solution.py:80
  33.9 6.7 %collective-permute-start.9 = (bf16[24,3584]{1,0:T(8,128)(2,1)S(1)}, bf16[24,3584]{1,0:T(8,128)(2,1)S(1)}, u32[]{:S(2)}, u32[]{:S(2)}) collective-permute-start(bf16[24,3584]{1,0:T(8,128)(2,1)S(1)} %get-tuple-element.28), channel_id=1, source_target_pairs={{0,3},{1,2},{2,1},{3,0},{4,7},{5,6},{6,5},{7,4},{8,11},{9,10},{10,... | collective-permute-start | bytes 516104 | tf_op jit(solution)/shard_map/ppermute | solution.py:80
  41.0 4.7 %collective-permute-start.10 = (bf16[4,7168]{1,0:T(4,128)(2,1)S(1)}, bf16[4,7168]{1,0:T(4,128)(2,1)S(1)}, u32[]{:S(2)}, u32[]{:S(2)}) collective-permute-start(bf16[4,7168]{1,0:T(4,128)(2,1)S(1)} %get-tuple-element.30), channel_id=1, source_target_pairs={{0,8},{4,12},{8,0},{12,4},{16,24},{20,28},{24,16},{28,20},{1,9},{5... | collective-permute-start | bytes 172040 | tf_op jit(solution)/shard_map/ppermute | solution.py:80
  42.1 5.7 %collective-permute-start.11 = (bf16[4,7168]{1,0:T(4,128)(2,1)S(1)}, bf16[4,7168]{1,0:T(4,128)(2,1)S(1)}, u32[]{:S(2)}, u32[]{:S(2)}) collective-permute-start(bf16[4,7168]{1,0:T(4,128)(2,1)S(1)} %get-tuple-element.31), channel_id=1, source_target_pairs={{0,16},{4,20},{8,24},{12,28},{16,0},{20,4},{24,8},{28,12},{1,17},{... | collective-permute-start | bytes 172040 | tf_op jit(solution)/shard_map/ppermute | solution.py:80
  43.2 6.0 %collective-permute-start.12 = (bf16[4,7168]{1,0:T(4,128)(2,1)S(1)}, bf16[4,7168]{1,0:T(4,128)(2,1)S(1)}, u32[]{:S(2)}, u32[]{:S(2)}) collective-permute-start(bf16[4,7168]{1,0:T(4,128)(2,1)S(1)} %get-tuple-element.32), channel_id=1, source_target_pairs={{0,24},{4,28},{8,16},{12,20},{16,8},{20,12},{24,0},{28,4},{1,25},{... | collective-permute-start | bytes 172040 | tf_op jit(solution)/shard_map/ppermute | solution.py:80

commit v4 on v3

--- a/solution.py
+++ b/solution.py
@@ -6,6 +6,7 @@
 from jax.experimental import pallas as pl
 from jax.experimental.pallas import tpu as pltpu
 from jax.sharding import PartitionSpec as P
+
 
 E_WIN = 2
 BUCKETS = 4
@@ -82,7 +83,6 @@
 
 NT = (((1,), (1,)), ((), ()))
 VMEM = pl.BlockSpec(memory_space=pltpu.VMEM)
-SMEM = pl.BlockSpec(memory_space=pltpu.SMEM)
 ANY = pl.BlockSpec(memory_space=pl.ANY)
 HBM = pl.BlockSpec(memory_space=pltpu.HBM)
 CODE = 128
@@ -93,16 +93,30 @@
     return [pltpu.with_memory_space_constraint(value, pltpu.VMEM) for value in values]
 
 
+def in_hbm(*values):
+    return [pltpu.with_memory_space_constraint(value, pltpu.HBM) for value in values]
+
+
 def limit(mib):
     return pltpu.CompilerParams(vmem_limit_bytes=mib * MIB)
 
 
-def prepare_body(route_ref, rows_ref, gain_ref, out_ref):
+def prepare_body(route_hbm, rows_hbm, gain_hbm, out_ref, route_ref, rows_ref, gain_ref, sems):
+    copies = [
+        pltpu.make_async_copy(source, target, sems.at[index])
+        for index, (source, target) in enumerate(
+            ((rows_hbm, rows_ref), (gain_hbm, gain_ref), (route_hbm, route_ref))
+        )
+    ]
+    for copy in copies:
+        copy.start()
+    for copy in copies:
+        copy.wait()
     row_count, width = rows_ref.shape
     rows = rows_ref[...].astype(jnp.float32)
     scale = lax.rsqrt(jnp.sum(rows * rows, axis=1, keepdims=True) * (1.0 / width) + epsilon)
     out_ref[:, :width] = (rows * scale * gain_ref[...]).astype(jnp.bfloat16)
-    named = [route_ref[row] for row in range(row_count)]
+    named = [route_ref[0, row] for row in range(row_count)]
     at = lax.broadcasted_iota(jnp.int32, (row_count, CODE), 0)
     code = jnp.zeros((row_count, CODE), jnp.int32)
     for row in range(row_count):
@@ -141,13 +155,16 @@
         blocks[expert][...] = total[expert * block : (expert + 1) * block].astype(jnp.bfloat16)
 
 
-def fetch_body(piece, owner_ref, resident, own, other, after, both, down, has_ref, sems):
+def fetch_body(piece, owner, resident, after, both, has_ref, owner_ref, sems):
+    owner_copy = pltpu.make_async_copy(owner, owner_ref, sems.at[2 * PAIR])
+    owner_copy.start()
+    owner_copy.wait()
     group = lax.axis_index("grp")
     copies = []
     for which, holder in enumerate((group, group ^ 1)):
         bucket, has = jnp.int32(0), jnp.int32(0)
         for index in range(BUCKETS):
-            hit = owner_ref[index] == holder
+            hit = owner_ref[0, index] == holder
             bucket, has = jnp.where(hit, index, bucket), jnp.where(hit, 1, has)
         here = pl.ds(which * piece, piece)
         for part in range(2):
@@ -155,12 +172,9 @@
                 pltpu.make_async_copy(
                     resident.at[part, pl.ds(pl.multiple_of(bucket * piece, piece), piece)],
                     both.at[part, here],
-                    sems.at[3 * which + part],
+                    sems.at[2 * which + part],
                 )
             )
-        copies.append(
-            pltpu.make_async_copy((own, other)[which], down.at[here], sems.at[3 * which + 2])
-        )
         has_ref[here, :] = jnp.broadcast_to(has.astype(jnp.float32), (piece, has_ref.shape[1]))
     for copy in copies:
         copy.start()
@@ -168,8 +182,16 @@
         copy.wait()
 
 
-def expert_body(devices, chips, lanes, both, down, has_ref, *refs):
-    blocks, partials, stacked = refs[:devices], refs[devices : 2 * devices], refs[-1]
+def expert_body(devices, chips, lanes, own, other, both, has_ref, *refs):
+    blocks, partials = refs[:devices], refs[devices : 2 * devices]
+    stacked, down, sems = refs[2 * devices :]
+    piece = own.shape[0]
+    copies = [
+        pltpu.make_async_copy(source, down.at[pl.ds(index * piece, piece)], sems.at[index])
+        for index, source in enumerate((own, other))
+    ]
+    for copy in copies:
+        copy.start()
     block, half = blocks[0].shape
     used = devices * block
     for index in range(devices):
@@ -191,6 +213,8 @@
     act = jnp.where(valid & (has_ref[...] > 0.5), act, 0.0)
     above = act.T.astype(jnp.bfloat16)[:used]
     below = pltpu.roll(act, chips, 1).T.astype(jnp.bfloat16)[:used]
+    for copy in copies:
+        copy.wait()
     step = half // 7 if half % (7 * 128) == 0 else half
     for start in range(0, half, step):
         out = jnp.dot(above, down[:, start : start + step], preferred_element_type=jnp.float32)
@@ -252,14 +276,21 @@
     payload = pl.pallas_call(
         prepare_body,
         out_shape=pltpu.VMEM((row_count, width + CODE), jnp.bfloat16),
-        in_specs=[SMEM, VMEM, VMEM],
+        in_specs=[HBM] * 3,
         out_specs=VMEM,
+        scratch_shapes=[
+            pltpu.SMEM((1, row_count), jnp.int32),
+            pltpu.VMEM((row_count, width), jnp.bfloat16),
+            pltpu.VMEM((1, width), jnp.float32),
+            pltpu.SemaphoreType.DMA((3,)),
+        ],
         compiler_params=limit(4),
         name="prepare",
-    )(route.reshape(row_count), rows, norm_gain.reshape(1, width))
-    gathered = [payload] + [swap(payload, "grp", PAIR * hop) for hop in range(1, chips)]
-    own_piece, payload = lax.optimization_barrier((sectioned[0], payload))
-    other_piece = swap(own_piece, "grp", 1)
+    )(*in_hbm(route.reshape(1, row_count), rows, norm_gain.reshape(1, width)))
+    gathered = [payload]
+    for hop in range(1, chips):
+        gathered.append(swap(payload, "grp", PAIR * hop))
+    other_piece = swap(sectioned[0], "grp", 1)
     half_block = pltpu.VMEM((block, half), jnp.bfloat16)
     packed = pl.pallas_call(
         functools.partial(pack_body, chips, shards),
@@ -271,29 +302,35 @@
     )(*held(*gathered))
     blocks = [packed[bits // shards] for bits in range(devices)]
     blocks = [blocks[0]] + [swap(blocks[bits], "exp", bits) for bits in range(1, devices)]
-    both, down, has = pl.pallas_call(
+    both, has = pl.pallas_call(
         functools.partial(fetch_body, piece),
         out_shape=[
             pltpu.VMEM((2, PAIR * piece, width), jnp.bfloat16),
-            pltpu.VMEM((PAIR * piece, width), jnp.bfloat16),
             pltpu.VMEM((PAIR * piece, 128), jnp.float32),
         ],
-        in_specs=[SMEM, HBM, HBM, ANY, ANY],
-        out_specs=[VMEM] * 3,
-        scratch_shapes=[pltpu.SemaphoreType.DMA((3 * PAIR,))],
+        in_specs=[HBM, HBM, ANY],
+        out_specs=[VMEM] * 2,
+        scratch_shapes=[
+            pltpu.SMEM((1, owner.shape[0]), jnp.int32),
+            pltpu.SemaphoreType.DMA((2 * PAIR + 1,)),
+        ],
         compiler_params=limit(2),
         name="fetch",
-    )(owner, resident, sectioned[0], other_piece, packed[0])
+    )(*in_hbm(owner.reshape(1, -1), resident), *held(packed[0]))
     lanes = -(-devices * block // 128) * 128
     partials = pl.pallas_call(
         functools.partial(expert_body, devices, chips, lanes),
         out_shape=[half_block] * devices,
-        in_specs=[VMEM] * (3 + devices),
+        in_specs=[HBM, ANY] + [VMEM] * (2 + devices),
         out_specs=[VMEM] * devices,
-        scratch_shapes=[pltpu.VMEM((lanes, half), jnp.bfloat16)],
-        compiler_params=limit(12),
+        scratch_shapes=[
+            pltpu.VMEM((lanes, half), jnp.bfloat16),
+            pltpu.VMEM((PAIR * piece, width), jnp.bfloat16),
+            pltpu.SemaphoreType.DMA((PAIR,)),
+        ],
+        compiler_params=limit(16),
         name="expert",
-    )(*held(both, down, has, *blocks))
+    )(*in_hbm(sectioned[0]), *held(other_piece, both, has, *blocks))
     returned = [partials[0]] + [swap(partials[bits], "exp", bits) for bits in range(1, devices)]
     home = pltpu.VMEM((row_count, width), jnp.bfloat16)
     sums = pl.pallas_call(

time: 50.2 us -> 48.2 us (0.960)
  local copies, waits for them, and re-layouts: 9.55 us -> 0.01 us
  waiting for transfers between devices: 15.9 us -> 20.6 us
  Pallas kernels: 6.29 us -> 9.28 us
    unnamed x14 -> x2, local copies, waits for them, and re-layouts: 9.55 us -> 0.01 us
    ppermute x13, waiting for transfers between devices: 15.9 us -> 20.6 us  [swap(): return lax.ppermute(value, axis, [(i, i ^ bits) for i in range(size)])]
    pallas_call x1, Pallas kernels: 1.36 us -> 3.87 us  [move_rows(): pl.pallas_call(functools.partial(fetch_body, piece), out_shape=[pltpu.VME...]
  transfers between devices with their start and end apart: 13 -> 13, of which waited for: 7 -> 10; matrix products, arithmetic and copies ran while one was open for 0% -> 0% of each run, Pallas kernels for 4% -> 12%
where the time goes in v4:
time: 48.2 us; the launch traced here: 48 us
  waiting for transfers between devices  20.6 us (43%)
  starting transfers between devices  17.3 us (36%)
  Pallas kernels  9.28 us (19%)
  other arithmetic  0.71 us (1%)
    ppermute x13, waiting for transfers between devices, swap(): return lax.ppermute(value, axis, [(i, i ^ bits) for i in range(size)])  20.6 us
    ppermute x13, starting transfers between devices, swap(): return lax.ppermute(value, axis, [(i, i ^ bits) for i in range(size)])  17.3 us
    pallas_call x1, Pallas kernels, move_rows(): pl.pallas_call(functools.partial(fetch_body, piece), out_shape=[pltpu.VME...  3.87 us
    pallas_call x1, Pallas kernels, move_rows(): pl.pallas_call(functools.partial(expert_body, devices, chips, lanes), out...  3.11 us
    pallas_call x1, Pallas kernels, move_rows(): pl.pallas_call(prepare_body, out_shape=pltpu.VMEM((row_count, width + COD...  1.02 us
  transfers between devices with their start and end apart: 13, of which 10 were waited for; matrix products, arithmetic and copies ran while one was open for 0% of the time, Pallas kernels for 12%

profile of v4, /device:TPU:0, one launch (start us, length us, event | category | flops | bytes accessed | tf_op | source)
XLA Modules:
  0.0 48.0 jit_solution(10984667416611427212)
XLA Ops:
  0.0 0.5 %collective-permute-start.3 = (bf16[128,7168]{1,0:T(8,128)(2,1)}, bf16[128,7168]{1,0:T(8,128)(2,1)S(1)}, u32[]{:S(2)}, u32[]{:S(2)}) collective-permute-start(bf16[128,7168]{1,0:T(8,128)(2,1)} %bitcast.8), channel_id=1, source_target_pairs={{0,4},{4,0},{8,12},{12,8},{16,20},{20,16},{24,28},{28,24},{1,5},{5... | collective-permute-start | bytes 5505032 | tf_op jit(solution)/shard_map/ppermute | solution.py:81
  0.5 1.0 %prepare.1.refs_0_ = bf16[4,7296]{1,0:T(4,128)(2,1)S(1)} custom-call(s32[1,4]{1,0:T(1,128)} %bitcast.12, bf16[4,7168]{1,0:T(4,128)(2,1)} %bitcast.10, f32[1,7168]{1,0:T(1,128)} %bitcast.11), custom_call_target="tpu_custom_call" | custom-call | tf_op jit(solution)/shard_map/prepare/pallas_call | solution.py:276
  1.5 4.7 %collective-permute-start.2 = (bf16[4,7296]{1,0:T(4,128)(2,1)S(1)}, bf16[4,7296]{1,0:T(4,128)(2,1)S(1)}, u32[]{:S(2)}, u32[]{:S(2)}) collective-permute-start(bf16[4,7296]{1,0:T(4,128)(2,1)S(1)} %prepare.1.refs_0_), channel_id=1, source_target_pairs={{0,24},{4,28},{8,16},{12,20},{16,8},{20,12},{24,0},{28,4},{1,25},{... | collective-permute-start | bytes 175112 | tf_op jit(solution)/shard_map/ppermute | solution.py:81
  6.2 0.0 collective-permute-start.1
  6.2 0.6 %collective-permute-start = (bf16[4,7296]{1,0:T(4,128)(2,1)S(1)}, bf16[4,7296]{1,0:T(4,128)(2,1)S(1)}, u32[]{:S(2)}, u32[]{:S(2)}) collective-permute-start(bf16[4,7296]{1,0:T(4,128)(2,1)S(1)} %prepare.1.refs_0_), channel_id=1, source_target_pairs={{0,8},{4,12},{8,0},{12,4},{16,24},{20,28},{24,16},{28,20},{1,9},{5... | collective-permute-start | bytes 175112 | tf_op jit(solution)/shard_map/ppermute | solution.py:81
  6.8 2.1 %collective-permute-done.2.refs_3_ = bf16[4,7296]{1,0:T(4,128)(2,1)S(1)} collective-permute-done((bf16[4,7296]{1,0:T(4,128)(2,1)S(1)}, bf16[4,7296]{1,0:T(4,128)(2,1)S(1)}, u32[]{:S(2)}, u32[]{:S(2)}) %collective-permute-start.2) | collective-permute-done | bytes 58400 | tf_op jit(solution)/shard_map/ppermute | solution.py:81
  8.9 2.8 %collective-permute-done.1.refs_2_ = bf16[4,7296]{1,0:T(4,128)(2,1)S(1)} collective-permute-done((bf16[4,7296]{1,0:T(4,128)(2,1)S(1)}, bf16[4,7296]{1,0:T(4,128)(2,1)S(1)}, u32[]{:S(2)}, u32[]{:S(2)}) %collective-permute-start.1) | collective-permute-done | bytes 58400 | tf_op jit(solution)/shard_map/ppermute | solution.py:81
  11.7 0.0 collective-permute-done.refs_1_
  11.7 0.9 %pack.1 = (bf16[24,3584]{1,0:T(8,128)(2,1)S(1)}, bf16[24,3584]{1,0:T(8,128)(2,1)S(1)}) custom-call(bf16[4,7296]{1,0:T(4,128)(2,1)S(1)} %prepare.1.refs_0_, bf16[4,7296]{1,0:T(4,128)(2,1)S(1)} %collective-permute-done.refs_1_, bf16[4,7296]{1,0:T(4,128)(2,1)S(1)} %collective-permute-done.1.refs_2_, bf16[4,7296]{1,0:T(4,128)(2,1)S(1)} %collective-permute-done.2.refs_3_), custom_call_target="tpu_custom_call" | custom-call | tf_op jit(solution)/shard_map/pack/pallas_call | solution.py:295
  12.6 2.5 %collective-permute-start.6 = (bf16[24,3584]{1,0:T(8,128)(2,1)S(1)}, bf16[24,3584]{1,0:T(8,128)(2,1)S(1)}, u32[]{:S(2)}, u32[]{:S(2)}) collective-permute-start(bf16[24,3584]{1,0:T(8,128)(2,1)S(1)} %get-tuple-element.20), channel_id=1, source_target_pairs={{0,3},{1,2},{2,1},{3,0},{4,7},{5,6},{6,5},{7,4},{8,11},{9,10},{10,... | collective-permute-start | bytes 516104 | tf_op jit(solution)/shard_map/ppermute | solution.py:81
  15.1 0.5 %collective-permute-start.5 = (bf16[24,3584]{1,0:T(8,128)(2,1)S(1)}, bf16[24,3584]{1,0:T(8,128)(2,1)S(1)}, u32[]{:S(2)}, u32[]{:S(2)}) collective-permute-start(bf16[24,3584]{1,0:T(8,128)(2,1)S(1)} %get-tuple-element.20), channel_id=1, source_target_pairs={{0,2},{1,3},{2,0},{3,1},{4,6},{5,7},{6,4},{7,5},{8,10},{9,11},{10,... | collective-permute-start | bytes 516104 | tf_op jit(solution)/shard_map/ppermute | solution.py:81
  15.6 0.5 %collective-permute-start.4 = (bf16[24,3584]{1,0:T(8,128)(2,1)S(1)}, bf16[24,3584]{1,0:T(8,128)(2,1)S(1)}, u32[]{:S(2)}, u32[]{:S(2)}) collective-permute-start(bf16[24,3584]{1,0:T(8,128)(2,1)S(1)} %get-tuple-element.17.after.refs_0_), channel_id=1, source_target_pairs={{0,1},{1,0},{2,3},{3,2},{4,5},{5,4},{6,7},{7,6},{8,9},{9,8},{10,11... | collective-permute-start | bytes 516104 | tf_op jit(solution)/shard_map/ppermute | solution.py:81
  16.1 3.9 %fetch.1 = (bf16[2,256,7168]{2,1,0:T(8,128)(2,1)S(1)}, f32[256,128]{1,0:T(8,128)S(1)}) custom-call(s32[1,8]{1,0:T(1,128)} %bitcast.13, bf16[2,512,7168]{2,1,0:T(8,128)(2,1)} %resident.1, bf16[24,3584]{1,0:T(8,128)(2,1)S(1)} %get-tuple-element.17.after.refs_0_), custom_call_target="tpu_custom_call" | custom-call | tf_op jit(solution)/shard_map/fetch/pallas_call | solution.py:305
  20.0 0.0 copy-start
  20.0 0.8 %collective-permute-done.6.refs_3_ = bf16[24,3584]{1,0:T(8,128)(2,1)S(1)} collective-permute-done((bf16[24,3584]{1,0:T(8,128)(2,1)S(1)}, bf16[24,3584]{1,0:T(8,128)(2,1)S(1)}, u32[]{:S(2)}, u32[]{:S(2)}) %collective-permute-start.6) | collective-permute-done | bytes 172064 | tf_op jit(solution)/shard_map/ppermute | solution.py:81
  20.8 2.6 %collective-permute-done.5.refs_2_ = bf16[24,3584]{1,0:T(8,128)(2,1)S(1)} collective-permute-done((bf16[24,3584]{1,0:T(8,128)(2,1)S(1)}, bf16[24,3584]{1,0:T(8,128)(2,1)S(1)}, u32[]{:S(2)}, u32[]{:S(2)}) %collective-permute-start.5) | collective-permute-done | bytes 172064 | tf_op jit(solution)/shard_map/ppermute | solution.py:81
  23.4 0.1 collective-permute-done.4.refs_1_
  23.5 0.0 collective-permute-done.3.other
  23.5 3.1 %expert.1 = (bf16[24,3584]{1,0:T(8,128)(2,1)S(1)}, bf16[24,3584]{1,0:T(8,128)(2,1)S(1)}, bf16[24,3584]{1,0:T(8,128)(2,1)S(1)}, bf16[24,3584]{1,0:T(8,128)(2,1)S(1)}) custom-call(bf16[128,7168]{1,0:T(8,128)(2,1)} %bitcast.9, bf16[128,7168]{1,0:T(8,128)(2,1)S(1)} %collective-permute-done.3.other, bf16[2,256,7168]{2,1,0:T(8,128)(2,1)S(1)} %get-tuple-element.18.both, ...), custom_call_target="tpu_custom_call" | custom-call | tf_op jit(solution)/shard_map/expert/pallas_call | solution.py:321
  26.6 1.6 %collective-permute-start.7 = (bf16[24,3584]{1,0:T(8,128)(2,1)S(1)}, bf16[24,3584]{1,0:T(8,128)(2,1)S(1)}, u32[]{:S(2)}, u32[]{:S(2)}) collective-permute-start(bf16[24,3584]{1,0:T(8,128)(2,1)S(1)} %get-tuple-element.22), channel_id=1, source_target_pairs={{0,1},{1,0},{2,3},{3,2},{4,5},{5,4},{6,7},{7,6},{8,9},{9,8},{10,11... | collective-permute-start | bytes 516104 | tf_op jit(solution)/shard_map/ppermute | solution.py:81
  28.2 0.7 %collective-permute-start.8 = (bf16[24,3584]{1,0:T(8,128)(2,1)S(1)}, bf16[24,3584]{1,0:T(8,128)(2,1)S(1)}, u32[]{:S(2)}, u32[]{:S(2)}) collective-permute-start(bf16[24,3584]{1,0:T(8,128)(2,1)S(1)} %get-tuple-element.23), channel_id=1, source_target_pairs={{0,2},{1,3},{2,0},{3,1},{4,6},{5,7},{6,4},{7,5},{8,10},{9,11},{10,... | collective-permute-start | bytes 516104 | tf_op jit(solution)/shard_map/ppermute | solution.py:81
  28.9 1.3 %collective-permute-start.9 = (bf16[24,3584]{1,0:T(8,128)(2,1)S(1)}, bf16[24,3584]{1,0:T(8,128)(2,1)S(1)}, u32[]{:S(2)}, u32[]{:S(2)}) collective-permute-start(bf16[24,3584]{1,0:T(8,128)(2,1)S(1)} %get-tuple-element.24), channel_id=1, source_target_pairs={{0,3},{1,2},{2,1},{3,0},{4,7},{5,6},{6,5},{7,4},{8,11},{9,10},{10,... | collective-permute-start | bytes 516104 | tf_op jit(solution)/shard_map/ppermute | solution.py:81
  30.2 3.8 %collective-permute-done.7.refs_5_ = bf16[24,3584]{1,0:T(8,128)(2,1)S(1)} collective-permute-done((bf16[24,3584]{1,0:T(8,128)(2,1)S(1)}, bf16[24,3584]{1,0:T(8,128)(2,1)S(1)}, u32[]{:S(2)}, u32[]{:S(2)}) %collective-permute-start.7) | collective-permute-done | bytes 172064 | tf_op jit(solution)/shard_map/ppermute | solution.py:81
  34.0 3.9 %collective-permute-done.8.refs_6_ = bf16[24,3584]{1,0:T(8,128)(2,1)S(1)} collective-permute-done((bf16[24,3584]{1,0:T(8,128)(2,1)S(1)}, bf16[24,3584]{1,0:T(8,128)(2,1)S(1)}, u32[]{:S(2)}, u32[]{:S(2)}) %collective-permute-start.8) | collective-permute-done | bytes 172064 | tf_op jit(solution)/shard_map/ppermute | solution.py:81
  37.8 0.0 collective-permute-done.9.refs_7_
  37.8 0.4 combine.1
  38.2 1.2 %collective-permute-start.10 = (bf16[4,7168]{1,0:T(4,128)(2,1)S(1)}, bf16[4,7168]{1,0:T(4,128)(2,1)S(1)}, u32[]{:S(2)}, u32[]{:S(2)}) collective-permute-start(bf16[4,7168]{1,0:T(4,128)(2,1)S(1)} %get-tuple-element.26), channel_id=1, source_target_pairs={{0,8},{4,12},{8,0},{12,4},{16,24},{20,28},{24,16},{28,20},{1,9},{5... | collective-permute-start | bytes 172040 | tf_op jit(solution)/shard_map/ppermute | solution.py:81
  39.4 1.9 %collective-permute-start.11 = (bf16[4,7168]{1,0:T(4,128)(2,1)S(1)}, bf16[4,7168]{1,0:T(4,128)(2,1)S(1)}, u32[]{:S(2)}, u32[]{:S(2)}) collective-permute-start(bf16[4,7168]{1,0:T(4,128)(2,1)S(1)} %get-tuple-element.27), channel_id=1, source_target_pairs={{0,16},{4,20},{8,24},{12,28},{16,0},{20,4},{24,8},{28,12},{1,17},{... | collective-permute-start | bytes 172040 | tf_op jit(solution)/shard_map/ppermute | solution.py:81
  41.3 1.4 %collective-permute-start.12 = (bf16[4,7168]{1,0:T(4,128)(2,1)S(1)}, bf16[4,7168]{1,0:T(4,128)(2,1)S(1)}, u32[]{:S(2)}, u32[]{:S(2)}) collective-permute-start(bf16[4,7168]{1,0:T(4,128)(2,1)S(1)} %get-tuple-element.28), channel_id=1, source_target_pairs={{0,24},{4,28},{8,16},{12,20},{16,8},{20,12},{24,0},{28,4},{1,25},{... | collective-permute-start | bytes 172040 | tf_op jit(solution)/shard_map/ppermute | solution.py:81
  42.7 0.1 collective-permute-done.10
  42.8 3.0 %collective-permute-done.11 = bf16[4,7168]{1,0:T(4,128)(2,1)S(1)} collective-permute-done((bf16[4,7168]{1,0:T(4,128)(2,1)S(1)}, bf16[4,7168]{1,0:T(4,128)(2,1)S(1)}, u32[]{:S(2)}, u32[]{:S(2)}) %collective-permute-start.11) | collective-permute-done | bytes 57376 | tf_op jit(solution)/shard_map/ppermute | solution.py:81
  45.7 1.6 %collective-permute-done.12 = bf16[4,7168]{1,0:T(4,128)(2,1)S(1)} collective-permute-done((bf16[4,7168]{1,0:T(4,128)(2,1)S(1)}, bf16[4,7168]{1,0:T(4,128)(2,1)S(1)}, u32[]{:S(2)}, u32[]{:S(2)}) %collective-permute-start.12) | collective-permute-done | bytes 57376 | tf_op jit(solution)/shard_map/ppermute | solution.py:81
  47.3 0.0 copy-done
  47.3 0.7 %fusion = bf16[1,4,7168]{2,1,0:T(4,128)(2,1)} fusion(bf16[4,7168]{1,0:T(4,128)(2,1)S(1)} %collective-permute-done.12, bf16[4,7168]{1,0:T(4,128)(2,1)S(1)} %collective-permute-done.11, bf16[4,7168]{1,0:T(4,128)(2,1)S(1)} %collective-permute-done.10, bf16[4,7168]{1,0:T(4,128)(2,1)S(1)} %get-tuple-element.25, f32[4]{0:T(128)S(1)} %bitcast.14), kind=kLoop, calls=%fused_computation.1 | loop fusion | flops 258048 | bytes 286736 | tf_op jit(solution)/shard_map/reshape | solution.py:349
Async XLA Ops:
  0.0 23.5 %collective-permute-start.3 = (bf16[128,7168]{1,0:T(8,128)(2,1)}, bf16[128,7168]{1,0:T(8,128)(2,1)S(1)}, u32[]{:S(2)}, u32[]{:S(2)}) collective-permute-start(bf16[128,7168]{1,0:T(8,128)(2,1)} %bitcast.8), channel_id=1, source_target_pairs={{0,4},{4,0},{8,12},{12,8},{16,20},{20,16},{24,28},{28,24},{1,5},{5... | collective-permute-start | bytes 5505032 | tf_op jit(solution)/shard_map/ppermute | solution.py:81
  1.5 7.4 %collective-permute-start.2 = (bf16[4,7296]{1,0:T(4,128)(2,1)S(1)}, bf16[4,7296]{1,0:T(4,128)(2,1)S(1)}, u32[]{:S(2)}, u32[]{:S(2)}) collective-permute-start(bf16[4,7296]{1,0:T(4,128)(2,1)S(1)} %prepare.1.refs_0_), channel_id=1, source_target_pairs={{0,24},{4,28},{8,16},{12,20},{16,8},{20,12},{24,0},{28,4},{1,25},{... | collective-permute-start | bytes 175112 | tf_op jit(solution)/shard_map/ppermute | solution.py:81
  6.2 5.5 %collective-permute-start.1 = (bf16[4,7296]{1,0:T(4,128)(2,1)S(1)}, bf16[4,7296]{1,0:T(4,128)(2,1)S(1)}, u32[]{:S(2)}, u32[]{:S(2)}) collective-permute-start(bf16[4,7296]{1,0:T(4,128)(2,1)S(1)} %prepare.1.refs_0_), channel_id=1, source_target_pairs={{0,16},{4,20},{8,24},{12,28},{16,0},{20,4},{24,8},{28,12},{1,17},{... | collective-permute-start | bytes 175112 | tf_op jit(solution)/shard_map/ppermute | solution.py:81
  6.2 5.5 %collective-permute-start = (bf16[4,7296]{1,0:T(4,128)(2,1)S(1)}, bf16[4,7296]{1,0:T(4,128)(2,1)S(1)}, u32[]{:S(2)}, u32[]{:S(2)}) collective-permute-start(bf16[4,7296]{1,0:T(4,128)(2,1)S(1)} %prepare.1.refs_0_), channel_id=1, source_target_pairs={{0,8},{4,12},{8,0},{12,4},{16,24},{20,28},{24,16},{28,20},{1,9},{5... | collective-permute-start | bytes 175112 | tf_op jit(solution)/shard_map/ppermute | solution.py:81
  12.6 8.2 %collective-permute-start.6 = (bf16[24,3584]{1,0:T(8,128)(2,1)S(1)}, bf16[24,3584]{1,0:T(8,128)(2,1)S(1)}, u32[]{:S(2)}, u32[]{:S(2)}) collective-permute-start(bf16[24,3584]{1,0:T(8,128)(2,1)S(1)} %get-tuple-element.20), channel_id=1, source_target_pairs={{0,3},{1,2},{2,1},{3,0},{4,7},{5,6},{6,5},{7,4},{8,11},{9,10},{10,... | collective-permute-start | bytes 516104 | tf_op jit(solution)/shard_map/ppermute | solution.py:81
  15.1 8.3 %collective-permute-start.5 = (bf16[24,3584]{1,0:T(8,128)(2,1)S(1)}, bf16[24,3584]{1,0:T(8,128)(2,1)S(1)}, u32[]{:S(2)}, u32[]{:S(2)}) collective-permute-start(bf16[24,3584]{1,0:T(8,128)(2,1)S(1)} %get-tuple-element.20), channel_id=1, source_target_pairs={{0,2},{1,3},{2,0},{3,1},{4,6},{5,7},{6,4},{7,5},{8,10},{9,11},{10,... | collective-permute-start | bytes 516104 | tf_op jit(solution)/shard_map/ppermute | solution.py:81
  15.6 7.9 %collective-permute-start.4 = (bf16[24,3584]{1,0:T(8,128)(2,1)S(1)}, bf16[24,3584]{1,0:T(8,128)(2,1)S(1)}, u32[]{:S(2)}, u32[]{:S(2)}) collective-permute-start(bf16[24,3584]{1,0:T(8,128)(2,1)S(1)} %get-tuple-element.17.after.refs_0_), channel_id=1, source_target_pairs={{0,1},{1,0},{2,3},{3,2},{4,5},{5,4},{6,7},{7,6},{8,9},{9,8},{10,11... | collective-permute-start | bytes 516104 | tf_op jit(solution)/shard_map/ppermute | solution.py:81
  20.0 27.3 %copy-start = (f32[1,4]{1,0:T(1,128)S(1)}, f32[1,4]{1,0:T(1,128)}, u32[]{:S(2)}) copy-start(f32[1,4]{1,0:T(1,128)} %param.10) | copy-start | bytes 52
  26.6 7.3 %collective-permute-start.7 = (bf16[24,3584]{1,0:T(8,128)(2,1)S(1)}, bf16[24,3584]{1,0:T(8,128)(2,1)S(1)}, u32[]{:S(2)}, u32[]{:S(2)}) collective-permute-start(bf16[24,3584]{1,0:T(8,128)(2,1)S(1)} %get-tuple-element.22), channel_id=1, source_target_pairs={{0,1},{1,0},{2,3},{3,2},{4,5},{5,4},{6,7},{7,6},{8,9},{9,8},{10,11... | collective-permute-start | bytes 516104 | tf_op jit(solution)/shard_map/ppermute | solution.py:81
  28.2 9.6 %collective-permute-start.8 = (bf16[24,3584]{1,0:T(8,128)(2,1)S(1)}, bf16[24,3584]{1,0:T(8,128)(2,1)S(1)}, u32[]{:S(2)}, u32[]{:S(2)}) collective-permute-start(bf16[24,3584]{1,0:T(8,128)(2,1)S(1)} %get-tuple-element.23), channel_id=1, source_target_pairs={{0,2},{1,3},{2,0},{3,1},{4,6},{5,7},{6,4},{7,5},{8,10},{9,11},{10,... | collective-permute-start | bytes 516104 | tf_op jit(solution)/shard_map/ppermute | solution.py:81
  28.9 8.9 %collective-permute-start.9 = (bf16[24,3584]{1,0:T(8,128)(2,1)S(1)}, bf16[24,3584]{1,0:T(8,128)(2,1)S(1)}, u32[]{:S(2)}, u32[]{:S(2)}) collective-permute-start(bf16[24,3584]{1,0:T(8,128)(2,1)S(1)} %get-tuple-element.24), channel_id=1, source_target_pairs={{0,3},{1,2},{2,1},{3,0},{4,7},{5,6},{6,5},{7,4},{8,11},{9,10},{10,... | collective-permute-start | bytes 516104 | tf_op jit(solution)/shard_map/ppermute | solution.py:81
  38.2 4.5 %collective-permute-start.10 = (bf16[4,7168]{1,0:T(4,128)(2,1)S(1)}, bf16[4,7168]{1,0:T(4,128)(2,1)S(1)}, u32[]{:S(2)}, u32[]{:S(2)}) collective-permute-start(bf16[4,7168]{1,0:T(4,128)(2,1)S(1)} %get-tuple-element.26), channel_id=1, source_target_pairs={{0,8},{4,12},{8,0},{12,4},{16,24},{20,28},{24,16},{28,20},{1,9},{5... | collective-permute-start | bytes 172040 | tf_op jit(solution)/shard_map/ppermute | solution.py:81
  39.4 6.3 %collective-permute-start.11 = (bf16[4,7168]{1,0:T(4,128)(2,1)S(1)}, bf16[4,7168]{1,0:T(4,128)(2,1)S(1)}, u32[]{:S(2)}, u32[]{:S(2)}) collective-permute-start(bf16[4,7168]{1,0:T(4,128)(2,1)S(1)} %get-tuple-element.27), channel_id=1, source_target_pairs={{0,16},{4,20},{8,24},{12,28},{16,0},{20,4},{24,8},{28,12},{1,17},{... | collective-permute-start | bytes 172040 | tf_op jit(solution)/shard_map/ppermute | solution.py:81
  41.3 6.0 %collective-permute-start.12 = (bf16[4,7168]{1,0:T(4,128)(2,1)S(1)}, bf16[4,7168]{1,0:T(4,128)(2,1)S(1)}, u32[]{:S(2)}, u32[]{:S(2)}) collective-permute-start(bf16[4,7168]{1,0:T(4,128)(2,1)S(1)} %get-tuple-element.28), channel_id=1, source_target_pairs={{0,24},{4,28},{8,16},{12,20},{16,8},{20,12},{24,0},{28,4},{1,25},{... | collective-permute-start | bytes 172040 | tf_op jit(solution)/shard_map/ppermute | solution.py:81

commit v5 on v4

v5 whole, which is shorter than its diff:
```python
import functools

import jax
import jax.numpy as jnp
from jax import lax
from jax.experimental import pallas as pl
from jax.experimental.pallas import tpu as pltpu
from jax.sharding import PartitionSpec as P


E_WIN = 2
BUCKETS = 4
CAP = 3
PAIR = 2


epsilon = 1e-06


def from_root(value, axis, source):
    kept = jnp.where(lax.axis_index(axis) == source, value, 0).astype(value.dtype)
    return lax.psum(kept, axis)


def activate(slot_rows, gate_up):
    gate_part = lax.dot_general(
        slot_rows, gate_up[0], (((1,), (1,)), ((), ())), preferred_element_type=jnp.float32
    )
    up_part = lax.dot_general(
        slot_rows, gate_up[1], (((1,), (1,)), ((), ())), preferred_element_type=jnp.float32
    )
    return (jax.nn.silu(gate_part) * up_part).astype(jnp.bfloat16)


def normalize(rows, norm_gain):
    row_data = rows.astype(jnp.float32)
    scale = lax.rsqrt(jnp.mean(row_data * row_data, axis=1, keepdims=True) + epsilon)
    return (row_data * scale * norm_gain[None, :]).astype(jnp.bfloat16)


def move_weights(hidden, norm_gain, route, route_weight, resident, sectioned, owner):
    normed = normalize(hidden[0], norm_gain)
    row_count, width = normed.shape
    devices = lax.axis_size("exp")
    shards = devices // E_WIN
    expert_ids = route[0, :, 0]
    onehot = (expert_ids[:, None] == jnp.arange(E_WIN, dtype=jnp.int32)[None, :]).astype(jnp.int32)
    position = jnp.cumsum(onehot, axis=0) - onehot
    slot_index = jnp.sum(position * onehot, axis=1)
    placing = onehot[:, :, None] * (
        slot_index[:, None, None] == jnp.arange(CAP, dtype=jnp.int32)[None, None, :]
    ).astype(jnp.int32)
    placing = placing.reshape(row_count, E_WIN * CAP)
    packed = jnp.dot(
        placing.astype(jnp.bfloat16).T, normed, preferred_element_type=jnp.float32
    ).astype(jnp.bfloat16)
    packed = packed.reshape(E_WIN, 1, CAP, width)
    outgoing = jnp.broadcast_to(packed, (E_WIN, shards, CAP, width)).reshape(devices, CAP, width)
    piece_rows = sectioned.shape[1]
    arrived = lax.all_to_all(outgoing, "exp", split_axis=0, concat_axis=0, tiled=True)
    flat_slots = arrived.reshape(-1, width)
    activation = activate(flat_slots, resident)
    running_sum = jnp.zeros((flat_slots.shape[0], width), jnp.float32)
    for bucket in range(BUCKETS):
        weight_piece = from_root(sectioned[0], "grp", owner[bucket])
        act_piece = activation[:, bucket * piece_rows : (bucket + 1) * piece_rows]
        running_sum = running_sum + jnp.dot(
            act_piece, weight_piece, preferred_element_type=jnp.float32
        )
    partials = running_sum.astype(jnp.bfloat16).reshape(arrived.shape)
    returned = lax.all_to_all(partials, "exp", split_axis=0, concat_axis=0, tiled=True)
    summed = jnp.sum(returned.astype(jnp.float32).reshape(E_WIN, shards, CAP, width), axis=1)
    summed = summed.reshape(E_WIN * CAP, width)
    combined = jnp.dot(placing.astype(jnp.float32), summed, precision=lax.Precision.HIGHEST)
    result = (combined * route_weight[0][:, None]).astype(jnp.bfloat16)
    return result.reshape(1, row_count, width)


def swap(value, axis, bits):
    size = lax.axis_size(axis)
    return lax.ppermute(value, axis, [(i, i ^ bits) for i in range(size)])


NT = (((1,), (1,)), ((), ()))
VMEM = pl.BlockSpec(memory_space=pltpu.VMEM)
ANY = pl.BlockSpec(memory_space=pl.ANY)
HBM = pl.BlockSpec(memory_space=pltpu.HBM)
CODE = 128
MIB = 1 << 20


def held(*values):
    return [pltpu.with_memory_space_constraint(value, pltpu.VMEM) for value in values]


def in_hbm(*values):
    return [pltpu.with_memory_space_constraint(value, pltpu.HBM) for value in values]


def limit(mib):
    return pltpu.CompilerParams(vmem_limit_bytes=mib * MIB)


def prepare_body(shards, route_hbm, rows_hbm, gain_hbm, *refs):
    blocks, code_ref = refs[:E_WIN], refs[E_WIN]
    route_ref, rows_ref, gain_ref, sems = refs[E_WIN + 1 :]
    copies = [
        pltpu.make_async_copy(source, target, sems.at[index])
        for index, (source, target) in enumerate(
            ((rows_hbm, rows_ref), (gain_hbm, gain_ref), (route_hbm, route_ref))
        )
    ]
    for copy in copies:
        copy.start()
    for copy in copies:
        copy.wait()
    row_count, width = rows_ref.shape
    rows = rows_ref[...].astype(jnp.float32)
    scale = lax.rsqrt(jnp.sum(rows * rows, axis=1, keepdims=True) * (1.0 / width) + epsilon)
    normed = (rows * scale * gain_ref[...]).astype(jnp.bfloat16)
    named = [route_ref[0, row] for row in range(row_count)]
    at = lax.broadcasted_iota(jnp.int32, code_ref.shape, 1)
    code = jnp.full(code_ref.shape, -1, jnp.int32)
    for row in range(row_count):
        slot = jnp.int32(0)
        for before in range(row):
            slot = slot + jnp.where(named[before] == named[row], 1, 0)
        code = jnp.where(at == row, named[row] * row_count + slot, code)
    code_ref[...] = code.astype(jnp.float32)
    mine = lax.axis_index("exp") // shards
    height = E_WIN * row_count
    row = lax.broadcasted_iota(jnp.int32, (height, CODE), 0)
    wanted = (mine ^ (row // row_count)) * row_count + row % row_count
    placing = jnp.where(wanted == code[0:1], 1.0, 0.0).astype(jnp.bfloat16)[:, :row_count]
    packed = jnp.dot(placing, normed, preferred_element_type=jnp.float32)
    for expert in range(E_WIN):
        blocks[expert][...] = packed[expert * row_count : (expert + 1) * row_count].astype(
            jnp.bfloat16
        )


def ahead_body(owner, resident, after, early, flags, owner_ref, sems):
    early_copy = pltpu.make_async_copy(resident.at[:, pl.ds(0, early.shape[1])], early, sems.at[0])
    early_copy.start()
    owner_copy = pltpu.make_async_copy(owner, owner_ref, sems.at[1])
    owner_copy.start()
    owner_copy.wait()
    group = lax.axis_index("grp")
    row = lax.broadcasted_iota(jnp.int32, flags.shape, 0)
    values = jnp.zeros(flags.shape, jnp.float32)
    for which in range(PAIR):
        for bucket in range(BUCKETS):
            hit = jnp.where(owner_ref[0, bucket] == (group ^ which), 1.0, 0.0)
            values = jnp.where(row == which * BUCKETS + bucket, hit, values)
    flags[...] = values
    early_copy.wait()


def activate_body(devices, resident, early, code_ref, *refs):
    blocks, out = refs[:devices], refs[devices]
    late, stacked, sem = refs[devices + 1 :]
    first = early.shape[1]
    late_copy = pltpu.make_async_copy(
        resident.at[:, pl.ds(first, late.shape[1])], late, sem.at[0]
    )
    late_copy.start()
    row_count = blocks[0].shape[0]
    for index in range(devices):
        stacked[index * row_count : (index + 1) * row_count, :] = blocks[index][...].astype(
            jnp.float32
        )
    rows = stacked[...].astype(jnp.bfloat16)

    def hidden_units(weights):
        gate = lax.dot_general(weights[0], rows, NT, preferred_element_type=jnp.float32)
        up = lax.dot_general(weights[1], rows, NT, preferred_element_type=jnp.float32)
        return (gate * jax.nn.sigmoid(gate) * up).T

    out[:, :first] = hidden_units(early).astype(jnp.bfloat16)
    late_copy.wait()
    out[:, first:] = hidden_units(late).astype(jnp.bfloat16)
    head = out[:, :CODE]
    spare = lax.broadcasted_iota(jnp.int32, head.shape, 0) == CAP
    out[:, :CODE] = jnp.where(spare, code_ref[0:1, :], head.astype(jnp.float32)).astype(
        jnp.bfloat16
    )


def hold_body(own, other, after, down, sems):
    piece = own.shape[0]
    copies = [
        pltpu.make_async_copy(source, down.at[pl.ds(index * piece, piece)], sems.at[index])
        for index, source in enumerate((own, other))
    ]
    for copy in copies:
        copy.start()
    for copy in copies:
        copy.wait()


def down_body(devices, chips, down, flags, *refs):
    acts, partials = refs[:chips], refs[chips:]
    block, half = partials[0].shape
    used = devices * block
    rows, units = acts[0].shape
    row_count, piece = rows // devices, units // BUCKETS
    row = lax.broadcasted_iota(jnp.int32, (2 * used, rows), 0)
    column = lax.broadcasted_iota(jnp.int32, (2 * used, rows), 1)
    lower, within = row // used, row % used
    home, spot = within // block, within % block
    slot, part, chip_at = spot // (2 * chips), (spot % (2 * chips)) // chips, spot % chips
    matches = (part == lower) & (home == column // row_count) & (slot == column % row_count)
    placed = jnp.zeros((2 * used, PAIR * piece), jnp.float32)
    for chip in range(chips):
        picked = []
        for which in range(PAIR):
            chosen = jnp.zeros((rows, piece), jnp.float32)
            for bucket in range(BUCKETS):
                flag = flags[which * BUCKETS + bucket : which * BUCKETS + bucket + 1, 0:piece]
                piece_of = acts[chip][:, bucket * piece : (bucket + 1) * piece].astype(jnp.float32)
                chosen = jnp.where(flag > 0.5, piece_of, chosen)
            picked.append(chosen.astype(jnp.bfloat16))
        placing = jnp.where(matches & (chip_at == chip), 1.0, 0.0).astype(jnp.bfloat16)
        placed = placed + jnp.dot(
            placing, jnp.concatenate(picked, axis=1), preferred_element_type=jnp.float32
        )
    placed = placed.astype(jnp.bfloat16)
    above, below = placed[:used], placed[used:]
    step = half // 7 if half % (7 * 128) == 0 else half
    for start in range(0, half, step):
        out = jnp.dot(above, down[:, start : start + step], preferred_element_type=jnp.float32)
        out = out + jnp.dot(
            below, down[:, half + start : half + start + step], preferred_element_type=jnp.float32
        )
        for index in range(devices):
            partials[index][:, start : start + step] = out[
                index * block : (index + 1) * block
            ].astype(jnp.bfloat16)


def combine_body(devices, chips, shards, *refs):
    acts, blocks = refs[:chips], refs[chips : chips + devices]
    outs, codes = refs[chips + devices : -1], refs[-1]
    block, half = blocks[0].shape
    row_count = outs[0].shape[0]
    mine = lax.axis_index("exp") // shards
    diagonal = lax.broadcasted_iota(jnp.int32, (row_count, CODE), 0) == lax.broadcasted_iota(
        jnp.int32, (row_count, CODE), 1
    )
    for chip in range(chips):
        line = acts[chip][:, :CODE].astype(jnp.float32)[CAP : CAP + 1, :]
        mark = jnp.sum(jnp.where(diagonal, line, 0.0), axis=1, keepdims=True)
        codes[chip * row_count : (chip + 1) * row_count, :] = jnp.broadcast_to(
            mark, (row_count, CODE)
        )
    code = codes[...]
    home = lax.broadcasted_iota(jnp.int32, code.shape, 0) // row_count
    at = lax.broadcasted_iota(jnp.int32, code.shape, 1)
    at_slot, at_part, at_chip = at // (2 * chips), (at % (2 * chips)) // chips, at % chips
    placing = []
    for expert in range(E_WIN):
        wanted = ((mine ^ expert) * row_count + at_slot).astype(jnp.float32)
        chosen = (wanted == code) & (at_chip == home) & (at < block)
        placing.append(
            [
                jnp.where(chosen & (at_part == part), 1.0, 0.0).astype(jnp.bfloat16)[:, :block]
                for part in range(2)
            ]
        )
    for part in range(2):
        total = 0.0
        for index in range(devices):
            total = total + jnp.dot(
                placing[index // shards][part],
                blocks[index][...],
                preferred_element_type=jnp.float32,
            )
        for chip in range(chips):
            outs[chip][:, part * half : (part + 1) * half] = total[
                chip * row_count : (chip + 1) * row_count
            ].astype(outs[chip].dtype)


def exchange(values, axis, unit):
    moved = [values[0]]
    for bits in range(1, len(values)):
        moved.append(swap(values[bits], axis, bits * unit))
    return moved


def move_rows(hidden, norm_gain, route, route_weight, resident, sectioned, owner):
    rows, own_piece = hidden[0], sectioned[0]
    row_count, width = rows.shape
    devices = lax.axis_size("exp")
    chips = lax.axis_size("grp") // PAIR
    shards = devices // E_WIN
    half, block = width // 2, 2 * CAP * chips
    piece, units = own_piece.shape[0], resident.shape[1]
    early_units = units * 5 // 8
    row_block = pltpu.VMEM((row_count, width), jnp.bfloat16)
    *packed, code = pl.pallas_call(
        functools.partial(prepare_body, shards),
        out_shape=[row_block] * E_WIN + [pltpu.VMEM((8, CODE), jnp.float32)],
        in_specs=[HBM] * 3,
        out_specs=[VMEM] * (E_WIN + 1),
        scratch_shapes=[
            pltpu.SMEM((1, row_count), jnp.int32),
            pltpu.VMEM((row_count, width), jnp.bfloat16),
            pltpu.VMEM((1, width), jnp.float32),
            pltpu.SemaphoreType.DMA((3,)),
        ],
        compiler_params=limit(4),
        name="prepare",
    )(*in_hbm(route.reshape(1, row_count), rows, norm_gain.reshape(1, width)))
    arrived = exchange([packed[bits // shards] for bits in range(devices)], "exp", 1)
    other_piece = swap(own_piece, "grp", 1)
    early, flags = pl.pallas_call(
        ahead_body,
        out_shape=[
            pltpu.VMEM((2, early_units, width), jnp.bfloat16),
            pltpu.VMEM((8, CODE), jnp.float32),
        ],
        in_specs=[HBM, HBM, ANY],
        out_specs=[VMEM] * 2,
        scratch_shapes=[
            pltpu.SMEM((1, owner.shape[0]), jnp.int32),
            pltpu.SemaphoreType.DMA((2,)),
        ],
        compiler_params=limit(2),
        name="ahead",
    )(*in_hbm(owner.reshape(1, -1), resident), *held(code))
    act = pl.pallas_call(
        functools.partial(activate_body, devices),
        out_shape=pltpu.VMEM((devices * row_count, units), jnp.bfloat16),
        in_specs=[HBM] + [VMEM] * (2 + devices),
        out_specs=VMEM,
        scratch_shapes=[
            pltpu.VMEM((2, units - early_units, width), jnp.bfloat16),
            pltpu.VMEM((devices * row_count, width), jnp.float32),
            pltpu.SemaphoreType.DMA((1,)),
        ],
        compiler_params=limit(16),
        name="activate",
    )(*in_hbm(resident), *held(early, code, *arrived))
    acts = exchange([act] * chips, "grp", PAIR)
    down = pl.pallas_call(
        hold_body,
        out_shape=pltpu.VMEM((PAIR * piece, width), jnp.bfloat16),
        in_specs=[HBM, ANY, ANY],
        out_specs=VMEM,
        scratch_shapes=[pltpu.SemaphoreType.DMA((PAIR,))],
        compiler_params=limit(2),
        name="hold",
    )(*in_hbm(own_piece), *held(other_piece, act))
    half_block = pltpu.VMEM((block, half), jnp.bfloat16)
    partials = pl.pallas_call(
        functools.partial(down_body, devices, chips),
        out_shape=[half_block] * devices,
        in_specs=[VMEM] * (2 + chips),
        out_specs=[VMEM] * devices,
        compiler_params=limit(12),
        name="down",
    )(*held(down, flags, *acts))
    returned = exchange(partials, "exp", 1)
    sums = pl.pallas_call(
        functools.partial(combine_body, devices, chips, shards),
        out_shape=[row_block] * chips,
        in_specs=[VMEM] * (chips + devices),
        out_specs=[VMEM] * chips,
        scratch_shapes=[pltpu.VMEM((chips * row_count, CODE), jnp.float32)],
        compiler_params=limit(8),
        name="combine",
    )(*held(*acts, *returned))
    combined = 0.0
    for share in exchange(sums, "grp", PAIR):
        combined = combined + share.astype(jnp.float32)
    result = (combined * route_weight[0][:, None]).astype(jnp.bfloat16)
    return result.reshape(1, row_count, width)


def per_device(hidden, norm_gain, route, route_weight, resident, sectioned, owner):
    weight_rows = BUCKETS * sectioned.shape[1]
    partial_rows = lax.axis_size("exp") * lax.axis_size("grp") // PAIR * hidden.shape[1]
    plan = move_rows if partial_rows < weight_rows else move_weights
    return plan(hidden, norm_gain, route, route_weight, resident, sectioned, owner)


def solution(mesh):
    in_specs = (
        P("grp", "exp", None),
        P(),
        P("grp", "exp", None),
        P("grp", "exp"),
        P(None, "exp", None),
        P("grp", "exp", None),
        P(),
    )
    out_specs = P("grp", "exp", None)
    return jax.shard_map(
        per_device, mesh=mesh, in_specs=in_specs, out_specs=out_specs, check_vma=False
    )
```

time: 48.2 us -> 46.2 us (0.959)
  waiting for transfers between devices: 20.6 us -> 13.3 us
  Pallas kernels: 9.28 us -> 14.8 us
    ppermute x13, waiting for transfers between devices: 20.6 us -> 13.3 us  [swap(): return lax.ppermute(value, axis, [(i, i ^ bits) for i in range(size)])]
    pallas_call x4 -> x5, Pallas kernels: 8.88 us -> 14.3 us  [the longest x1 6.64 us: move_rows(): pl.pallas_call(functools.partial(activate_body, devices), out_shape=pltpu...]
  transfers between devices with their start and end apart: 13 -> 13, of which waited for: 10 -> 7; matrix products, arithmetic and copies ran while one was open for 0% -> 0% of each run, Pallas kernels for 12% -> 28%
where the time goes in v5:
time: 46.2 us; the launch traced here: 45.9 us
  starting transfers between devices  17 us (37%)
  Pallas kernels  14.8 us (32%)
  waiting for transfers between devices  13.3 us (29%)
  other arithmetic  0.71 us (2%)
    ppermute x13, starting transfers between devices, swap(): return lax.ppermute(value, axis, [(i, i ^ bits) for i in range(size)])  17 us
    ppermute x13, waiting for transfers between devices, swap(): return lax.ppermute(value, axis, [(i, i ^ bits) for i in range(size)])  13.3 us
    pallas_call x1, Pallas kernels, move_rows(): pl.pallas_call(functools.partial(activate_body, devices), out_shape=pltpu...  6.64 us
    pallas_call x1, Pallas kernels, move_rows(): pl.pallas_call(ahead_body, out_shape=[pltpu.VMEM((2, early_units, width),...  3.62 us
    pallas_call x1, Pallas kernels, move_rows(): pl.pallas_call(hold_body, out_shape=pltpu.VMEM((PAIR * piece, width), jnp...  1.52 us
    pallas_call x1, Pallas kernels, move_rows(): pl.pallas_call(functools.partial(down_body, devices, chips), out_shape=[h...  1.3 us
    pallas_call x1, Pallas kernels, move_rows(): pl.pallas_call(functools.partial(prepare_body, shards), out_shape=[row_bl...  1.2 us
  transfers between devices with their start and end apart: 13, of which 7 were waited for; matrix products, arithmetic and copies ran while one was open for 0% of the time, Pallas kernels for 28%

profile of v5, /device:TPU:0, one launch (start us, length us, event | category | flops | bytes accessed | tf_op | source)
XLA Modules:
  0.0 45.9 jit_solution(14544115148157022350)
XLA Ops:
  0.0 0.5 %collective-permute-start.6 = (bf16[128,7168]{1,0:T(8,128)(2,1)}, bf16[128,7168]{1,0:T(8,128)(2,1)S(1)}, u32[]{:S(2)}, u32[]{:S(2)}) collective-permute-start(bf16[128,7168]{1,0:T(8,128)(2,1)} %bitcast.8), channel_id=1, source_target_pairs={{0,4},{4,0},{8,12},{12,8},{16,20},{20,16},{24,28},{28,24},{1,5},{5... | collective-permute-start | bytes 5505032 | tf_op jit(solution)/shard_map/ppermute | solution.py:81
  0.5 1.2 %prepare.1 = (bf16[4,7168]{1,0:T(4,128)(2,1)S(1)}, bf16[4,7168]{1,0:T(4,128)(2,1)S(1)}, f32[8,128]{1,0:T(8,128)S(1)}) custom-call(s32[1,4]{1,0:T(1,128)} %bitcast.13, bf16[4,7168]{1,0:T(4,128)(2,1)} %bitcast.10, f32[1,7168]{1,0:T(1,128)} %bitcast.11), custom_call_target="tpu_custom_call" | custom-call | tf_op jit(solution)/shard_map/prepare/pallas_call | solution.py:301
  1.7 2.5 %collective-permute-start = (bf16[4,7168]{1,0:T(4,128)(2,1)S(1)}, bf16[4,7168]{1,0:T(4,128)(2,1)S(1)}, u32[]{:S(2)}, u32[]{:S(2)}) collective-permute-start(bf16[4,7168]{1,0:T(4,128)(2,1)S(1)} %get-tuple-element.20.refs_0_), channel_id=1, source_target_pairs={{0,1},{1,0},{2,3},{3,2},{4,5},{5,4},{6,7},{7,6},{8,9},{9,8},{10,11... | collective-permute-start | bytes 172040 | tf_op jit(solution)/shard_map/ppermute | solution.py:81
  4.2 1.5 %collective-permute-start.1 = (bf16[4,7168]{1,0:T(4,128)(2,1)S(1)}, bf16[4,7168]{1,0:T(4,128)(2,1)S(1)}, u32[]{:S(2)}, u32[]{:S(2)}) collective-permute-start(bf16[4,7168]{1,0:T(4,128)(2,1)S(1)} %get-tuple-element.21), channel_id=1, source_target_pairs={{0,2},{1,3},{2,0},{3,1},{4,6},{5,7},{6,4},{7,5},{8,10},{9,11},{10,... | collective-permute-start | bytes 172040 | tf_op jit(solution)/shard_map/ppermute | solution.py:81
  5.8 0.0 collective-permute-start.2
  5.8 3.6 %ahead.1 = (bf16[2,320,7168]{2,1,0:T(8,128)(2,1)S(1)}, f32[8,128]{1,0:T(8,128)S(1)}) custom-call(s32[1,8]{1,0:T(1,128)} %bitcast.12, bf16[2,512,7168]{2,1,0:T(8,128)(2,1)} %resident.3, f32[8,128]{1,0:T(8,128)S(1)} %get-tuple-element.18.after.code_ref), custom_call_target="tpu_custom_call" | custom-call | tf_op jit(solution)/shard_map/ahead/pallas_call | solution.py:317
  9.4 0.0 collective-permute-done.refs_1_
  9.4 0.0 collective-permute-done.1.refs_2_
  9.4 1.4 %collective-permute-done.2.refs_3_ = bf16[4,7168]{1,0:T(4,128)(2,1)S(1)} collective-permute-done((bf16[4,7168]{1,0:T(4,128)(2,1)S(1)}, bf16[4,7168]{1,0:T(4,128)(2,1)S(1)}, u32[]{:S(2)}, u32[]{:S(2)}) %collective-permute-start.2) | collective-permute-done | bytes 57376 | tf_op jit(solution)/shard_map/ppermute | solution.py:81
  10.8 6.6 %activate.1.after.refs_0_ = bf16[16,512]{1,0:T(8,128)(2,1)S(1)} custom-call(bf16[2,512,7168]{2,1,0:T(8,128)(2,1)} %resident.3, bf16[2,320,7168]{2,1,0:T(8,128)(2,1)S(1)} %get-tuple-element.19.early, f32[8,128]{1,0:T(8,128)S(1)} %get-tuple-element.18.after.code_ref, bf16[4,7168]{1,0:T(4,128)(2,1)S(1)} %get-tuple-element.20.refs_0_, ...), custom_call_target="tpu_custom_call" | custom-call | tf_op jit(solution)/shard_map/activate/pallas_call | solution.py:332
  17.5 1.6 %collective-permute-start.3 = (bf16[16,512]{1,0:T(8,128)(2,1)S(1)}, bf16[16,512]{1,0:T(8,128)(2,1)S(1)}, u32[]{:S(2)}, u32[]{:S(2)}) collective-permute-start(bf16[16,512]{1,0:T(8,128)(2,1)S(1)} %activate.1.after.refs_0_), channel_id=1, source_target_pairs={{0,8},{4,12},{8,0},{12,4},{16,24},{20,28},{24,16},{28,20},{1,9},{5... | collective-permute-start | bytes 49160 | tf_op jit(solution)/shard_map/ppermute | solution.py:81
  19.1 2.6 %collective-permute-start.4 = (bf16[16,512]{1,0:T(8,128)(2,1)S(1)}, bf16[16,512]{1,0:T(8,128)(2,1)S(1)}, u32[]{:S(2)}, u32[]{:S(2)}) collective-permute-start(bf16[16,512]{1,0:T(8,128)(2,1)S(1)} %activate.1.after.refs_0_), channel_id=1, source_target_pairs={{0,16},{4,20},{8,24},{12,28},{16,0},{20,4},{24,8},{28,12},{1,17},{... | collective-permute-start | bytes 49160 | tf_op jit(solution)/shard_map/ppermute | solution.py:81
  21.7 0.2 collective-permute-start.5
  21.9 0.0 collective-permute-done.6.other
  22.0 1.5 %hold.1.down = bf16[256,7168]{1,0:T(8,128)(2,1)S(1)} custom-call(bf16[128,7168]{1,0:T(8,128)(2,1)} %bitcast.9, bf16[128,7168]{1,0:T(8,128)(2,1)S(1)} %collective-permute-done.6.other, bf16[16,512]{1,0:T(8,128)(2,1)S(1)} %activate.1.after.refs_0_), custom_call_target="tpu_custom_call" | custom-call | tf_op jit(solution)/shard_map/hold/pallas_call | solution.py:346
  23.5 0.0 copy-start
  23.5 0.0 collective-permute-done.3.refs_1_
  23.5 0.3 collective-permute-done.4.refs_2_
  23.8 3.4 %collective-permute-done.5.refs_3_ = bf16[16,512]{1,0:T(8,128)(2,1)S(1)} collective-permute-done((bf16[16,512]{1,0:T(8,128)(2,1)S(1)}, bf16[16,512]{1,0:T(8,128)(2,1)S(1)}, u32[]{:S(2)}, u32[]{:S(2)}) %collective-permute-start.5) | collective-permute-done | bytes 16416 | tf_op jit(solution)/shard_map/ppermute | solution.py:81
  27.3 1.3 %down.1 = (bf16[24,3584]{1,0:T(8,128)(2,1)S(1)}, bf16[24,3584]{1,0:T(8,128)(2,1)S(1)}, bf16[24,3584]{1,0:T(8,128)(2,1)S(1)}, bf16[24,3584]{1,0:T(8,128)(2,1)S(1)}) custom-call(bf16[256,7168]{1,0:T(8,128)(2,1)S(1)} %hold.1.down, f32[8,128]{1,0:T(8,128)S(1)} %get-tuple-element.22.flags, bf16[16,512]{1,0:T(8,128)(2,1)S(1)} %activate.1.after.refs_0_, ...), custom_call_target="tpu_custom_call" | custom-call | tf_op jit(solution)/shard_map/down/pallas_call | solution.py:356
  28.6 0.6 %collective-permute-start.7 = (bf16[24,3584]{1,0:T(8,128)(2,1)S(1)}, bf16[24,3584]{1,0:T(8,128)(2,1)S(1)}, u32[]{:S(2)}, u32[]{:S(2)}) collective-permute-start(bf16[24,3584]{1,0:T(8,128)(2,1)S(1)} %get-tuple-element.24), channel_id=1, source_target_pairs={{0,1},{1,0},{2,3},{3,2},{4,5},{5,4},{6,7},{7,6},{8,9},{9,8},{10,11... | collective-permute-start | bytes 516104 | tf_op jit(solution)/shard_map/ppermute | solution.py:81
  29.2 1.5 %collective-permute-start.8 = (bf16[24,3584]{1,0:T(8,128)(2,1)S(1)}, bf16[24,3584]{1,0:T(8,128)(2,1)S(1)}, u32[]{:S(2)}, u32[]{:S(2)}) collective-permute-start(bf16[24,3584]{1,0:T(8,128)(2,1)S(1)} %get-tuple-element.25), channel_id=1, source_target_pairs={{0,2},{1,3},{2,0},{3,1},{4,6},{5,7},{6,4},{7,5},{8,10},{9,11},{10,... | collective-permute-start | bytes 516104 | tf_op jit(solution)/shard_map/ppermute | solution.py:81
  30.7 1.4 %collective-permute-start.9 = (bf16[24,3584]{1,0:T(8,128)(2,1)S(1)}, bf16[24,3584]{1,0:T(8,128)(2,1)S(1)}, u32[]{:S(2)}, u32[]{:S(2)}) collective-permute-start(bf16[24,3584]{1,0:T(8,128)(2,1)S(1)} %get-tuple-element.26), channel_id=1, source_target_pairs={{0,3},{1,2},{2,1},{3,0},{4,7},{5,6},{6,5},{7,4},{8,11},{9,10},{10,... | collective-permute-start | bytes 516104 | tf_op jit(solution)/shard_map/ppermute | solution.py:81
  32.1 2.4 %collective-permute-done.7.refs_5_ = bf16[24,3584]{1,0:T(8,128)(2,1)S(1)} collective-permute-done((bf16[24,3584]{1,0:T(8,128)(2,1)S(1)}, bf16[24,3584]{1,0:T(8,128)(2,1)S(1)}, u32[]{:S(2)}, u32[]{:S(2)}) %collective-permute-start.7) | collective-permute-done | bytes 172064 | tf_op jit(solution)/shard_map/ppermute | solution.py:81
  34.5 3.0 %collective-permute-done.8.refs_6_ = bf16[24,3584]{1,0:T(8,128)(2,1)S(1)} collective-permute-done((bf16[24,3584]{1,0:T(8,128)(2,1)S(1)}, bf16[24,3584]{1,0:T(8,128)(2,1)S(1)}, u32[]{:S(2)}, u32[]{:S(2)}) %collective-permute-start.8) | collective-permute-done | bytes 172064 | tf_op jit(solution)/shard_map/ppermute | solution.py:81
  37.5 0.0 collective-permute-done.9.refs_7_
  37.5 0.5 %combine.1 = (bf16[4,7168]{1,0:T(4,128)(2,1)S(1)}, bf16[4,7168]{1,0:T(4,128)(2,1)S(1)}, bf16[4,7168]{1,0:T(4,128)(2,1)S(1)}, bf16[4,7168]{1,0:T(4,128)(2,1)S(1)}) custom-call(bf16[16,512]{1,0:T(8,128)(2,1)S(1)} %activate.1.after.refs_0_, bf16[16,512]{1,0:T(8,128)(2,1)S(1)} %collective-permute-done.3.refs_1_, ...), custom_call_target="tpu_custom_call" | custom-call | tf_op jit(solution)/shard_map/combine/pallas_call | solution.py:365
  38.0 0.1 collective-permute-start.10
  38.1 1.2 %collective-permute-start.11 = (bf16[4,7168]{1,0:T(4,128)(2,1)S(1)}, bf16[4,7168]{1,0:T(4,128)(2,1)S(1)}, u32[]{:S(2)}, u32[]{:S(2)}) collective-permute-start(bf16[4,7168]{1,0:T(4,128)(2,1)S(1)} %get-tuple-element.29), channel_id=1, source_target_pairs={{0,16},{4,20},{8,24},{12,28},{16,0},{20,4},{24,8},{28,12},{1,17},{... | collective-permute-start | bytes 172040 | tf_op jit(solution)/shard_map/ppermute | solution.py:81
  39.2 3.2 %collective-permute-start.12 = (bf16[4,7168]{1,0:T(4,128)(2,1)S(1)}, bf16[4,7168]{1,0:T(4,128)(2,1)S(1)}, u32[]{:S(2)}, u32[]{:S(2)}) collective-permute-start(bf16[4,7168]{1,0:T(4,128)(2,1)S(1)} %get-tuple-element.30), channel_id=1, source_target_pairs={{0,24},{4,28},{8,16},{12,20},{16,8},{20,12},{24,0},{28,4},{1,25},{... | collective-permute-start | bytes 172040 | tf_op jit(solution)/shard_map/ppermute | solution.py:81
  42.4 0.0 collective-permute-done.10
  42.4 0.8 %collective-permute-done.11 = bf16[4,7168]{1,0:T(4,128)(2,1)S(1)} collective-permute-done((bf16[4,7168]{1,0:T(4,128)(2,1)S(1)}, bf16[4,7168]{1,0:T(4,128)(2,1)S(1)}, u32[]{:S(2)}, u32[]{:S(2)}) %collective-permute-start.11) | collective-permute-done | bytes 57376 | tf_op jit(solution)/shard_map/ppermute | solution.py:81
  43.2 2.0 %collective-permute-done.12 = bf16[4,7168]{1,0:T(4,128)(2,1)S(1)} collective-permute-done((bf16[4,7168]{1,0:T(4,128)(2,1)S(1)}, bf16[4,7168]{1,0:T(4,128)(2,1)S(1)}, u32[]{:S(2)}, u32[]{:S(2)}) %collective-permute-start.12) | collective-permute-done | bytes 57376 | tf_op jit(solution)/shard_map/ppermute | solution.py:81
  45.2 0.0 copy-done
  45.2 0.7 %fusion = bf16[1,4,7168]{2,1,0:T(4,128)(2,1)} fusion(bf16[4,7168]{1,0:T(4,128)(2,1)S(1)} %collective-permute-done.12, bf16[4,7168]{1,0:T(4,128)(2,1)S(1)} %collective-permute-done.11, bf16[4,7168]{1,0:T(4,128)(2,1)S(1)} %collective-permute-done.10, bf16[4,7168]{1,0:T(4,128)(2,1)S(1)} %get-tuple-element.27, f32[4]{0:T(128)S(1)} %bitcast.14), kind=kLoop, calls=%fused_computation.1 | loop fusion | flops 258048 | bytes 286736 | tf_op jit(solution)/shard_map/reshape | solution.py:378
Async XLA Ops:
  0.0 21.9 %collective-permute-start.6 = (bf16[128,7168]{1,0:T(8,128)(2,1)}, bf16[128,7168]{1,0:T(8,128)(2,1)S(1)}, u32[]{:S(2)}, u32[]{:S(2)}) collective-permute-start(bf16[128,7168]{1,0:T(8,128)(2,1)} %bitcast.8), channel_id=1, source_target_pairs={{0,4},{4,0},{8,12},{12,8},{16,20},{20,16},{24,28},{28,24},{1,5},{5... | collective-permute-start | bytes 5505032 | tf_op jit(solution)/shard_map/ppermute | solution.py:81
  1.7 7.7 %collective-permute-start = (bf16[4,7168]{1,0:T(4,128)(2,1)S(1)}, bf16[4,7168]{1,0:T(4,128)(2,1)S(1)}, u32[]{:S(2)}, u32[]{:S(2)}) collective-permute-start(bf16[4,7168]{1,0:T(4,128)(2,1)S(1)} %get-tuple-element.20.refs_0_), channel_id=1, source_target_pairs={{0,1},{1,0},{2,3},{3,2},{4,5},{5,4},{6,7},{7,6},{8,9},{9,8},{10,11... | collective-permute-start | bytes 172040 | tf_op jit(solution)/shard_map/ppermute | solution.py:81
  4.2 5.2 %collective-permute-start.1 = (bf16[4,7168]{1,0:T(4,128)(2,1)S(1)}, bf16[4,7168]{1,0:T(4,128)(2,1)S(1)}, u32[]{:S(2)}, u32[]{:S(2)}) collective-permute-start(bf16[4,7168]{1,0:T(4,128)(2,1)S(1)} %get-tuple-element.21), channel_id=1, source_target_pairs={{0,2},{1,3},{2,0},{3,1},{4,6},{5,7},{6,4},{7,5},{8,10},{9,11},{10,... | collective-permute-start | bytes 172040 | tf_op jit(solution)/shard_map/ppermute | solution.py:81
  5.8 5.1 %collective-permute-start.2 = (bf16[4,7168]{1,0:T(4,128)(2,1)S(1)}, bf16[4,7168]{1,0:T(4,128)(2,1)S(1)}, u32[]{:S(2)}, u32[]{:S(2)}) collective-permute-start(bf16[4,7168]{1,0:T(4,128)(2,1)S(1)} %get-tuple-element.21), channel_id=1, source_target_pairs={{0,3},{1,2},{2,1},{3,0},{4,7},{5,6},{6,5},{7,4},{8,11},{9,10},{10,... | collective-permute-start | bytes 172040 | tf_op jit(solution)/shard_map/ppermute | solution.py:81
  17.5 6.0 %collective-permute-start.3 = (bf16[16,512]{1,0:T(8,128)(2,1)S(1)}, bf16[16,512]{1,0:T(8,128)(2,1)S(1)}, u32[]{:S(2)}, u32[]{:S(2)}) collective-permute-start(bf16[16,512]{1,0:T(8,128)(2,1)S(1)} %activate.1.after.refs_0_), channel_id=1, source_target_pairs={{0,8},{4,12},{8,0},{12,4},{16,24},{20,28},{24,16},{28,20},{1,9},{5... | collective-permute-start | bytes 49160 | tf_op jit(solution)/shard_map/ppermute | solution.py:81
  19.1 4.7 %collective-permute-start.4 = (bf16[16,512]{1,0:T(8,128)(2,1)S(1)}, bf16[16,512]{1,0:T(8,128)(2,1)S(1)}, u32[]{:S(2)}, u32[]{:S(2)}) collective-permute-start(bf16[16,512]{1,0:T(8,128)(2,1)S(1)} %activate.1.after.refs_0_), channel_id=1, source_target_pairs={{0,16},{4,20},{8,24},{12,28},{16,0},{20,4},{24,8},{28,12},{1,17},{... | collective-permute-start | bytes 49160 | tf_op jit(solution)/shard_map/ppermute | solution.py:81
  21.7 5.5 %collective-permute-start.5 = (bf16[16,512]{1,0:T(8,128)(2,1)S(1)}, bf16[16,512]{1,0:T(8,128)(2,1)S(1)}, u32[]{:S(2)}, u32[]{:S(2)}) collective-permute-start(bf16[16,512]{1,0:T(8,128)(2,1)S(1)} %activate.1.after.refs_0_), channel_id=1, source_target_pairs={{0,24},{4,28},{8,16},{12,20},{16,8},{20,12},{24,0},{28,4},{1,25},{... | collective-permute-start | bytes 49160 | tf_op jit(solution)/shard_map/ppermute | solution.py:81
  23.5 21.7 %copy-start = (f32[1,4]{1,0:T(1,128)S(1)}, f32[1,4]{1,0:T(1,128)}, u32[]{:S(2)}) copy-start(f32[1,4]{1,0:T(1,128)} %param.10) | copy-start | bytes 52
  28.6 5.9 %collective-permute-start.7 = (bf16[24,3584]{1,0:T(8,128)(2,1)S(1)}, bf16[24,3584]{1,0:T(8,128)(2,1)S(1)}, u32[]{:S(2)}, u32[]{:S(2)}) collective-permute-start(bf16[24,3584]{1,0:T(8,128)(2,1)S(1)} %get-tuple-element.24), channel_id=1, source_target_pairs={{0,1},{1,0},{2,3},{3,2},{4,5},{5,4},{6,7},{7,6},{8,9},{9,8},{10,11... | collective-permute-start | bytes 516104 | tf_op jit(solution)/shard_map/ppermute | solution.py:81
  29.2 8.3 %collective-permute-start.8 = (bf16[24,3584]{1,0:T(8,128)(2,1)S(1)}, bf16[24,3584]{1,0:T(8,128)(2,1)S(1)}, u32[]{:S(2)}, u32[]{:S(2)}) collective-permute-start(bf16[24,3584]{1,0:T(8,128)(2,1)S(1)} %get-tuple-element.25), channel_id=1, source_target_pairs={{0,2},{1,3},{2,0},{3,1},{4,6},{5,7},{6,4},{7,5},{8,10},{9,11},{10,... | collective-permute-start | bytes 516104 | tf_op jit(solution)/shard_map/ppermute | solution.py:81
  30.7 6.8 %collective-permute-start.9 = (bf16[24,3584]{1,0:T(8,128)(2,1)S(1)}, bf16[24,3584]{1,0:T(8,128)(2,1)S(1)}, u32[]{:S(2)}, u32[]{:S(2)}) collective-permute-start(bf16[24,3584]{1,0:T(8,128)(2,1)S(1)} %get-tuple-element.26), channel_id=1, source_target_pairs={{0,3},{1,2},{2,1},{3,0},{4,7},{5,6},{6,5},{7,4},{8,11},{9,10},{10,... | collective-permute-start | bytes 516104 | tf_op jit(solution)/shard_map/ppermute | solution.py:81
  38.0 4.5 %collective-permute-start.10 = (bf16[4,7168]{1,0:T(4,128)(2,1)S(1)}, bf16[4,7168]{1,0:T(4,128)(2,1)S(1)}, u32[]{:S(2)}, u32[]{:S(2)}) collective-permute-start(bf16[4,7168]{1,0:T(4,128)(2,1)S(1)} %get-tuple-element.28), channel_id=1, source_target_pairs={{0,8},{4,12},{8,0},{12,4},{16,24},{20,28},{24,16},{28,20},{1,9},{5... | collective-permute-start | bytes 172040 | tf_op jit(solution)/shard_map/ppermute | solution.py:81
  38.1 5.1 %collective-permute-start.11 = (bf16[4,7168]{1,0:T(4,128)(2,1)S(1)}, bf16[4,7168]{1,0:T(4,128)(2,1)S(1)}, u32[]{:S(2)}, u32[]{:S(2)}) collective-permute-start(bf16[4,7168]{1,0:T(4,128)(2,1)S(1)} %get-tuple-element.29), channel_id=1, source_target_pairs={{0,16},{4,20},{8,24},{12,28},{16,0},{20,4},{24,8},{28,12},{1,17},{... | collective-permute-start | bytes 172040 | tf_op jit(solution)/shard_map/ppermute | solution.py:81
  39.2 6.0 %collective-permute-start.12 = (bf16[4,7168]{1,0:T(4,128)(2,1)S(1)}, bf16[4,7168]{1,0:T(4,128)(2,1)S(1)}, u32[]{:S(2)}, u32[]{:S(2)}) collective-permute-start(bf16[4,7168]{1,0:T(4,128)(2,1)S(1)} %get-tuple-element.30), channel_id=1, source_target_pairs={{0,24},{4,28},{8,16},{12,20},{16,8},{20,12},{24,0},{28,4},{1,25},{... | collective-permute-start | bytes 172040 | tf_op jit(solution)/shard_map/ppermute | solution.py:81

commit v6 on v5

--- a/solution.py
+++ b/solution.py
@@ -139,10 +139,8 @@
         )
 
 
-def ahead_body(owner, resident, after, early, flags, owner_ref, sems):
-    early_copy = pltpu.make_async_copy(resident.at[:, pl.ds(0, early.shape[1])], early, sems.at[0])
-    early_copy.start()
-    owner_copy = pltpu.make_async_copy(owner, owner_ref, sems.at[1])
+def flag_body(owner, after, flags, owner_ref, sems):
+    owner_copy = pltpu.make_async_copy(owner, owner_ref, sems.at[0])
     owner_copy.start()
     owner_copy.wait()
     group = lax.axis_index("grp")
@@ -153,37 +151,22 @@
             hit = jnp.where(owner_ref[0, bucket] == (group ^ which), 1.0, 0.0)
             values = jnp.where(row == which * BUCKETS + bucket, hit, values)
     flags[...] = values
-    early_copy.wait()
-
-
-def activate_body(devices, resident, early, code_ref, *refs):
-    blocks, out = refs[:devices], refs[devices]
-    late, stacked, sem = refs[devices + 1 :]
-    first = early.shape[1]
-    late_copy = pltpu.make_async_copy(
-        resident.at[:, pl.ds(first, late.shape[1])], late, sem.at[0]
-    )
-    late_copy.start()
+
+
+def activate_body(devices, weights, code_ref, *refs):
+    blocks, out, stacked = refs[:devices], refs[devices], refs[devices + 1]
     row_count = blocks[0].shape[0]
     for index in range(devices):
         stacked[index * row_count : (index + 1) * row_count, :] = blocks[index][...].astype(
             jnp.float32
         )
     rows = stacked[...].astype(jnp.bfloat16)
-
-    def hidden_units(weights):
-        gate = lax.dot_general(weights[0], rows, NT, preferred_element_type=jnp.float32)
-        up = lax.dot_general(weights[1], rows, NT, preferred_element_type=jnp.float32)
-        return (gate * jax.nn.sigmoid(gate) * up).T
-
-    out[:, :first] = hidden_units(early).astype(jnp.bfloat16)
-    late_copy.wait()
-    out[:, first:] = hidden_units(late).astype(jnp.bfloat16)
-    head = out[:, :CODE]
-    spare = lax.broadcasted_iota(jnp.int32, head.shape, 0) == CAP
-    out[:, :CODE] = jnp.where(spare, code_ref[0:1, :], head.astype(jnp.float32)).astype(
-        jnp.bfloat16
-    )
+    gate = lax.dot_general(weights[0], rows, NT, preferred_element_type=jnp.float32)
+    up = lax.dot_general(weights[1], rows, NT, preferred_element_type=jnp.float32)
+    act = (gate * jax.nn.sigmoid(gate) * up).T
+    spare = lax.broadcasted_iota(jnp.int32, (act.shape[0], CODE), 0) == CAP
+    out[:, :CODE] = jnp.where(spare, code_ref[0:1, :], act[:, :CODE]).astype(jnp.bfloat16)
+    out[:, CODE:] = act[:, CODE:].astype(jnp.bfloat16)
 
 
 def hold_body(own, other, after, down, sems):
@@ -296,7 +279,6 @@
     shards = devices // E_WIN
     half, block = width // 2, 2 * CAP * chips
     piece, units = own_piece.shape[0], resident.shape[1]
-    early_units = units * 5 // 8
     row_block = pltpu.VMEM((row_count, width), jnp.bfloat16)
     *packed, code = pl.pallas_call(
         functools.partial(prepare_body, shards),
@@ -314,34 +296,28 @@
     )(*in_hbm(route.reshape(1, row_count), rows, norm_gain.reshape(1, width)))
     arrived = exchange([packed[bits // shards] for bits in range(devices)], "exp", 1)
     other_piece = swap(own_piece, "grp", 1)
-    early, flags = pl.pallas_call(
-        ahead_body,
-        out_shape=[
-            pltpu.VMEM((2, early_units, width), jnp.bfloat16),
-            pltpu.VMEM((8, CODE), jnp.float32),
-        ],
-        in_specs=[HBM, HBM, ANY],
-        out_specs=[VMEM] * 2,
+    weights = swap(resident, "grp", 0)
+    flags = pl.pallas_call(
+        flag_body,
+        out_shape=pltpu.VMEM((8, CODE), jnp.float32),
+        in_specs=[HBM, ANY],
+        out_specs=VMEM,
         scratch_shapes=[
             pltpu.SMEM((1, owner.shape[0]), jnp.int32),
-            pltpu.SemaphoreType.DMA((2,)),
+            pltpu.SemaphoreType.DMA((1,)),
         ],
         compiler_params=limit(2),
-        name="ahead",
-    )(*in_hbm(owner.reshape(1, -1), resident), *held(code))
+        name="flag",
+    )(*in_hbm(owner.reshape(1, -1)), *held(code))
     act = pl.pallas_call(
         functools.partial(activate_body, devices),
         out_shape=pltpu.VMEM((devices * row_count, units), jnp.bfloat16),
-        in_specs=[HBM] + [VMEM] * (2 + devices),
+        in_specs=[VMEM] * (2 + devices),
         out_specs=VMEM,
-        scratch_shapes=[
-            pltpu.VMEM((2, units - early_units, width), jnp.bfloat16),
-            pltpu.VMEM((devices * row_count, width), jnp.float32),
-            pltpu.SemaphoreType.DMA((1,)),
-        ],
-        compiler_params=limit(16),
+        scratch_shapes=[pltpu.VMEM((devices * row_count, width), jnp.float32)],
+        compiler_params=limit(8),
         name="activate",
-    )(*in_hbm(resident), *held(early, code, *arrived))
+    )(*held(weights, code, *arrived))
     acts = exchange([act] * chips, "grp", PAIR)
     down = pl.pallas_call(
         hold_body,

time: 46.2 us -> 48.5 us (1.050)
  Pallas kernels: 14.8 us -> 9.15 us
  starting transfers between devices: 17 us -> 22.2 us
  waiting for transfers between devices: 13.3 us -> 16.2 us
    ppermute x13 -> x14, starting transfers between devices: 17 us -> 22.2 us  [swap(): return lax.ppermute(value, axis, [(i, i ^ bits) for i in range(size)])]
    pallas_call x1, Pallas kernels: 3.62 us -> 0.69 us  [move_rows(): pl.pallas_call(flag_body, out_shape=pltpu.VMEM((8, CODE), jnp.float32), i...]
    ppermute x13 -> x14, waiting for transfers between devices: 13.3 us -> 16.2 us  [swap(): return lax.ppermute(value, axis, [(i, i ^ bits) for i in range(size)])]
    pallas_call x1, Pallas kernels: 6.64 us -> 3.97 us  [move_rows(): pl.pallas_call(functools.partial(activate_body, devices), out_shape=pltpu...]
  transfers between devices with their start and end apart: 13 -> 14, of which waited for: 7 -> 9; matrix products, arithmetic and copies ran while one was open for 0% -> 0% of each run, Pallas kernels for 28% -> 15%
where the time goes in v6:
time: 48.5 us; the launch traced here: 48.3 us
  starting transfers between devices  22.2 us (46%)
  waiting for transfers between devices  16.2 us (33%)
  Pallas kernels  9.15 us (19%)
  other arithmetic  0.71 us (1%)
    ppermute x14, starting transfers between devices, swap(): return lax.ppermute(value, axis, [(i, i ^ bits) for i in range(size)])  22.2 us
    ppermute x14, waiting for transfers between devices, swap(): return lax.ppermute(value, axis, [(i, i ^ bits) for i in range(size)])  16.2 us
    pallas_call x1, Pallas kernels, move_rows(): pl.pallas_call(functools.partial(activate_body, devices), out_shape=pltpu...  3.97 us
    pallas_call x1, Pallas kernels, move_rows(): pl.pallas_call(hold_body, out_shape=pltpu.VMEM((PAIR * piece, width), jnp...  1.52 us
    pallas_call x1, Pallas kernels, move_rows(): pl.pallas_call(functools.partial(down_body, devices, chips), out_shape=[h...  1.3 us
    pallas_call x1, Pallas kernels, move_rows(): pl.pallas_call(functools.partial(prepare_body, shards), out_shape=[row_bl...  1.2 us
  transfers between devices with their start and end apart: 14, of which 9 were waited for; matrix products, arithmetic and copies ran while one was open for 0% of the time, Pallas kernels for 15%

profile of v6, /device:TPU:0, one launch (start us, length us, event | category | flops | bytes accessed | tf_op | source)
XLA Modules:
  0.0 48.3 jit_solution(6131792045163208482)
XLA Ops:
  0.0 5.2 %collective-permute-start = (bf16[2,512,7168]{2,1,0:T(8,128)(2,1)}, bf16[2,512,7168]{2,1,0:T(8,128)(2,1)S(1)}, u32[]{:S(2)}, u32[]{:S(2)}) collective-permute-start(bf16[2,512,7168]{2,1,0:T(8,128)(2,1)} %param.11), channel_id=1, source_target_pairs={{0,0},{4,4},{8,8},{12,12},{16,16},{20,20},{24,24},{28,28},{1,1},{5... | collective-permute-start | bytes 44040200 | tf_op jit(solution)/shard_map/ppermute | solution.py:81
  5.2 0.5 %collective-permute-start.7 = (bf16[128,7168]{1,0:T(8,128)(2,1)}, bf16[128,7168]{1,0:T(8,128)(2,1)S(1)}, u32[]{:S(2)}, u32[]{:S(2)}) collective-permute-start(bf16[128,7168]{1,0:T(8,128)(2,1)} %bitcast.8), channel_id=1, source_target_pairs={{0,4},{4,0},{8,12},{12,8},{16,20},{20,16},{24,28},{28,24},{1,5},{5... | collective-permute-start | bytes 5505032 | tf_op jit(solution)/shard_map/ppermute | solution.py:81
  5.7 1.2 %prepare.1 = (bf16[4,7168]{1,0:T(4,128)(2,1)S(1)}, bf16[4,7168]{1,0:T(4,128)(2,1)S(1)}, f32[8,128]{1,0:T(8,128)S(1)}) custom-call(s32[1,4]{1,0:T(1,128)} %bitcast.12, bf16[4,7168]{1,0:T(4,128)(2,1)} %bitcast.10, f32[1,7168]{1,0:T(1,128)} %bitcast.11), custom_call_target="tpu_custom_call" | custom-call | tf_op jit(solution)/shard_map/prepare/pallas_call | solution.py:283
  6.9 2.5 %collective-permute-start.1 = (bf16[4,7168]{1,0:T(4,128)(2,1)S(1)}, bf16[4,7168]{1,0:T(4,128)(2,1)S(1)}, u32[]{:S(2)}, u32[]{:S(2)}) collective-permute-start(bf16[4,7168]{1,0:T(4,128)(2,1)S(1)} %get-tuple-element.17.refs_0_), channel_id=1, source_target_pairs={{0,1},{1,0},{2,3},{3,2},{4,5},{5,4},{6,7},{7,6},{8,9},{9,8},{10,11... | collective-permute-start | bytes 172040 | tf_op jit(solution)/shard_map/ppermute | solution.py:81
  9.4 1.5 %collective-permute-start.2 = (bf16[4,7168]{1,0:T(4,128)(2,1)S(1)}, bf16[4,7168]{1,0:T(4,128)(2,1)S(1)}, u32[]{:S(2)}, u32[]{:S(2)}) collective-permute-start(bf16[4,7168]{1,0:T(4,128)(2,1)S(1)} %get-tuple-element.18), channel_id=1, source_target_pairs={{0,2},{1,3},{2,0},{3,1},{4,6},{5,7},{6,4},{7,5},{8,10},{9,11},{10,... | collective-permute-start | bytes 172040 | tf_op jit(solution)/shard_map/ppermute | solution.py:81
  10.9 0.0 collective-permute-start.3
  11.0 1.0 %collective-permute-done.1.refs_1_ = bf16[4,7168]{1,0:T(4,128)(2,1)S(1)} collective-permute-done((bf16[4,7168]{1,0:T(4,128)(2,1)S(1)}, bf16[4,7168]{1,0:T(4,128)(2,1)S(1)}, u32[]{:S(2)}, u32[]{:S(2)}) %collective-permute-start.1) | collective-permute-done | bytes 57376 | tf_op jit(solution)/shard_map/ppermute | solution.py:81
  12.0 1.6 %collective-permute-done.2.refs_2_ = bf16[4,7168]{1,0:T(4,128)(2,1)S(1)} collective-permute-done((bf16[4,7168]{1,0:T(4,128)(2,1)S(1)}, bf16[4,7168]{1,0:T(4,128)(2,1)S(1)}, u32[]{:S(2)}, u32[]{:S(2)}) %collective-permute-start.2) | collective-permute-done | bytes 57376 | tf_op jit(solution)/shard_map/ppermute | solution.py:81
  13.6 2.4 %collective-permute-done.3.refs_3_ = bf16[4,7168]{1,0:T(4,128)(2,1)S(1)} collective-permute-done((bf16[4,7168]{1,0:T(4,128)(2,1)S(1)}, bf16[4,7168]{1,0:T(4,128)(2,1)S(1)}, u32[]{:S(2)}, u32[]{:S(2)}) %collective-permute-start.3) | collective-permute-done | bytes 57376 | tf_op jit(solution)/shard_map/ppermute | solution.py:81
  16.0 0.0 collective-permute-done.weights
  16.0 4.0 %activate.1.after.refs_0_ = bf16[16,512]{1,0:T(8,128)(2,1)S(1)} custom-call(bf16[2,512,7168]{2,1,0:T(8,128)(2,1)S(1)} %collective-permute-done.weights, f32[8,128]{1,0:T(8,128)S(1)} %get-tuple-element.16.code_ref.after, bf16[4,7168]{1,0:T(4,128)(2,1)S(1)} %get-tuple-element.17.refs_0_, bf16[4,7168]{1,0:T(4,128)(2,1)S(1)} %collective-permute-done.1.refs_1_, ...), custom_call_target="tpu_custom_call" | custom-call | tf_op jit(solution)/shard_map/activate/pallas_call | solution.py:312
  20.0 1.6 %collective-permute-start.4 = (bf16[16,512]{1,0:T(8,128)(2,1)S(1)}, bf16[16,512]{1,0:T(8,128)(2,1)S(1)}, u32[]{:S(2)}, u32[]{:S(2)}) collective-permute-start(bf16[16,512]{1,0:T(8,128)(2,1)S(1)} %activate.1.after.refs_0_), channel_id=1, source_target_pairs={{0,8},{4,12},{8,0},{12,4},{16,24},{20,28},{24,16},{28,20},{1,9},{5... | collective-permute-start | bytes 49160 | tf_op jit(solution)/shard_map/ppermute | solution.py:81
  21.6 2.6 %collective-permute-start.5 = (bf16[16,512]{1,0:T(8,128)(2,1)S(1)}, bf16[16,512]{1,0:T(8,128)(2,1)S(1)}, u32[]{:S(2)}, u32[]{:S(2)}) collective-permute-start(bf16[16,512]{1,0:T(8,128)(2,1)S(1)} %activate.1.after.refs_0_), channel_id=1, source_target_pairs={{0,16},{4,20},{8,24},{12,28},{16,0},{20,4},{24,8},{28,12},{1,17},{... | collective-permute-start | bytes 49160 | tf_op jit(solution)/shard_map/ppermute | solution.py:81
  24.2 0.2 collective-permute-start.6
  24.4 0.7 %flag.1.flags = f32[8,128]{1,0:T(8,128)S(1)} custom-call(s32[1,8]{1,0:T(1,128)} %bitcast.14, f32[8,128]{1,0:T(8,128)S(1)} %get-tuple-element.16.code_ref.after), custom_call_target="tpu_custom_call" | custom-call | tf_op jit(solution)/shard_map/flag/pallas_call | solution.py:300
  25.1 0.0 collective-permute-done.7.other
  25.1 1.5 %hold.1.down = bf16[256,7168]{1,0:T(8,128)(2,1)S(1)} custom-call(bf16[128,7168]{1,0:T(8,128)(2,1)} %bitcast.9, bf16[128,7168]{1,0:T(8,128)(2,1)S(1)} %collective-permute-done.7.other, bf16[16,512]{1,0:T(8,128)(2,1)S(1)} %activate.1.after.refs_0_), custom_call_target="tpu_custom_call" | custom-call | tf_op jit(solution)/shard_map/hold/pallas_call | solution.py:322
  26.6 0.0 copy-start
  26.7 0.0 collective-permute-done.4.refs_1_
  26.7 0.0 collective-permute-done.5.refs_2_
  26.7 3.0 %collective-permute-done.6.refs_3_ = bf16[16,512]{1,0:T(8,128)(2,1)S(1)} collective-permute-done((bf16[16,512]{1,0:T(8,128)(2,1)S(1)}, bf16[16,512]{1,0:T(8,128)(2,1)S(1)}, u32[]{:S(2)}, u32[]{:S(2)}) %collective-permute-start.6) | collective-permute-done | bytes 16416 | tf_op jit(solution)/shard_map/ppermute | solution.py:81
  29.7 1.3 %down.1 = (bf16[24,3584]{1,0:T(8,128)(2,1)S(1)}, bf16[24,3584]{1,0:T(8,128)(2,1)S(1)}, bf16[24,3584]{1,0:T(8,128)(2,1)S(1)}, bf16[24,3584]{1,0:T(8,128)(2,1)S(1)}) custom-call(bf16[256,7168]{1,0:T(8,128)(2,1)S(1)} %hold.1.down, f32[8,128]{1,0:T(8,128)S(1)} %flag.1.flags, bf16[16,512]{1,0:T(8,128)(2,1)S(1)} %activate.1.after.refs_0_, ...), custom_call_target="tpu_custom_call" | custom-call | tf_op jit(solution)/shard_map/down/pallas_call | solution.py:332
  31.0 0.5 %collective-permute-start.10 = (bf16[24,3584]{1,0:T(8,128)(2,1)S(1)}, bf16[24,3584]{1,0:T(8,128)(2,1)S(1)}, u32[]{:S(2)}, u32[]{:S(2)}) collective-permute-start(bf16[24,3584]{1,0:T(8,128)(2,1)S(1)} %get-tuple-element.22), channel_id=1, source_target_pairs={{0,3},{1,2},{2,1},{3,0},{4,7},{5,6},{6,5},{7,4},{8,11},{9,10},{10,... | collective-permute-start | bytes 516104 | tf_op jit(solution)/shard_map/ppermute | solution.py:81
  31.6 1.5 %collective-permute-start.8 = (bf16[24,3584]{1,0:T(8,128)(2,1)S(1)}, bf16[24,3584]{1,0:T(8,128)(2,1)S(1)}, u32[]{:S(2)}, u32[]{:S(2)}) collective-permute-start(bf16[24,3584]{1,0:T(8,128)(2,1)S(1)} %get-tuple-element.20), channel_id=1, source_target_pairs={{0,1},{1,0},{2,3},{3,2},{4,5},{5,4},{6,7},{7,6},{8,9},{9,8},{10,11... | collective-permute-start | bytes 516104 | tf_op jit(solution)/shard_map/ppermute | solution.py:81
  33.1 1.5 %collective-permute-start.9 = (bf16[24,3584]{1,0:T(8,128)(2,1)S(1)}, bf16[24,3584]{1,0:T(8,128)(2,1)S(1)}, u32[]{:S(2)}, u32[]{:S(2)}) collective-permute-start(bf16[24,3584]{1,0:T(8,128)(2,1)S(1)} %get-tuple-element.21), channel_id=1, source_target_pairs={{0,2},{1,3},{2,0},{3,1},{4,6},{5,7},{6,4},{7,5},{8,10},{9,11},{10,... | collective-permute-start | bytes 516104 | tf_op jit(solution)/shard_map/ppermute | solution.py:81
  34.6 2.9 %collective-permute-done.10.refs_7_ = bf16[24,3584]{1,0:T(8,128)(2,1)S(1)} collective-permute-done((bf16[24,3584]{1,0:T(8,128)(2,1)S(1)}, bf16[24,3584]{1,0:T(8,128)(2,1)S(1)}, u32[]{:S(2)}, u32[]{:S(2)}) %collective-permute-start.10) | collective-permute-done | bytes 172064 | tf_op jit(solution)/shard_map/ppermute | solution.py:81
  37.5 0.8 %collective-permute-done.8.refs_5_ = bf16[24,3584]{1,0:T(8,128)(2,1)S(1)} collective-permute-done((bf16[24,3584]{1,0:T(8,128)(2,1)S(1)}, bf16[24,3584]{1,0:T(8,128)(2,1)S(1)}, u32[]{:S(2)}, u32[]{:S(2)}) %collective-permute-start.8) | collective-permute-done | bytes 172064 | tf_op jit(solution)/shard_map/ppermute | solution.py:81
  38.3 1.0 %collective-permute-done.9.refs_6_ = bf16[24,3584]{1,0:T(8,128)(2,1)S(1)} collective-permute-done((bf16[24,3584]{1,0:T(8,128)(2,1)S(1)}, bf16[24,3584]{1,0:T(8,128)(2,1)S(1)}, u32[]{:S(2)}, u32[]{:S(2)}) %collective-permute-start.9) | collective-permute-done | bytes 172064 | tf_op jit(solution)/shard_map/ppermute | solution.py:81
  39.2 0.5 combine.1
  39.7 0.1 collective-permute-start.11
  39.8 1.8 %collective-permute-start.12 = (bf16[4,7168]{1,0:T(4,128)(2,1)S(1)}, bf16[4,7168]{1,0:T(4,128)(2,1)S(1)}, u32[]{:S(2)}, u32[]{:S(2)}) collective-permute-start(bf16[4,7168]{1,0:T(4,128)(2,1)S(1)} %get-tuple-element.25), channel_id=1, source_target_pairs={{0,16},{4,20},{8,24},{12,28},{16,0},{20,4},{24,8},{28,12},{1,17},{... | collective-permute-start | bytes 172040 | tf_op jit(solution)/shard_map/ppermute | solution.py:81
  41.6 2.6 %collective-permute-start.13 = (bf16[4,7168]{1,0:T(4,128)(2,1)S(1)}, bf16[4,7168]{1,0:T(4,128)(2,1)S(1)}, u32[]{:S(2)}, u32[]{:S(2)}) collective-permute-start(bf16[4,7168]{1,0:T(4,128)(2,1)S(1)} %get-tuple-element.26), channel_id=1, source_target_pairs={{0,24},{4,28},{8,16},{12,20},{16,8},{20,12},{24,0},{28,4},{1,25},{... | collective-permute-start | bytes 172040 | tf_op jit(solution)/shard_map/ppermute | solution.py:81
  44.2 1.0 %collective-permute-done.11 = bf16[4,7168]{1,0:T(4,128)(2,1)S(1)} collective-permute-done((bf16[4,7168]{1,0:T(4,128)(2,1)S(1)}, bf16[4,7168]{1,0:T(4,128)(2,1)S(1)}, u32[]{:S(2)}, u32[]{:S(2)}) %collective-permute-start.11) | collective-permute-done | bytes 57376 | tf_op jit(solution)/shard_map/ppermute | solution.py:81
  45.2 0.0 collective-permute-done.12
  45.2 2.4 %collective-permute-done.13 = bf16[4,7168]{1,0:T(4,128)(2,1)S(1)} collective-permute-done((bf16[4,7168]{1,0:T(4,128)(2,1)S(1)}, bf16[4,7168]{1,0:T(4,128)(2,1)S(1)}, u32[]{:S(2)}, u32[]{:S(2)}) %collective-permute-start.13) | collective-permute-done | bytes 57376 | tf_op jit(solution)/shard_map/ppermute | solution.py:81
  47.6 0.0 copy-done
  47.6 0.7 %fusion = bf16[1,4,7168]{2,1,0:T(4,128)(2,1)} fusion(bf16[4,7168]{1,0:T(4,128)(2,1)S(1)} %collective-permute-done.13, bf16[4,7168]{1,0:T(4,128)(2,1)S(1)} %collective-permute-done.12, bf16[4,7168]{1,0:T(4,128)(2,1)S(1)} %collective-permute-done.11, bf16[4,7168]{1,0:T(4,128)(2,1)S(1)} %get-tuple-element.23, f32[4]{0:T(128)S(1)} %bitcast.13), kind=kLoop, calls=%fused_computation.1 | loop fusion | flops 258048 | bytes 286736 | tf_op jit(solution)/shard_map/reshape | solution.py:354
Async XLA Ops:
  0.0 16.0 %collective-permute-start = (bf16[2,512,7168]{2,1,0:T(8,128)(2,1)}, bf16[2,512,7168]{2,1,0:T(8,128)(2,1)S(1)}, u32[]{:S(2)}, u32[]{:S(2)}) collective-permute-start(bf16[2,512,7168]{2,1,0:T(8,128)(2,1)} %param.11), channel_id=1, source_target_pairs={{0,0},{4,4},{8,8},{12,12},{16,16},{20,20},{24,24},{28,28},{1,1},{5... | collective-permute-start | bytes 44040200 | tf_op jit(solution)/shard_map/ppermute | solution.py:81
  5.2 19.9 %collective-permute-start.7 = (bf16[128,7168]{1,0:T(8,128)(2,1)}, bf16[128,7168]{1,0:T(8,128)(2,1)S(1)}, u32[]{:S(2)}, u32[]{:S(2)}) collective-permute-start(bf16[128,7168]{1,0:T(8,128)(2,1)} %bitcast.8), channel_id=1, source_target_pairs={{0,4},{4,0},{8,12},{12,8},{16,20},{20,16},{24,28},{28,24},{1,5},{5... | collective-permute-start | bytes 5505032 | tf_op jit(solution)/shard_map/ppermute | solution.py:81
  6.9 5.1 %collective-permute-start.1 = (bf16[4,7168]{1,0:T(4,128)(2,1)S(1)}, bf16[4,7168]{1,0:T(4,128)(2,1)S(1)}, u32[]{:S(2)}, u32[]{:S(2)}) collective-permute-start(bf16[4,7168]{1,0:T(4,128)(2,1)S(1)} %get-tuple-element.17.refs_0_), channel_id=1, source_target_pairs={{0,1},{1,0},{2,3},{3,2},{4,5},{5,4},{6,7},{7,6},{8,9},{9,8},{10,11... | collective-permute-start | bytes 172040 | tf_op jit(solution)/shard_map/ppermute | solution.py:81
  9.4 4.2 %collective-permute-start.2 = (bf16[4,7168]{1,0:T(4,128)(2,1)S(1)}, bf16[4,7168]{1,0:T(4,128)(2,1)S(1)}, u32[]{:S(2)}, u32[]{:S(2)}) collective-permute-start(bf16[4,7168]{1,0:T(4,128)(2,1)S(1)} %get-tuple-element.18), channel_id=1, source_target_pairs={{0,2},{1,3},{2,0},{3,1},{4,6},{5,7},{6,4},{7,5},{8,10},{9,11},{10,... | collective-permute-start | bytes 172040 | tf_op jit(solution)/shard_map/ppermute | solution.py:81
  10.9 5.1 %collective-permute-start.3 = (bf16[4,7168]{1,0:T(4,128)(2,1)S(1)}, bf16[4,7168]{1,0:T(4,128)(2,1)S(1)}, u32[]{:S(2)}, u32[]{:S(2)}) collective-permute-start(bf16[4,7168]{1,0:T(4,128)(2,1)S(1)} %get-tuple-element.18), channel_id=1, source_target_pairs={{0,3},{1,2},{2,1},{3,0},{4,7},{5,6},{6,5},{7,4},{8,11},{9,10},{10,... | collective-permute-start | bytes 172040 | tf_op jit(solution)/shard_map/ppermute | solution.py:81
  20.0 6.7 %collective-permute-start.4 = (bf16[16,512]{1,0:T(8,128)(2,1)S(1)}, bf16[16,512]{1,0:T(8,128)(2,1)S(1)}, u32[]{:S(2)}, u32[]{:S(2)}) collective-permute-start(bf16[16,512]{1,0:T(8,128)(2,1)S(1)} %activate.1.after.refs_0_), channel_id=1, source_target_pairs={{0,8},{4,12},{8,0},{12,4},{16,24},{20,28},{24,16},{28,20},{1,9},{5... | collective-permute-start | bytes 49160 | tf_op jit(solution)/shard_map/ppermute | solution.py:81
  21.6 5.1 %collective-permute-start.5 = (bf16[16,512]{1,0:T(8,128)(2,1)S(1)}, bf16[16,512]{1,0:T(8,128)(2,1)S(1)}, u32[]{:S(2)}, u32[]{:S(2)}) collective-permute-start(bf16[16,512]{1,0:T(8,128)(2,1)S(1)} %activate.1.after.refs_0_), channel_id=1, source_target_pairs={{0,16},{4,20},{8,24},{12,28},{16,0},{20,4},{24,8},{28,12},{1,17},{... | collective-permute-start | bytes 49160 | tf_op jit(solution)/shard_map/ppermute | solution.py:81
  24.2 5.5 %collective-permute-start.6 = (bf16[16,512]{1,0:T(8,128)(2,1)S(1)}, bf16[16,512]{1,0:T(8,128)(2,1)S(1)}, u32[]{:S(2)}, u32[]{:S(2)}) collective-permute-start(bf16[16,512]{1,0:T(8,128)(2,1)S(1)} %activate.1.after.refs_0_), channel_id=1, source_target_pairs={{0,24},{4,28},{8,16},{12,20},{16,8},{20,12},{24,0},{28,4},{1,25},{... | collective-permute-start | bytes 49160 | tf_op jit(solution)/shard_map/ppermute | solution.py:81
  26.6 20.9 %copy-start = (f32[1,4]{1,0:T(1,128)S(1)}, f32[1,4]{1,0:T(1,128)}, u32[]{:S(2)}) copy-start(f32[1,4]{1,0:T(1,128)} %param.10) | copy-start | bytes 52
  31.0 6.5 %collective-permute-start.10 = (bf16[24,3584]{1,0:T(8,128)(2,1)S(1)}, bf16[24,3584]{1,0:T(8,128)(2,1)S(1)}, u32[]{:S(2)}, u32[]{:S(2)}) collective-permute-start(bf16[24,3584]{1,0:T(8,128)(2,1)S(1)} %get-tuple-element.22), channel_id=1, source_target_pairs={{0,3},{1,2},{2,1},{3,0},{4,7},{5,6},{6,5},{7,4},{8,11},{9,10},{10,... | collective-permute-start | bytes 516104 | tf_op jit(solution)/shard_map/ppermute | solution.py:81
  31.6 6.7 %collective-permute-start.8 = (bf16[24,3584]{1,0:T(8,128)(2,1)S(1)}, bf16[24,3584]{1,0:T(8,128)(2,1)S(1)}, u32[]{:S(2)}, u32[]{:S(2)}) collective-permute-start(bf16[24,3584]{1,0:T(8,128)(2,1)S(1)} %get-tuple-element.20), channel_id=1, source_target_pairs={{0,1},{1,0},{2,3},{3,2},{4,5},{5,4},{6,7},{7,6},{8,9},{9,8},{10,11... | collective-permute-start | bytes 516104 | tf_op jit(solution)/shard_map/ppermute | solution.py:81
  33.1 6.2 %collective-permute-start.9 = (bf16[24,3584]{1,0:T(8,128)(2,1)S(1)}, bf16[24,3584]{1,0:T(8,128)(2,1)S(1)}, u32[]{:S(2)}, u32[]{:S(2)}) collective-permute-start(bf16[24,3584]{1,0:T(8,128)(2,1)S(1)} %get-tuple-element.21), channel_id=1, source_target_pairs={{0,2},{1,3},{2,0},{3,1},{4,6},{5,7},{6,4},{7,5},{8,10},{9,11},{10,... | collective-permute-start | bytes 516104 | tf_op jit(solution)/shard_map/ppermute | solution.py:81
  39.7 5.5 %collective-permute-start.11 = (bf16[4,7168]{1,0:T(4,128)(2,1)S(1)}, bf16[4,7168]{1,0:T(4,128)(2,1)S(1)}, u32[]{:S(2)}, u32[]{:S(2)}) collective-permute-start(bf16[4,7168]{1,0:T(4,128)(2,1)S(1)} %get-tuple-element.24), channel_id=1, source_target_pairs={{0,8},{4,12},{8,0},{12,4},{16,24},{20,28},{24,16},{28,20},{1,9},{5... | collective-permute-start | bytes 172040 | tf_op jit(solution)/shard_map/ppermute | solution.py:81
  39.8 5.4 %collective-permute-start.12 = (bf16[4,7168]{1,0:T(4,128)(2,1)S(1)}, bf16[4,7168]{1,0:T(4,128)(2,1)S(1)}, u32[]{:S(2)}, u32[]{:S(2)}) collective-permute-start(bf16[4,7168]{1,0:T(4,128)(2,1)S(1)} %get-tuple-element.25), channel_id=1, source_target_pairs={{0,16},{4,20},{8,24},{12,28},{16,0},{20,4},{24,8},{28,12},{1,17},{... | collective-permute-start | bytes 172040 | tf_op jit(solution)/shard_map/ppermute | solution.py:81
  41.6 6.0 %collective-permute-start.13 = (bf16[4,7168]{1,0:T(4,128)(2,1)S(1)}, bf16[4,7168]{1,0:T(4,128)(2,1)S(1)}, u32[]{:S(2)}, u32[]{:S(2)}) collective-permute-start(bf16[4,7168]{1,0:T(4,128)(2,1)S(1)} %get-tuple-element.26), channel_id=1, source_target_pairs={{0,24},{4,28},{8,16},{12,20},{16,8},{20,12},{24,0},{28,4},{1,25},{... | collective-permute-start | bytes 172040 | tf_op jit(solution)/shard_map/ppermute | solution.py:81

commit v7 on v6

--- a/solution.py
+++ b/solution.py
@@ -101,9 +101,12 @@
     return pltpu.CompilerParams(vmem_limit_bytes=mib * MIB)
 
 
-def prepare_body(shards, route_hbm, rows_hbm, gain_hbm, *refs):
-    blocks, code_ref = refs[:E_WIN], refs[E_WIN]
-    route_ref, rows_ref, gain_ref, sems = refs[E_WIN + 1 :]
+def prepare_body(shards, route_hbm, rows_hbm, gain_hbm, resident, *refs):
+    blocks, code_ref, early = refs[:E_WIN], refs[E_WIN], refs[E_WIN + 1]
+    route_ref, rows_ref, gain_ref, sems = refs[E_WIN + 2 :]
+    early_copy = pltpu.make_async_copy(
+        resident.at[:, pl.ds(0, early.shape[1])], early, sems.at[3]
+    )
     copies = [
         pltpu.make_async_copy(source, target, sems.at[index])
         for index, (source, target) in enumerate(
@@ -112,6 +115,7 @@
     ]
     for copy in copies:
         copy.start()
+    early_copy.start()
     for copy in copies:
         copy.wait()
     row_count, width = rows_ref.shape
@@ -137,10 +141,16 @@
         blocks[expert][...] = packed[expert * row_count : (expert + 1) * row_count].astype(
             jnp.bfloat16
         )
-
-
-def flag_body(owner, after, flags, owner_ref, sems):
-    owner_copy = pltpu.make_async_copy(owner, owner_ref, sems.at[0])
+    early_copy.wait()
+
+
+def ahead_body(owner, resident, after, late, flags, owner_ref, sems):
+    late_rows = late.shape[1]
+    late_copy = pltpu.make_async_copy(
+        resident.at[:, pl.ds(resident.shape[1] - late_rows, late_rows)], late, sems.at[0]
+    )
+    late_copy.start()
+    owner_copy = pltpu.make_async_copy(owner, owner_ref, sems.at[1])
     owner_copy.start()
     owner_copy.wait()
     group = lax.axis_index("grp")
@@ -151,25 +161,29 @@
             hit = jnp.where(owner_ref[0, bucket] == (group ^ which), 1.0, 0.0)
             values = jnp.where(row == which * BUCKETS + bucket, hit, values)
     flags[...] = values
-
-
-def activate_body(devices, weights, code_ref, *refs):
+    late_copy.wait()
+
+
+def activate_body(devices, early, late, code_ref, *refs):
     blocks, out, stacked = refs[:devices], refs[devices], refs[devices + 1]
+    first = early.shape[1]
     row_count = blocks[0].shape[0]
     for index in range(devices):
         stacked[index * row_count : (index + 1) * row_count, :] = blocks[index][...].astype(
             jnp.float32
         )
     rows = stacked[...].astype(jnp.bfloat16)
-    gate = lax.dot_general(weights[0], rows, NT, preferred_element_type=jnp.float32)
-    up = lax.dot_general(weights[1], rows, NT, preferred_element_type=jnp.float32)
-    act = (gate * jax.nn.sigmoid(gate) * up).T
-    spare = lax.broadcasted_iota(jnp.int32, (act.shape[0], CODE), 0) == CAP
-    out[:, :CODE] = jnp.where(spare, code_ref[0:1, :], act[:, :CODE]).astype(jnp.bfloat16)
-    out[:, CODE:] = act[:, CODE:].astype(jnp.bfloat16)
-
-
-def hold_body(own, other, after, down, sems):
+    spare = lax.broadcasted_iota(jnp.int32, (devices * row_count, CODE), 0) == CAP
+    for start, weights in ((0, early), (first, late)):
+        gate = lax.dot_general(weights[0], rows, NT, preferred_element_type=jnp.float32)
+        up = lax.dot_general(weights[1], rows, NT, preferred_element_type=jnp.float32)
+        act = (gate * jax.nn.sigmoid(gate) * up).T
+        out[:, start : start + act.shape[1]] = act.astype(jnp.bfloat16)
+    head = out[:, :CODE].astype(jnp.float32)
+    out[:, :CODE] = jnp.where(spare, code_ref[0:1, :], head).astype(jnp.bfloat16)
+
+
+def hold_body(chips, row_count, own, other, after, down, placing, sems):
     piece = own.shape[0]
     copies = [
         pltpu.make_async_copy(source, down.at[pl.ds(index * piece, piece)], sems.at[index])
@@ -177,22 +191,24 @@
     ]
     for copy in copies:
         copy.start()
+    shape = placing.shape[1:]
+    row, column = (lax.broadcasted_iota(jnp.int32, shape, axis) for axis in (0, 1))
+    block, used = 2 * CAP * chips, shape[0] // 2
+    lower, home, spot = row // used, (row % used) // block, row % block
+    slot, part, at = spot // (2 * chips), (spot % (2 * chips)) // chips, spot % chips
+    matches = (part == lower) & (home == column // row_count) & (slot == column % row_count)
+    for chip in range(chips):
+        placing[chip] = jnp.where(matches & (at == chip), 1.0, 0.0).astype(jnp.bfloat16)
     for copy in copies:
         copy.wait()
 
 
-def down_body(devices, chips, down, flags, *refs):
+def down_body(devices, chips, down, flags, placing, *refs):
     acts, partials = refs[:chips], refs[chips:]
     block, half = partials[0].shape
     used = devices * block
     rows, units = acts[0].shape
-    row_count, piece = rows // devices, units // BUCKETS
-    row = lax.broadcasted_iota(jnp.int32, (2 * used, rows), 0)
-    column = lax.broadcasted_iota(jnp.int32, (2 * used, rows), 1)
-    lower, within = row // used, row % used
-    home, spot = within // block, within % block
-    slot, part, chip_at = spot // (2 * chips), (spot % (2 * chips)) // chips, spot % chips
-    matches = (part == lower) & (home == column // row_count) & (slot == column % row_count)
+    piece = units // BUCKETS
     placed = jnp.zeros((2 * used, PAIR * piece), jnp.float32)
     for chip in range(chips):
         picked = []
@@ -203,9 +219,8 @@
                 piece_of = acts[chip][:, bucket * piece : (bucket + 1) * piece].astype(jnp.float32)
                 chosen = jnp.where(flag > 0.5, piece_of, chosen)
             picked.append(chosen.astype(jnp.bfloat16))
-        placing = jnp.where(matches & (chip_at == chip), 1.0, 0.0).astype(jnp.bfloat16)
         placed = placed + jnp.dot(
-            placing, jnp.concatenate(picked, axis=1), preferred_element_type=jnp.float32
+            placing[chip], jnp.concatenate(picked, axis=1), preferred_element_type=jnp.float32
         )
     placed = placed.astype(jnp.bfloat16)
     above, below = placed[:used], placed[used:]
@@ -221,11 +236,8 @@
             ].astype(jnp.bfloat16)
 
 
-def combine_body(devices, chips, shards, *refs):
-    acts, blocks = refs[:chips], refs[chips : chips + devices]
-    outs, codes = refs[chips + devices : -1], refs[-1]
-    block, half = blocks[0].shape
-    row_count = outs[0].shape[0]
+def place_body(chips, shards, row_count, block, *refs):
+    acts, placing, codes = refs[:chips], refs[-2], refs[-1]
     mine = lax.axis_index("exp") // shards
     diagonal = lax.broadcasted_iota(jnp.int32, (row_count, CODE), 0) == lax.broadcasted_iota(
         jnp.int32, (row_count, CODE), 1
@@ -240,21 +252,24 @@
     home = lax.broadcasted_iota(jnp.int32, code.shape, 0) // row_count
     at = lax.broadcasted_iota(jnp.int32, code.shape, 1)
     at_slot, at_part, at_chip = at // (2 * chips), (at % (2 * chips)) // chips, at % chips
-    placing = []
     for expert in range(E_WIN):
         wanted = ((mine ^ expert) * row_count + at_slot).astype(jnp.float32)
         chosen = (wanted == code) & (at_chip == home) & (at < block)
-        placing.append(
-            [
-                jnp.where(chosen & (at_part == part), 1.0, 0.0).astype(jnp.bfloat16)[:, :block]
-                for part in range(2)
-            ]
-        )
+        for part in range(2):
+            placing[2 * expert + part] = jnp.where(chosen & (at_part == part), 1.0, 0.0).astype(
+                jnp.bfloat16
+            )
+
+
+def combine_body(devices, chips, shards, placing, *refs):
+    blocks, outs = refs[:devices], refs[devices:]
+    block, half = blocks[0].shape
+    row_count = outs[0].shape[0]
     for part in range(2):
         total = 0.0
         for index in range(devices):
             total = total + jnp.dot(
-                placing[index // shards][part],
+                placing[2 * (index // shards) + part][:, :block],
                 blocks[index][...],
                 preferred_element_type=jnp.float32,
             )
@@ -279,51 +294,61 @@
     shards = devices // E_WIN
     half, block = width // 2, 2 * CAP * chips
     piece, units = own_piece.shape[0], resident.shape[1]
+    early_units = units // 8
     row_block = pltpu.VMEM((row_count, width), jnp.bfloat16)
-    *packed, code = pl.pallas_call(
+    *packed, code, early = pl.pallas_call(
         functools.partial(prepare_body, shards),
-        out_shape=[row_block] * E_WIN + [pltpu.VMEM((8, CODE), jnp.float32)],
-        in_specs=[HBM] * 3,
-        out_specs=[VMEM] * (E_WIN + 1),
+        out_shape=[row_block] * E_WIN
+        + [
+            pltpu.VMEM((8, CODE), jnp.float32),
+            pltpu.VMEM((2, early_units, width), jnp.bfloat16),
+        ],
+        in_specs=[HBM] * 4,
+        out_specs=[VMEM] * (E_WIN + 2),
         scratch_shapes=[
             pltpu.SMEM((1, row_count), jnp.int32),
             pltpu.VMEM((row_count, width), jnp.bfloat16),
             pltpu.VMEM((1, width), jnp.float32),
-            pltpu.SemaphoreType.DMA((3,)),
+            pltpu.SemaphoreType.DMA((4,)),
         ],
         compiler_params=limit(4),
         name="prepare",
-    )(*in_hbm(route.reshape(1, row_count), rows, norm_gain.reshape(1, width)))
+    )(*in_hbm(route.reshape(1, row_count), rows, norm_gain.reshape(1, width), resident))
     arrived = exchange([packed[bits // shards] for bits in range(devices)], "exp", 1)
     other_piece = swap(own_piece, "grp", 1)
-    weights = swap(resident, "grp", 0)
-    flags = pl.pallas_call(
-        flag_body,
-        out_shape=pltpu.VMEM((8, CODE), jnp.float32),
-        in_specs=[HBM, ANY],
-        out_specs=VMEM,
+    late, flags = pl.pallas_call(
+        ahead_body,
+        out_shape=[
+            pltpu.VMEM((2, units - early_units, width), jnp.bfloat16),
+            pltpu.VMEM((8, CODE), jnp.float32),
+        ],
+        in_specs=[HBM, HBM, ANY],
+        out_specs=[VMEM] * 2,
         scratch_shapes=[
             pltpu.SMEM((1, owner.shape[0]), jnp.int32),
-            pltpu.SemaphoreType.DMA((1,)),
+            pltpu.SemaphoreType.DMA((2,)),
         ],
         compiler_params=limit(2),
-        name="flag",
-    )(*in_hbm(owner.reshape(1, -1)), *held(code))
+        name="ahead",
+    )(*in_hbm(owner.reshape(1, -1), resident), *held(code))
     act = pl.pallas_call(
         functools.partial(activate_body, devices),
         out_shape=pltpu.VMEM((devices * row_count, units), jnp.bfloat16),
-        in_specs=[VMEM] * (2 + devices),
+        in_specs=[VMEM] * (3 + devices),
         out_specs=VMEM,
         scratch_shapes=[pltpu.VMEM((devices * row_count, width), jnp.float32)],
         compiler_params=limit(8),
         name="activate",
-    )(*held(weights, code, *arrived))
+    )(*held(early, late, code, *arrived))
     acts = exchange([act] * chips, "grp", PAIR)
-    down = pl.pallas_call(
-        hold_body,
-        out_shape=pltpu.VMEM((PAIR * piece, width), jnp.bfloat16),
+    down, placing = pl.pallas_call(
+        functools.partial(hold_body, chips, row_count),
+        out_shape=[
+            pltpu.VMEM((PAIR * piece, width), jnp.bfloat16),
+            pltpu.VMEM((chips, 2 * devices * block, devices * row_count), jnp.bfloat16),
+        ],
         in_specs=[HBM, ANY, ANY],
-        out_specs=VMEM,
+        out_specs=[VMEM] * 2,
         scratch_shapes=[pltpu.SemaphoreType.DMA((PAIR,))],
         compiler_params=limit(2),
         name="hold",
@@ -332,21 +357,29 @@
     partials = pl.pallas_call(
         functools.partial(down_body, devices, chips),
         out_shape=[half_block] * devices,
-        in_specs=[VMEM] * (2 + chips),
+        in_specs=[VMEM] * (3 + chips),
         out_specs=[VMEM] * devices,
         compiler_params=limit(12),
         name="down",
-    )(*held(down, flags, *acts))
+    )(*held(down, flags, placing, *acts))
     returned = exchange(partials, "exp", 1)
+    placing = pl.pallas_call(
+        functools.partial(place_body, chips, shards, row_count, block),
+        out_shape=pltpu.VMEM((2 * E_WIN, chips * row_count, CODE), jnp.bfloat16),
+        in_specs=[VMEM] * chips + [ANY],
+        out_specs=VMEM,
+        scratch_shapes=[pltpu.VMEM((chips * row_count, CODE), jnp.float32)],
+        compiler_params=limit(2),
+        name="place",
+    )(*held(*acts, partials[0]))
     sums = pl.pallas_call(
         functools.partial(combine_body, devices, chips, shards),
         out_shape=[row_block] * chips,
-        in_specs=[VMEM] * (chips + devices),
+        in_specs=[VMEM] * (1 + devices),
         out_specs=[VMEM] * chips,
-        scratch_shapes=[pltpu.VMEM((chips * row_count, CODE), jnp.float32)],
         compiler_params=limit(8),
         name="combine",
-    )(*held(*acts, *returned))
+    )(*held(placing, *returned))
     combined = 0.0
     for share in exchange(sums, "grp", PAIR):
         combined = combined + share.astype(jnp.float32)

time: 48.5 us -> 44.3 us (0.913)
  starting transfers between devices: 22.2 us -> 17 us
  Pallas kernels: 9.15 us -> 13.3 us
  waiting for transfers between devices: 16.2 us -> 13 us
    ppermute x14 -> x13, starting transfers between devices: 22.2 us -> 17 us  [swap(): return lax.ppermute(value, axis, [(i, i ^ bits) for i in range(size)])]
    pallas_call x2 -> x3, Pallas kernels: 2.21 us -> 6.28 us  [the longest x1 4.67 us: move_rows(): pl.pallas_call(ahead_body, out_shape=[pltpu.VMEM((2, units - early_units,...]
    ppermute x14 -> x13, waiting for transfers between devices: 16.2 us -> 13 us  [swap(): return lax.ppermute(value, axis, [(i, i ^ bits) for i in range(size)])]
  transfers between devices with their start and end apart: 14 -> 13, of which waited for: 9 -> 7; matrix products, arithmetic and copies ran while one was open for 0% -> 0% of each run, Pallas kernels for 15% -> 27%
where the time goes in v7:
time: 44.3 us; the launch traced here: 44.1 us
  starting transfers between devices  17 us (38%)
  Pallas kernels  13.3 us (30%)
  waiting for transfers between devices  13 us (29%)
  other arithmetic  0.71 us (2%)
    ppermute x13, starting transfers between devices, swap(): return lax.ppermute(value, axis, [(i, i ^ bits) for i in range(size)])  17 us
    ppermute x13, waiting for transfers between devices, swap(): return lax.ppermute(value, axis, [(i, i ^ bits) for i in range(size)])  13 us
    pallas_call x1, Pallas kernels, move_rows(): pl.pallas_call(ahead_body, out_shape=[pltpu.VMEM((2, units - early_units,...  4.67 us
    pallas_call x1, Pallas kernels, move_rows(): pl.pallas_call(functools.partial(activate_body, devices), out_shape=pltpu...  4.04 us
    pallas_call x1, Pallas kernels, move_rows(): pl.pallas_call(functools.partial(prepare_body, shards), out_shape=[row_bl...  1.59 us
    pallas_call x1, Pallas kernels, move_rows(): pl.pallas_call(functools.partial(hold_body, chips, row_count), out_shape=...  1.52 us
    pallas_call x1, Pallas kernels, move_rows(): pl.pallas_call(functools.partial(down_body, devices, chips), out_shape=[h...  1.03 us
  transfers between devices with their start and end apart: 13, of which 7 were waited for; matrix products, arithmetic and copies ran while one was open for 0% of the time, Pallas kernels for 27%

profile of v7, /device:TPU:0, one launch (start us, length us, event | category | flops | bytes accessed | tf_op | source)
XLA Modules:
  0.0 44.1 jit_solution(6850696849840219871)
XLA Ops:
  0.0 0.5 %collective-permute-start.6 = (bf16[128,7168]{1,0:T(8,128)(2,1)}, bf16[128,7168]{1,0:T(8,128)(2,1)S(1)}, u32[]{:S(2)}, u32[]{:S(2)}) collective-permute-start(bf16[128,7168]{1,0:T(8,128)(2,1)} %bitcast.8), channel_id=1, source_target_pairs={{0,4},{4,0},{8,12},{12,8},{16,20},{20,16},{24,28},{28,24},{1,5},{5... | collective-permute-start | bytes 5505032 | tf_op jit(solution)/shard_map/ppermute | solution.py:81
  0.5 1.6 %prepare.1 = (bf16[4,7168]{1,0:T(4,128)(2,1)S(1)}, bf16[4,7168]{1,0:T(4,128)(2,1)S(1)}, f32[8,128]{1,0:T(8,128)S(1)}, bf16[2,64,7168]{2,1,0:T(8,128)(2,1)S(1)}) custom-call(s32[1,4]{1,0:T(1,128)} %bitcast.13, bf16[4,7168]{1,0:T(4,128)(2,1)} %bitcast.10, f32[1,7168]{1,0:T(1,128)} %bitcast.11, bf16[2,512,7168]{2,1,0:T(8,128)(2,1)} %resident.3), custom_call_target="tpu_custom_call" | custom-call | tf_op jit(solution)/shard_map/prepare/pallas_call | solution.py:299
  2.1 2.5 %collective-permute-start = (bf16[4,7168]{1,0:T(4,128)(2,1)S(1)}, bf16[4,7168]{1,0:T(4,128)(2,1)S(1)}, u32[]{:S(2)}, u32[]{:S(2)}) collective-permute-start(bf16[4,7168]{1,0:T(4,128)(2,1)S(1)} %get-tuple-element.24.refs_0_), channel_id=1, source_target_pairs={{0,1},{1,0},{2,3},{3,2},{4,5},{5,4},{6,7},{7,6},{8,9},{9,8},{10,11... | collective-permute-start | bytes 172040 | tf_op jit(solution)/shard_map/ppermute | solution.py:81
  4.6 1.5 %collective-permute-start.1 = (bf16[4,7168]{1,0:T(4,128)(2,1)S(1)}, bf16[4,7168]{1,0:T(4,128)(2,1)S(1)}, u32[]{:S(2)}, u32[]{:S(2)}) collective-permute-start(bf16[4,7168]{1,0:T(4,128)(2,1)S(1)} %get-tuple-element.25), channel_id=1, source_target_pairs={{0,2},{1,3},{2,0},{3,1},{4,6},{5,7},{6,4},{7,5},{8,10},{9,11},{10,... | collective-permute-start | bytes 172040 | tf_op jit(solution)/shard_map/ppermute | solution.py:81
  6.2 0.0 collective-permute-start.2
  6.2 4.7 %ahead.1 = (bf16[2,448,7168]{2,1,0:T(8,128)(2,1)S(1)}, f32[8,128]{1,0:T(8,128)S(1)}) custom-call(s32[1,8]{1,0:T(1,128)} %bitcast.12, bf16[2,512,7168]{2,1,0:T(8,128)(2,1)} %resident.3, f32[8,128]{1,0:T(8,128)S(1)} %get-tuple-element.22.after.code_ref), custom_call_target="tpu_custom_call" | custom-call | tf_op jit(solution)/shard_map/ahead/pallas_call | solution.py:319
  10.8 0.0 collective-permute-done.refs_1_
  10.9 0.0 collective-permute-done.1.refs_2_
  10.9 0.4 collective-permute-done.2.refs_3_
  11.2 4.0 %activate.1.after.refs_0_ = bf16[16,512]{1,0:T(8,128)(2,1)S(1)} custom-call(bf16[2,64,7168]{2,1,0:T(8,128)(2,1)S(1)} %get-tuple-element.21.early, bf16[2,448,7168]{2,1,0:T(8,128)(2,1)S(1)} %get-tuple-element.23.late, f32[8,128]{1,0:T(8,128)S(1)} %get-tuple-element.22.after.code_ref, bf16[4,7168]{1,0:T(4,128)(2,1)S(1)} %get-tuple-element.24.refs_0_, ...), custom_call_target="tpu_custom_call" | custom-call | tf_op jit(solution)/shard_map/activate/pallas_call | solution.py:334
  15.3 0.0 copy-start
  15.3 1.7 %collective-permute-start.3 = (bf16[16,512]{1,0:T(8,128)(2,1)S(1)}, bf16[16,512]{1,0:T(8,128)(2,1)S(1)}, u32[]{:S(2)}, u32[]{:S(2)}) collective-permute-start(bf16[16,512]{1,0:T(8,128)(2,1)S(1)} %activate.1.after.refs_0_), channel_id=1, source_target_pairs={{0,8},{4,12},{8,0},{12,4},{16,24},{20,28},{24,16},{28,20},{1,9},{5... | collective-permute-start | bytes 49160 | tf_op jit(solution)/shard_map/ppermute | solution.py:81
  17.0 2.6 %collective-permute-start.4 = (bf16[16,512]{1,0:T(8,128)(2,1)S(1)}, bf16[16,512]{1,0:T(8,128)(2,1)S(1)}, u32[]{:S(2)}, u32[]{:S(2)}) collective-permute-start(bf16[16,512]{1,0:T(8,128)(2,1)S(1)} %activate.1.after.refs_0_), channel_id=1, source_target_pairs={{0,16},{4,20},{8,24},{12,28},{16,0},{20,4},{24,8},{28,12},{1,17},{... | collective-permute-start | bytes 49160 | tf_op jit(solution)/shard_map/ppermute | solution.py:81
  19.6 0.1 collective-permute-start.5
  19.7 0.0 collective-permute-done.6.other
  19.7 1.5 %hold.1 = (bf16[256,7168]{1,0:T(8,128)(2,1)S(1)}, bf16[4,192,16]{2,1,0:T(8,128)(2,1)S(1)}) custom-call(bf16[128,7168]{1,0:T(8,128)(2,1)} %bitcast.9, bf16[128,7168]{1,0:T(8,128)(2,1)S(1)} %collective-permute-done.6.other, bf16[16,512]{1,0:T(8,128)(2,1)S(1)} %activate.1.after.refs_0_), custom_call_target="tpu_custom_call" | custom-call | tf_op jit(solution)/shard_map/hold/pallas_call | solution.py:344
  21.2 0.0 collective-permute-done.3.refs_1_
  21.2 0.5 %collective-permute-done.4.refs_2_ = bf16[16,512]{1,0:T(8,128)(2,1)S(1)} collective-permute-done((bf16[16,512]{1,0:T(8,128)(2,1)S(1)}, bf16[16,512]{1,0:T(8,128)(2,1)S(1)}, u32[]{:S(2)}, u32[]{:S(2)}) %collective-permute-start.4) | collective-permute-done | bytes 16416 | tf_op jit(solution)/shard_map/ppermute | solution.py:81
  21.7 3.4 %collective-permute-done.5.refs_3_ = bf16[16,512]{1,0:T(8,128)(2,1)S(1)} collective-permute-done((bf16[16,512]{1,0:T(8,128)(2,1)S(1)}, bf16[16,512]{1,0:T(8,128)(2,1)S(1)}, u32[]{:S(2)}, u32[]{:S(2)}) %collective-permute-start.5) | collective-permute-done | bytes 16416 | tf_op jit(solution)/shard_map/ppermute | solution.py:81
  25.1 1.0 %down.1 = (bf16[24,3584]{1,0:T(8,128)(2,1)S(1)}, bf16[24,3584]{1,0:T(8,128)(2,1)S(1)}, bf16[24,3584]{1,0:T(8,128)(2,1)S(1)}, bf16[24,3584]{1,0:T(8,128)(2,1)S(1)}) custom-call(bf16[256,7168]{1,0:T(8,128)(2,1)S(1)} %get-tuple-element.26.down, f32[8,128]{1,0:T(8,128)S(1)} %get-tuple-element.27.flags, bf16[4,192,16]{2,1,0:T(8,128)(2,1)S(1)} %get-tuple-element.28.placing, ...), custom_call_target="tpu_custom_call" | custom-call | tf_op jit(solution)/shard_map/down/pallas_call | solution.py:357
  26.2 1.5 %collective-permute-start.7 = (bf16[24,3584]{1,0:T(8,128)(2,1)S(1)}, bf16[24,3584]{1,0:T(8,128)(2,1)S(1)}, u32[]{:S(2)}, u32[]{:S(2)}) collective-permute-start(bf16[24,3584]{1,0:T(8,128)(2,1)S(1)} %get-tuple-element.30), channel_id=1, source_target_pairs={{0,1},{1,0},{2,3},{3,2},{4,5},{5,4},{6,7},{7,6},{8,9},{9,8},{10,11... | collective-permute-start | bytes 516104 | tf_op jit(solution)/shard_map/ppermute | solution.py:81
  27.7 1.5 %collective-permute-start.8 = (bf16[24,3584]{1,0:T(8,128)(2,1)S(1)}, bf16[24,3584]{1,0:T(8,128)(2,1)S(1)}, u32[]{:S(2)}, u32[]{:S(2)}) collective-permute-start(bf16[24,3584]{1,0:T(8,128)(2,1)S(1)} %get-tuple-element.31), channel_id=1, source_target_pairs={{0,2},{1,3},{2,0},{3,1},{4,6},{5,7},{6,4},{7,5},{8,10},{9,11},{10,... | collective-permute-start | bytes 516104 | tf_op jit(solution)/shard_map/ppermute | solution.py:81
  29.2 0.5 %collective-permute-start.9 = (bf16[24,3584]{1,0:T(8,128)(2,1)S(1)}, bf16[24,3584]{1,0:T(8,128)(2,1)S(1)}, u32[]{:S(2)}, u32[]{:S(2)}) collective-permute-start(bf16[24,3584]{1,0:T(8,128)(2,1)S(1)} %get-tuple-element.32), channel_id=1, source_target_pairs={{0,3},{1,2},{2,1},{3,0},{4,7},{5,6},{6,5},{7,4},{8,11},{9,10},{10,... | collective-permute-start | bytes 516104 | tf_op jit(solution)/shard_map/ppermute | solution.py:81
  29.7 0.1 place.1.placing
  29.8 3.1 %collective-permute-done.7.refs_1_ = bf16[24,3584]{1,0:T(8,128)(2,1)S(1)} collective-permute-done((bf16[24,3584]{1,0:T(8,128)(2,1)S(1)}, bf16[24,3584]{1,0:T(8,128)(2,1)S(1)}, u32[]{:S(2)}, u32[]{:S(2)}) %collective-permute-start.7) | collective-permute-done | bytes 172064 | tf_op jit(solution)/shard_map/ppermute | solution.py:81
  33.0 3.1 %collective-permute-done.8.refs_2_ = bf16[24,3584]{1,0:T(8,128)(2,1)S(1)} collective-permute-done((bf16[24,3584]{1,0:T(8,128)(2,1)S(1)}, bf16[24,3584]{1,0:T(8,128)(2,1)S(1)}, u32[]{:S(2)}, u32[]{:S(2)}) %collective-permute-start.8) | collective-permute-done | bytes 172064 | tf_op jit(solution)/shard_map/ppermute | solution.py:81
  36.0 0.0 collective-permute-done.9.refs_3_
  36.0 0.4 combine.1
  36.4 0.7 %collective-permute-start.12 = (bf16[4,7168]{1,0:T(4,128)(2,1)S(1)}, bf16[4,7168]{1,0:T(4,128)(2,1)S(1)}, u32[]{:S(2)}, u32[]{:S(2)}) collective-permute-start(bf16[4,7168]{1,0:T(4,128)(2,1)S(1)} %get-tuple-element.36), channel_id=1, source_target_pairs={{0,24},{4,28},{8,16},{12,20},{16,8},{20,12},{24,0},{28,4},{1,25},{... | collective-permute-start | bytes 172040 | tf_op jit(solution)/shard_map/ppermute | solution.py:81
  37.1 0.0 collective-permute-start.11
  37.1 3.8 %collective-permute-start.10 = (bf16[4,7168]{1,0:T(4,128)(2,1)S(1)}, bf16[4,7168]{1,0:T(4,128)(2,1)S(1)}, u32[]{:S(2)}, u32[]{:S(2)}) collective-permute-start(bf16[4,7168]{1,0:T(4,128)(2,1)S(1)} %get-tuple-element.34), channel_id=1, source_target_pairs={{0,8},{4,12},{8,0},{12,4},{16,24},{20,28},{24,16},{28,20},{1,9},{5... | collective-permute-start | bytes 172040 | tf_op jit(solution)/shard_map/ppermute | solution.py:81
  40.9 1.7 %collective-permute-done.12 = bf16[4,7168]{1,0:T(4,128)(2,1)S(1)} collective-permute-done((bf16[4,7168]{1,0:T(4,128)(2,1)S(1)}, bf16[4,7168]{1,0:T(4,128)(2,1)S(1)}, u32[]{:S(2)}, u32[]{:S(2)}) %collective-permute-start.12) | collective-permute-done | bytes 57376 | tf_op jit(solution)/shard_map/ppermute | solution.py:81
  42.6 0.8 %collective-permute-done.11 = bf16[4,7168]{1,0:T(4,128)(2,1)S(1)} collective-permute-done((bf16[4,7168]{1,0:T(4,128)(2,1)S(1)}, bf16[4,7168]{1,0:T(4,128)(2,1)S(1)}, u32[]{:S(2)}, u32[]{:S(2)}) %collective-permute-start.11) | collective-permute-done | bytes 57376 | tf_op jit(solution)/shard_map/ppermute | solution.py:81
  43.4 0.0 collective-permute-done.10
  43.4 0.0 copy-done
  43.4 0.7 %fusion = bf16[1,4,7168]{2,1,0:T(4,128)(2,1)} fusion(bf16[4,7168]{1,0:T(4,128)(2,1)S(1)} %collective-permute-done.12, bf16[4,7168]{1,0:T(4,128)(2,1)S(1)} %collective-permute-done.11, bf16[4,7168]{1,0:T(4,128)(2,1)S(1)} %collective-permute-done.10, bf16[4,7168]{1,0:T(4,128)(2,1)S(1)} %get-tuple-element.33, f32[4]{0:T(128)S(1)} %bitcast.14), kind=kLoop, calls=%fused_computation.1 | loop fusion | flops 258048 | bytes 286736 | tf_op jit(solution)/shard_map/reshape | solution.py:387
Async XLA Ops:
  0.0 19.7 %collective-permute-start.6 = (bf16[128,7168]{1,0:T(8,128)(2,1)}, bf16[128,7168]{1,0:T(8,128)(2,1)S(1)}, u32[]{:S(2)}, u32[]{:S(2)}) collective-permute-start(bf16[128,7168]{1,0:T(8,128)(2,1)} %bitcast.8), channel_id=1, source_target_pairs={{0,4},{4,0},{8,12},{12,8},{16,20},{20,16},{24,28},{28,24},{1,5},{5... | collective-permute-start | bytes 5505032 | tf_op jit(solution)/shard_map/ppermute | solution.py:81
  2.1 8.8 %collective-permute-start = (bf16[4,7168]{1,0:T(4,128)(2,1)S(1)}, bf16[4,7168]{1,0:T(4,128)(2,1)S(1)}, u32[]{:S(2)}, u32[]{:S(2)}) collective-permute-start(bf16[4,7168]{1,0:T(4,128)(2,1)S(1)} %get-tuple-element.24.refs_0_), channel_id=1, source_target_pairs={{0,1},{1,0},{2,3},{3,2},{4,5},{5,4},{6,7},{7,6},{8,9},{9,8},{10,11... | collective-permute-start | bytes 172040 | tf_op jit(solution)/shard_map/ppermute | solution.py:81
  4.6 6.2 %collective-permute-start.1 = (bf16[4,7168]{1,0:T(4,128)(2,1)S(1)}, bf16[4,7168]{1,0:T(4,128)(2,1)S(1)}, u32[]{:S(2)}, u32[]{:S(2)}) collective-permute-start(bf16[4,7168]{1,0:T(4,128)(2,1)S(1)} %get-tuple-element.25), channel_id=1, source_target_pairs={{0,2},{1,3},{2,0},{3,1},{4,6},{5,7},{6,4},{7,5},{8,10},{9,11},{10,... | collective-permute-start | bytes 172040 | tf_op jit(solution)/shard_map/ppermute | solution.py:81
  6.2 5.1 %collective-permute-start.2 = (bf16[4,7168]{1,0:T(4,128)(2,1)S(1)}, bf16[4,7168]{1,0:T(4,128)(2,1)S(1)}, u32[]{:S(2)}, u32[]{:S(2)}) collective-permute-start(bf16[4,7168]{1,0:T(4,128)(2,1)S(1)} %get-tuple-element.25), channel_id=1, source_target_pairs={{0,3},{1,2},{2,1},{3,0},{4,7},{5,6},{6,5},{7,4},{8,11},{9,10},{10,... | collective-permute-start | bytes 172040 | tf_op jit(solution)/shard_map/ppermute | solution.py:81
  15.3 28.2 %copy-start = (f32[1,4]{1,0:T(1,128)S(1)}, f32[1,4]{1,0:T(1,128)}, u32[]{:S(2)}) copy-start(f32[1,4]{1,0:T(1,128)} %param.10) | copy-start | bytes 52
  15.3 6.0 %collective-permute-start.3 = (bf16[16,512]{1,0:T(8,128)(2,1)S(1)}, bf16[16,512]{1,0:T(8,128)(2,1)S(1)}, u32[]{:S(2)}, u32[]{:S(2)}) collective-permute-start(bf16[16,512]{1,0:T(8,128)(2,1)S(1)} %activate.1.after.refs_0_), channel_id=1, source_target_pairs={{0,8},{4,12},{8,0},{12,4},{16,24},{20,28},{24,16},{28,20},{1,9},{5... | collective-permute-start | bytes 49160 | tf_op jit(solution)/shard_map/ppermute | solution.py:81
  17.0 4.7 %collective-permute-start.4 = (bf16[16,512]{1,0:T(8,128)(2,1)S(1)}, bf16[16,512]{1,0:T(8,128)(2,1)S(1)}, u32[]{:S(2)}, u32[]{:S(2)}) collective-permute-start(bf16[16,512]{1,0:T(8,128)(2,1)S(1)} %activate.1.after.refs_0_), channel_id=1, source_target_pairs={{0,16},{4,20},{8,24},{12,28},{16,0},{20,4},{24,8},{28,12},{1,17},{... | collective-permute-start | bytes 49160 | tf_op jit(solution)/shard_map/ppermute | solution.py:81
  19.6 5.5 %collective-permute-start.5 = (bf16[16,512]{1,0:T(8,128)(2,1)S(1)}, bf16[16,512]{1,0:T(8,128)(2,1)S(1)}, u32[]{:S(2)}, u32[]{:S(2)}) collective-permute-start(bf16[16,512]{1,0:T(8,128)(2,1)S(1)} %activate.1.after.refs_0_), channel_id=1, source_target_pairs={{0,24},{4,28},{8,16},{12,20},{16,8},{20,12},{24,0},{28,4},{1,25},{... | collective-permute-start | bytes 49160 | tf_op jit(solution)/shard_map/ppermute | solution.py:81
  26.2 6.8 %collective-permute-start.7 = (bf16[24,3584]{1,0:T(8,128)(2,1)S(1)}, bf16[24,3584]{1,0:T(8,128)(2,1)S(1)}, u32[]{:S(2)}, u32[]{:S(2)}) collective-permute-start(bf16[24,3584]{1,0:T(8,128)(2,1)S(1)} %get-tuple-element.30), channel_id=1, source_target_pairs={{0,1},{1,0},{2,3},{3,2},{4,5},{5,4},{6,7},{7,6},{8,9},{9,8},{10,11... | collective-permute-start | bytes 516104 | tf_op jit(solution)/shard_map/ppermute | solution.py:81
  27.7 8.3 %collective-permute-start.8 = (bf16[24,3584]{1,0:T(8,128)(2,1)S(1)}, bf16[24,3584]{1,0:T(8,128)(2,1)S(1)}, u32[]{:S(2)}, u32[]{:S(2)}) collective-permute-start(bf16[24,3584]{1,0:T(8,128)(2,1)S(1)} %get-tuple-element.31), channel_id=1, source_target_pairs={{0,2},{1,3},{2,0},{3,1},{4,6},{5,7},{6,4},{7,5},{8,10},{9,11},{10,... | collective-permute-start | bytes 516104 | tf_op jit(solution)/shard_map/ppermute | solution.py:81
  29.2 6.8 %collective-permute-start.9 = (bf16[24,3584]{1,0:T(8,128)(2,1)S(1)}, bf16[24,3584]{1,0:T(8,128)(2,1)S(1)}, u32[]{:S(2)}, u32[]{:S(2)}) collective-permute-start(bf16[24,3584]{1,0:T(8,128)(2,1)S(1)} %get-tuple-element.32), channel_id=1, source_target_pairs={{0,3},{1,2},{2,1},{3,0},{4,7},{5,6},{6,5},{7,4},{8,11},{9,10},{10,... | collective-permute-start | bytes 516104 | tf_op jit(solution)/shard_map/ppermute | solution.py:81
  36.4 6.2 %collective-permute-start.12 = (bf16[4,7168]{1,0:T(4,128)(2,1)S(1)}, bf16[4,7168]{1,0:T(4,128)(2,1)S(1)}, u32[]{:S(2)}, u32[]{:S(2)}) collective-permute-start(bf16[4,7168]{1,0:T(4,128)(2,1)S(1)} %get-tuple-element.36), channel_id=1, source_target_pairs={{0,24},{4,28},{8,16},{12,20},{16,8},{20,12},{24,0},{28,4},{1,25},{... | collective-permute-start | bytes 172040 | tf_op jit(solution)/shard_map/ppermute | solution.py:81
  37.1 6.3 %collective-permute-start.11 = (bf16[4,7168]{1,0:T(4,128)(2,1)S(1)}, bf16[4,7168]{1,0:T(4,128)(2,1)S(1)}, u32[]{:S(2)}, u32[]{:S(2)}) collective-permute-start(bf16[4,7168]{1,0:T(4,128)(2,1)S(1)} %get-tuple-element.35), channel_id=1, source_target_pairs={{0,16},{4,20},{8,24},{12,28},{16,0},{20,4},{24,8},{28,12},{1,17},{... | collective-permute-start | bytes 172040 | tf_op jit(solution)/shard_map/ppermute | solution.py:81
  37.1 6.3 %collective-permute-start.10 = (bf16[4,7168]{1,0:T(4,128)(2,1)S(1)}, bf16[4,7168]{1,0:T(4,128)(2,1)S(1)}, u32[]{:S(2)}, u32[]{:S(2)}) collective-permute-start(bf16[4,7168]{1,0:T(4,128)(2,1)S(1)} %get-tuple-element.34), channel_id=1, source_target_pairs={{0,8},{4,12},{8,0},{12,4},{16,24},{20,28},{24,16},{28,20},{1,9},{5... | collective-permute-start | bytes 172040 | tf_op jit(solution)/shard_map/ppermute | solution.py:81

commit v8 on v7

--- a/solution.py
+++ b/solution.py
@@ -101,12 +101,9 @@
     return pltpu.CompilerParams(vmem_limit_bytes=mib * MIB)
 
 
-def prepare_body(shards, route_hbm, rows_hbm, gain_hbm, resident, *refs):
-    blocks, code_ref, early = refs[:E_WIN], refs[E_WIN], refs[E_WIN + 1]
-    route_ref, rows_ref, gain_ref, sems = refs[E_WIN + 2 :]
-    early_copy = pltpu.make_async_copy(
-        resident.at[:, pl.ds(0, early.shape[1])], early, sems.at[3]
-    )
+def prepare_body(shards, route_hbm, rows_hbm, gain_hbm, *refs):
+    blocks, code_ref = refs[:E_WIN], refs[E_WIN]
+    route_ref, rows_ref, gain_ref, sems = refs[E_WIN + 1 :]
     copies = [
         pltpu.make_async_copy(source, target, sems.at[index])
         for index, (source, target) in enumerate(
@@ -115,7 +112,6 @@
     ]
     for copy in copies:
         copy.start()
-    early_copy.start()
     for copy in copies:
         copy.wait()
     row_count, width = rows_ref.shape
@@ -141,16 +137,10 @@
         blocks[expert][...] = packed[expert * row_count : (expert + 1) * row_count].astype(
             jnp.bfloat16
         )
-    early_copy.wait()
-
-
-def ahead_body(owner, resident, after, late, flags, owner_ref, sems):
-    late_rows = late.shape[1]
-    late_copy = pltpu.make_async_copy(
-        resident.at[:, pl.ds(resident.shape[1] - late_rows, late_rows)], late, sems.at[0]
-    )
-    late_copy.start()
-    owner_copy = pltpu.make_async_copy(owner, owner_ref, sems.at[1])
+
+
+def flag_body(owner, after, flags, owner_ref, sems):
+    owner_copy = pltpu.make_async_copy(owner, owner_ref, sems.at[0])
     owner_copy.start()
     owner_copy.wait()
     group = lax.axis_index("grp")
@@ -161,26 +151,22 @@
             hit = jnp.where(owner_ref[0, bucket] == (group ^ which), 1.0, 0.0)
             values = jnp.where(row == which * BUCKETS + bucket, hit, values)
     flags[...] = values
-    late_copy.wait()
-
-
-def activate_body(devices, early, late, code_ref, *refs):
+
+
+def activate_body(devices, weights, code_ref, *refs):
     blocks, out, stacked = refs[:devices], refs[devices], refs[devices + 1]
-    first = early.shape[1]
     row_count = blocks[0].shape[0]
     for index in range(devices):
         stacked[index * row_count : (index + 1) * row_count, :] = blocks[index][...].astype(
             jnp.float32
         )
     rows = stacked[...].astype(jnp.bfloat16)
-    spare = lax.broadcasted_iota(jnp.int32, (devices * row_count, CODE), 0) == CAP
-    for start, weights in ((0, early), (first, late)):
-        gate = lax.dot_general(weights[0], rows, NT, preferred_element_type=jnp.float32)
-        up = lax.dot_general(weights[1], rows, NT, preferred_element_type=jnp.float32)
-        act = (gate * jax.nn.sigmoid(gate) * up).T
-        out[:, start : start + act.shape[1]] = act.astype(jnp.bfloat16)
-    head = out[:, :CODE].astype(jnp.float32)
-    out[:, :CODE] = jnp.where(spare, code_ref[0:1, :], head).astype(jnp.bfloat16)
+    gate = lax.dot_general(weights[0], rows, NT, preferred_element_type=jnp.float32)
+    up = lax.dot_general(weights[1], rows, NT, preferred_element_type=jnp.float32)
+    act = (gate * jax.nn.sigmoid(gate) * up).T
+    spare = lax.broadcasted_iota(jnp.int32, (act.shape[0], CODE), 0) == CAP
+    out[:, :CODE] = jnp.where(spare, code_ref[0:1, :], act[:, :CODE]).astype(jnp.bfloat16)
+    out[:, CODE:] = act[:, CODE:].astype(jnp.bfloat16)
 
 
 def hold_body(chips, row_count, own, other, after, down, placing, sems):
@@ -294,52 +280,45 @@
     shards = devices // E_WIN
     half, block = width // 2, 2 * CAP * chips
     piece, units = own_piece.shape[0], resident.shape[1]
-    early_units = units // 8
     row_block = pltpu.VMEM((row_count, width), jnp.bfloat16)
-    *packed, code, early = pl.pallas_call(
+    *packed, code = pl.pallas_call(
         functools.partial(prepare_body, shards),
-        out_shape=[row_block] * E_WIN
-        + [
-            pltpu.VMEM((8, CODE), jnp.float32),
-            pltpu.VMEM((2, early_units, width), jnp.bfloat16),
-        ],
-        in_specs=[HBM] * 4,
-        out_specs=[VMEM] * (E_WIN + 2),
+        out_shape=[row_block] * E_WIN + [pltpu.VMEM((8, CODE), jnp.float32)],
+        in_specs=[HBM] * 3,
+        out_specs=[VMEM] * (E_WIN + 1),
         scratch_shapes=[
             pltpu.SMEM((1, row_count), jnp.int32),
             pltpu.VMEM((row_count, width), jnp.bfloat16),
             pltpu.VMEM((1, width), jnp.float32),
-            pltpu.SemaphoreType.DMA((4,)),
+            pltpu.SemaphoreType.DMA((3,)),
         ],
         compiler_params=limit(4),
+        cost_estimate=pl.CostEstimate(flops=10**10, transcendentals=0, bytes_accessed=2 * 10**7),
         name="prepare",
-    )(*in_hbm(route.reshape(1, row_count), rows, norm_gain.reshape(1, width), resident))
+    )(*in_hbm(route.reshape(1, row_count), rows, norm_gain.reshape(1, width)))
     arrived = exchange([packed[bits // shards] for bits in range(devices)], "exp", 1)
     other_piece = swap(own_piece, "grp", 1)
-    late, flags = pl.pallas_call(
-        ahead_body,
-        out_shape=[
-            pltpu.VMEM((2, units - early_units, width), jnp.bfloat16),
-            pltpu.VMEM((8, CODE), jnp.float32),
-        ],
-        in_specs=[HBM, HBM, ANY],
-        out_specs=[VMEM] * 2,
+    flags = pl.pallas_call(
+        flag_body,
+        out_shape=pltpu.VMEM((8, CODE), jnp.float32),
+        in_specs=[HBM, ANY],
+        out_specs=VMEM,
         scratch_shapes=[
             pltpu.SMEM((1, owner.shape[0]), jnp.int32),
-            pltpu.SemaphoreType.DMA((2,)),
+            pltpu.SemaphoreType.DMA((1,)),
         ],
         compiler_params=limit(2),
-        name="ahead",
-    )(*in_hbm(owner.reshape(1, -1), resident), *held(code))
+        name="flag",
+    )(*in_hbm(owner.reshape(1, -1)), *held(code))
     act = pl.pallas_call(
         functools.partial(activate_body, devices),
         out_shape=pltpu.VMEM((devices * row_count, units), jnp.bfloat16),
-        in_specs=[VMEM] * (3 + devices),
+        in_specs=[VMEM] * (2 + devices),
         out_specs=VMEM,
         scratch_shapes=[pltpu.VMEM((devices * row_count, width), jnp.float32)],
-        compiler_params=limit(8),
+        compiler_params=limit(20),
         name="activate",
-    )(*held(early, late, code, *arrived))
+    )(resident, *held(code, *arrived))
     acts = exchange([act] * chips, "grp", PAIR)
     down, placing = pl.pallas_call(
         functools.partial(hold_body, chips, row_count),

time: 44.3 us -> 42.6 us (0.962)
  Pallas kernels: 13.3 us -> 9.06 us
  waiting for transfers between devices: 13 us -> 15.5 us
    pallas_call x1, Pallas kernels: 4.67 us -> 0.69 us  [move_rows(): pl.pallas_call(flag_body, out_shape=pltpu.VMEM((8, CODE), jnp.float32), i...]
    ppermute x13, waiting for transfers between devices: 13 us -> 15.5 us  [swap(): return lax.ppermute(value, axis, [(i, i ^ bits) for i in range(size)])]
  transfers between devices with their start and end apart: 13 -> 13, of which waited for: 7 -> 8; matrix products, arithmetic and copies ran while one was open for 0% -> 0% of each run, Pallas kernels for 27% -> 18%
where the time goes in v8:
time: 42.6 us; the launch traced here: 42.5 us
  starting transfers between devices  17 us (40%)
  waiting for transfers between devices  15.5 us (36%)
  Pallas kernels  9.06 us (21%)
  other arithmetic  0.71 us (2%)
    ppermute x13, starting transfers between devices, swap(): return lax.ppermute(value, axis, [(i, i ^ bits) for i in range(size)])  17 us
    ppermute x13, waiting for transfers between devices, swap(): return lax.ppermute(value, axis, [(i, i ^ bits) for i in range(size)])  15.5 us
    pallas_call x1, Pallas kernels, move_rows(): pl.pallas_call(functools.partial(activate_body, devices), out_shape=pltpu...  3.97 us
    pallas_call x1, Pallas kernels, move_rows(): pl.pallas_call(functools.partial(hold_body, chips, row_count), out_shape=...  1.52 us
    pallas_call x1, Pallas kernels, move_rows(): pl.pallas_call(functools.partial(prepare_body, shards), out_shape=[row_bl...  1.35 us
    pallas_call x1, Pallas kernels, move_rows(): pl.pallas_call(functools.partial(down_body, devices, chips), out_shape=[h...  1.03 us
  transfers between devices with their start and end apart: 13, of which 8 were waited for; matrix products, arithmetic and copies ran while one was open for 0% of the time, Pallas kernels for 18%

profile of v8, /device:TPU:0, one launch (start us, length us, event | category | flops | bytes accessed | tf_op | source)
XLA Modules:
  0.0 42.5 jit_solution(17006178916356590727)
XLA Ops:
  0.0 0.5 %collective-permute-start.6 = (bf16[128,7168]{1,0:T(8,128)(2,1)}, bf16[128,7168]{1,0:T(8,128)(2,1)S(1)}, u32[]{:S(2)}, u32[]{:S(2)}) collective-permute-start(bf16[128,7168]{1,0:T(8,128)(2,1)} %bitcast.10), channel_id=1, source_target_pairs={{0,4},{4,0},{8,12},{12,8},{16,20},{20,16},{24,28},{28,24},{1,5},{5... | collective-permute-start | bytes 5505032 | tf_op jit(solution)/shard_map/ppermute | solution.py:81
  0.5 0.0 slice-start
  0.5 0.0 slice-start.1
  0.5 0.0 slice-start.2
  0.5 0.0 slice-start.3
  0.5 1.4 %prepare.1 = (bf16[4,7168]{1,0:T(4,128)(2,1)S(1)}, bf16[4,7168]{1,0:T(4,128)(2,1)S(1)}, f32[8,128]{1,0:T(8,128)S(1)}) custom-call(s32[1,4]{1,0:T(1,128)} %bitcast.16, bf16[4,7168]{1,0:T(4,128)(2,1)} %bitcast.14, f32[1,7168]{1,0:T(1,128)} %bitcast.15), custom_call_target="tpu_custom_call" | custom-call | flops 10000000000 | bytes 20000000 | tf_op jit(solution)/shard_map/prepare/pallas_call | solution.py:284
  1.9 2.6 %collective-permute-start = (bf16[4,7168]{1,0:T(4,128)(2,1)S(1)}, bf16[4,7168]{1,0:T(4,128)(2,1)S(1)}, u32[]{:S(2)}, u32[]{:S(2)}) collective-permute-start(bf16[4,7168]{1,0:T(4,128)(2,1)S(1)} %get-tuple-element.19.refs_0_), channel_id=1, source_target_pairs={{0,1},{1,0},{2,3},{3,2},{4,5},{5,4},{6,7},{7,6},{8,9},{9,8},{10,11... | collective-permute-start | bytes 172040 | tf_op jit(solution)/shard_map/ppermute | solution.py:81
  4.4 1.5 %collective-permute-start.1 = (bf16[4,7168]{1,0:T(4,128)(2,1)S(1)}, bf16[4,7168]{1,0:T(4,128)(2,1)S(1)}, u32[]{:S(2)}, u32[]{:S(2)}) collective-permute-start(bf16[4,7168]{1,0:T(4,128)(2,1)S(1)} %get-tuple-element.20), channel_id=1, source_target_pairs={{0,2},{1,3},{2,0},{3,1},{4,6},{5,7},{6,4},{7,5},{8,10},{9,11},{10,... | collective-permute-start | bytes 172040 | tf_op jit(solution)/shard_map/ppermute | solution.py:81
  5.9 0.0 collective-permute-start.2
  6.0 1.0 %collective-permute-done.refs_1_ = bf16[4,7168]{1,0:T(4,128)(2,1)S(1)} collective-permute-done((bf16[4,7168]{1,0:T(4,128)(2,1)S(1)}, bf16[4,7168]{1,0:T(4,128)(2,1)S(1)}, u32[]{:S(2)}, u32[]{:S(2)}) %collective-permute-start) | collective-permute-done | bytes 57376 | tf_op jit(solution)/shard_map/ppermute | solution.py:81
  7.0 1.6 %collective-permute-done.1.refs_2_ = bf16[4,7168]{1,0:T(4,128)(2,1)S(1)} collective-permute-done((bf16[4,7168]{1,0:T(4,128)(2,1)S(1)}, bf16[4,7168]{1,0:T(4,128)(2,1)S(1)}, u32[]{:S(2)}, u32[]{:S(2)}) %collective-permute-start.1) | collective-permute-done | bytes 57376 | tf_op jit(solution)/shard_map/ppermute | solution.py:81
  8.6 2.4 %collective-permute-done.2.refs_3_ = bf16[4,7168]{1,0:T(4,128)(2,1)S(1)} collective-permute-done((bf16[4,7168]{1,0:T(4,128)(2,1)S(1)}, bf16[4,7168]{1,0:T(4,128)(2,1)S(1)}, u32[]{:S(2)}, u32[]{:S(2)}) %collective-permute-start.2) | collective-permute-done | bytes 57376 | tf_op jit(solution)/shard_map/ppermute | solution.py:81
  11.0 0.0 slice-done
  11.0 0.0 slice-done.1
  11.0 0.0 slice-done.2
  11.0 0.0 slice-done.3
  11.1 4.0 %activate.1.after.refs_0_ = bf16[16,512]{1,0:T(8,128)(2,1)S(1)} custom-call(bf16[2,512,7168]{2,1,0:T(8,128)(2,1)S(1)} %bitcast.9, f32[8,128]{1,0:T(8,128)S(1)} %get-tuple-element.18.code_ref.after, bf16[4,7168]{1,0:T(4,128)(2,1)S(1)} %get-tuple-element.19.refs_0_, bf16[4,7168]{1,0:T(4,128)(2,1)S(1)} %collective-permute-done.refs_1_, ...), custom_call_target="tpu_custom_call" | custom-call | tf_op jit(solution)/shard_map/activate/pallas_call | solution.py:313
  15.0 1.6 %collective-permute-start.3 = (bf16[16,512]{1,0:T(8,128)(2,1)S(1)}, bf16[16,512]{1,0:T(8,128)(2,1)S(1)}, u32[]{:S(2)}, u32[]{:S(2)}) collective-permute-start(bf16[16,512]{1,0:T(8,128)(2,1)S(1)} %activate.1.after.refs_0_), channel_id=1, source_target_pairs={{0,8},{4,12},{8,0},{12,4},{16,24},{20,28},{24,16},{28,20},{1,9},{5... | collective-permute-start | bytes 49160 | tf_op jit(solution)/shard_map/ppermute | solution.py:81
  16.6 2.6 %collective-permute-start.4 = (bf16[16,512]{1,0:T(8,128)(2,1)S(1)}, bf16[16,512]{1,0:T(8,128)(2,1)S(1)}, u32[]{:S(2)}, u32[]{:S(2)}) collective-permute-start(bf16[16,512]{1,0:T(8,128)(2,1)S(1)} %activate.1.after.refs_0_), channel_id=1, source_target_pairs={{0,16},{4,20},{8,24},{12,28},{16,0},{20,4},{24,8},{28,12},{1,17},{... | collective-permute-start | bytes 49160 | tf_op jit(solution)/shard_map/ppermute | solution.py:81
  19.2 0.2 collective-permute-start.5
  19.4 0.7 %flag.1.flags = f32[8,128]{1,0:T(8,128)S(1)} custom-call(s32[1,8]{1,0:T(1,128)} %bitcast.13, f32[8,128]{1,0:T(8,128)S(1)} %get-tuple-element.18.code_ref.after), custom_call_target="tpu_custom_call" | custom-call | tf_op jit(solution)/shard_map/flag/pallas_call | solution.py:301
  20.1 0.0 copy-start
  20.2 0.0 collective-permute-done.6.other
  20.2 1.5 %hold.1 = (bf16[256,7168]{1,0:T(8,128)(2,1)S(1)}, bf16[4,192,16]{2,1,0:T(8,128)(2,1)S(1)}) custom-call(bf16[128,7168]{1,0:T(8,128)(2,1)} %bitcast.11, bf16[128,7168]{1,0:T(8,128)(2,1)S(1)} %collective-permute-done.6.other, bf16[16,512]{1,0:T(8,128)(2,1)S(1)} %activate.1.after.refs_0_), custom_call_target="tpu_custom_call" | custom-call | tf_op jit(solution)/shard_map/hold/pallas_call | solution.py:323
  21.7 0.0 collective-permute-done.3.refs_1_
  21.7 0.0 collective-permute-done.4.refs_2_
  21.7 3.0 %collective-permute-done.5.refs_3_ = bf16[16,512]{1,0:T(8,128)(2,1)S(1)} collective-permute-done((bf16[16,512]{1,0:T(8,128)(2,1)S(1)}, bf16[16,512]{1,0:T(8,128)(2,1)S(1)}, u32[]{:S(2)}, u32[]{:S(2)}) %collective-permute-start.5) | collective-permute-done | bytes 16416 | tf_op jit(solution)/shard_map/ppermute | solution.py:81
  24.8 1.0 %down.1 = (bf16[24,3584]{1,0:T(8,128)(2,1)S(1)}, bf16[24,3584]{1,0:T(8,128)(2,1)S(1)}, bf16[24,3584]{1,0:T(8,128)(2,1)S(1)}, bf16[24,3584]{1,0:T(8,128)(2,1)S(1)}) custom-call(bf16[256,7168]{1,0:T(8,128)(2,1)S(1)} %get-tuple-element.21.down, f32[8,128]{1,0:T(8,128)S(1)} %flag.1.flags, bf16[4,192,16]{2,1,0:T(8,128)(2,1)S(1)} %get-tuple-element.22.placing, ...), custom_call_target="tpu_custom_call" | custom-call | tf_op jit(solution)/shard_map/down/pallas_call | solution.py:336
  25.8 0.6 %collective-permute-start.7 = (bf16[24,3584]{1,0:T(8,128)(2,1)S(1)}, bf16[24,3584]{1,0:T(8,128)(2,1)S(1)}, u32[]{:S(2)}, u32[]{:S(2)}) collective-permute-start(bf16[24,3584]{1,0:T(8,128)(2,1)S(1)} %get-tuple-element.24), channel_id=1, source_target_pairs={{0,1},{1,0},{2,3},{3,2},{4,5},{5,4},{6,7},{7,6},{8,9},{9,8},{10,11... | collective-permute-start | bytes 516104 | tf_op jit(solution)/shard_map/ppermute | solution.py:81
  26.4 0.5 %collective-permute-start.8 = (bf16[24,3584]{1,0:T(8,128)(2,1)S(1)}, bf16[24,3584]{1,0:T(8,128)(2,1)S(1)}, u32[]{:S(2)}, u32[]{:S(2)}) collective-permute-start(bf16[24,3584]{1,0:T(8,128)(2,1)S(1)} %get-tuple-element.25), channel_id=1, source_target_pairs={{0,2},{1,3},{2,0},{3,1},{4,6},{5,7},{6,4},{7,5},{8,10},{9,11},{10,... | collective-permute-start | bytes 516104 | tf_op jit(solution)/shard_map/ppermute | solution.py:81
  26.9 2.5 %collective-permute-start.9 = (bf16[24,3584]{1,0:T(8,128)(2,1)S(1)}, bf16[24,3584]{1,0:T(8,128)(2,1)S(1)}, u32[]{:S(2)}, u32[]{:S(2)}) collective-permute-start(bf16[24,3584]{1,0:T(8,128)(2,1)S(1)} %get-tuple-element.26), channel_id=1, source_target_pairs={{0,3},{1,2},{2,1},{3,0},{4,7},{5,6},{6,5},{7,4},{8,11},{9,10},{10,... | collective-permute-start | bytes 516104 | tf_op jit(solution)/shard_map/ppermute | solution.py:81
  29.4 0.1 place.1.placing
  29.5 1.8 %collective-permute-done.7.refs_1_ = bf16[24,3584]{1,0:T(8,128)(2,1)S(1)} collective-permute-done((bf16[24,3584]{1,0:T(8,128)(2,1)S(1)}, bf16[24,3584]{1,0:T(8,128)(2,1)S(1)}, u32[]{:S(2)}, u32[]{:S(2)}) %collective-permute-start.7) | collective-permute-done | bytes 172064 | tf_op jit(solution)/shard_map/ppermute | solution.py:81
  31.3 2.4 %collective-permute-done.8.refs_2_ = bf16[24,3584]{1,0:T(8,128)(2,1)S(1)} collective-permute-done((bf16[24,3584]{1,0:T(8,128)(2,1)S(1)}, bf16[24,3584]{1,0:T(8,128)(2,1)S(1)}, u32[]{:S(2)}, u32[]{:S(2)}) %collective-permute-start.8) | collective-permute-done | bytes 172064 | tf_op jit(solution)/shard_map/ppermute | solution.py:81
  33.7 0.0 collective-permute-done.9.refs_3_
  33.7 0.4 combine.1
  34.1 0.1 collective-permute-start.10
  34.1 1.6 %collective-permute-start.11 = (bf16[4,7168]{1,0:T(4,128)(2,1)S(1)}, bf16[4,7168]{1,0:T(4,128)(2,1)S(1)}, u32[]{:S(2)}, u32[]{:S(2)}) collective-permute-start(bf16[4,7168]{1,0:T(4,128)(2,1)S(1)} %get-tuple-element.29), channel_id=1, source_target_pairs={{0,16},{4,20},{8,24},{12,28},{16,0},{20,4},{24,8},{28,12},{1,17},{... | collective-permute-start | bytes 172040 | tf_op jit(solution)/shard_map/ppermute | solution.py:81
  35.8 2.8 %collective-permute-start.12 = (bf16[4,7168]{1,0:T(4,128)(2,1)S(1)}, bf16[4,7168]{1,0:T(4,128)(2,1)S(1)}, u32[]{:S(2)}, u32[]{:S(2)}) collective-permute-start(bf16[4,7168]{1,0:T(4,128)(2,1)S(1)} %get-tuple-element.30), channel_id=1, source_target_pairs={{0,24},{4,28},{8,16},{12,20},{16,8},{20,12},{24,0},{28,4},{1,25},{... | collective-permute-start | bytes 172040 | tf_op jit(solution)/shard_map/ppermute | solution.py:81
  38.5 0.0 collective-permute-done.10
  38.5 0.8 %collective-permute-done.11 = bf16[4,7168]{1,0:T(4,128)(2,1)S(1)} collective-permute-done((bf16[4,7168]{1,0:T(4,128)(2,1)S(1)}, bf16[4,7168]{1,0:T(4,128)(2,1)S(1)}, u32[]{:S(2)}, u32[]{:S(2)}) %collective-permute-start.11) | collective-permute-done | bytes 57376 | tf_op jit(solution)/shard_map/ppermute | solution.py:81
  39.3 2.5 %collective-permute-done.12 = bf16[4,7168]{1,0:T(4,128)(2,1)S(1)} collective-permute-done((bf16[4,7168]{1,0:T(4,128)(2,1)S(1)}, bf16[4,7168]{1,0:T(4,128)(2,1)S(1)}, u32[]{:S(2)}, u32[]{:S(2)}) %collective-permute-start.12) | collective-permute-done | bytes 57376 | tf_op jit(solution)/shard_map/ppermute | solution.py:81
  41.7 0.0 copy-done
  41.7 0.7 %fusion = bf16[1,4,7168]{2,1,0:T(4,128)(2,1)} fusion(bf16[4,7168]{1,0:T(4,128)(2,1)S(1)} %collective-permute-done.12, bf16[4,7168]{1,0:T(4,128)(2,1)S(1)} %collective-permute-done.11, bf16[4,7168]{1,0:T(4,128)(2,1)S(1)} %collective-permute-done.10, bf16[4,7168]{1,0:T(4,128)(2,1)S(1)} %get-tuple-element.27, f32[4]{0:T(128)S(1)} %bitcast.12), kind=kLoop, calls=%fused_computation.1 | loop fusion | flops 258048 | bytes 286736 | tf_op jit(solution)/shard_map/reshape | solution.py:366
  (1 shorter events, 0.0 us)
Async XLA Ops:
  0.0 20.2 %collective-permute-start.6 = (bf16[128,7168]{1,0:T(8,128)(2,1)}, bf16[128,7168]{1,0:T(8,128)(2,1)S(1)}, u32[]{:S(2)}, u32[]{:S(2)}) collective-permute-start(bf16[128,7168]{1,0:T(8,128)(2,1)} %bitcast.10), channel_id=1, source_target_pairs={{0,4},{4,0},{8,12},{12,8},{16,20},{20,16},{24,28},{28,24},{1,5},{5... | collective-permute-start | bytes 5505032 | tf_op jit(solution)/shard_map/ppermute | solution.py:81
  0.5 10.5 %slice-start = ((s8[14680064]{0:T(1024)(128)(4,1)}), s8[4194304]{0:T(1024)(128)(4,1)S(1)}, s32[]{:S(2)}) async-start(s8[14680064]{0:T(1024)(128)(4,1)} %bitcast.8), calls=%async_computation | async-start | bytes 8388608
  0.5 10.5 %slice-start.1 = ((s8[14680064]{0:T(1024)(128)(4,1)}), s8[4194304]{0:T(1024)(128)(4,1)S(1)}, s32[]{:S(2)}) async-start(s8[14680064]{0:T(1024)(128)(4,1)} %bitcast.8), calls=%async_computation.1 | async-start | bytes 8388608
  0.5 10.5 %slice-start.2 = ((s8[14680064]{0:T(1024)(128)(4,1)}), s8[4194304]{0:T(1024)(128)(4,1)S(1)}, s32[]{:S(2)}) async-start(s8[14680064]{0:T(1024)(128)(4,1)} %bitcast.8), calls=%async_computation.2 | async-start | bytes 8388608
  0.5 10.5 %slice-start.3 = ((s8[14680064]{0:T(1024)(128)(4,1)}), s8[2097152]{0:T(1024)(128)(4,1)S(1)}, s32[]{:S(2)}) async-start(s8[14680064]{0:T(1024)(128)(4,1)} %bitcast.8), calls=%async_computation.3 | async-start | bytes 4194304
  1.9 5.1 %collective-permute-start = (bf16[4,7168]{1,0:T(4,128)(2,1)S(1)}, bf16[4,7168]{1,0:T(4,128)(2,1)S(1)}, u32[]{:S(2)}, u32[]{:S(2)}) collective-permute-start(bf16[4,7168]{1,0:T(4,128)(2,1)S(1)} %get-tuple-element.19.refs_0_), channel_id=1, source_target_pairs={{0,1},{1,0},{2,3},{3,2},{4,5},{5,4},{6,7},{7,6},{8,9},{9,8},{10,11... | collective-permute-start | bytes 172040 | tf_op jit(solution)/shard_map/ppermute | solution.py:81
  4.4 4.2 %collective-permute-start.1 = (bf16[4,7168]{1,0:T(4,128)(2,1)S(1)}, bf16[4,7168]{1,0:T(4,128)(2,1)S(1)}, u32[]{:S(2)}, u32[]{:S(2)}) collective-permute-start(bf16[4,7168]{1,0:T(4,128)(2,1)S(1)} %get-tuple-element.20), channel_id=1, source_target_pairs={{0,2},{1,3},{2,0},{3,1},{4,6},{5,7},{6,4},{7,5},{8,10},{9,11},{10,... | collective-permute-start | bytes 172040 | tf_op jit(solution)/shard_map/ppermute | solution.py:81
  5.9 5.1 %collective-permute-start.2 = (bf16[4,7168]{1,0:T(4,128)(2,1)S(1)}, bf16[4,7168]{1,0:T(4,128)(2,1)S(1)}, u32[]{:S(2)}, u32[]{:S(2)}) collective-permute-start(bf16[4,7168]{1,0:T(4,128)(2,1)S(1)} %get-tuple-element.20), channel_id=1, source_target_pairs={{0,3},{1,2},{2,1},{3,0},{4,7},{5,6},{6,5},{7,4},{8,11},{9,10},{10,... | collective-permute-start | bytes 172040 | tf_op jit(solution)/shard_map/ppermute | solution.py:81
  15.0 6.7 %collective-permute-start.3 = (bf16[16,512]{1,0:T(8,128)(2,1)S(1)}, bf16[16,512]{1,0:T(8,128)(2,1)S(1)}, u32[]{:S(2)}, u32[]{:S(2)}) collective-permute-start(bf16[16,512]{1,0:T(8,128)(2,1)S(1)} %activate.1.after.refs_0_), channel_id=1, source_target_pairs={{0,8},{4,12},{8,0},{12,4},{16,24},{20,28},{24,16},{28,20},{1,9},{5... | collective-permute-start | bytes 49160 | tf_op jit(solution)/shard_map/ppermute | solution.py:81
  16.6 5.1 %collective-permute-start.4 = (bf16[16,512]{1,0:T(8,128)(2,1)S(1)}, bf16[16,512]{1,0:T(8,128)(2,1)S(1)}, u32[]{:S(2)}, u32[]{:S(2)}) collective-permute-start(bf16[16,512]{1,0:T(8,128)(2,1)S(1)} %activate.1.after.refs_0_), channel_id=1, source_target_pairs={{0,16},{4,20},{8,24},{12,28},{16,0},{20,4},{24,8},{28,12},{1,17},{... | collective-permute-start | bytes 49160 | tf_op jit(solution)/shard_map/ppermute | solution.py:81
  19.2 5.5 %collective-permute-start.5 = (bf16[16,512]{1,0:T(8,128)(2,1)S(1)}, bf16[16,512]{1,0:T(8,128)(2,1)S(1)}, u32[]{:S(2)}, u32[]{:S(2)}) collective-permute-start(bf16[16,512]{1,0:T(8,128)(2,1)S(1)} %activate.1.after.refs_0_), channel_id=1, source_target_pairs={{0,24},{4,28},{8,16},{12,20},{16,8},{20,12},{24,0},{28,4},{1,25},{... | collective-permute-start | bytes 49160 | tf_op jit(solution)/shard_map/ppermute | solution.py:81
  20.1 21.6 %copy-start = (f32[1,4]{1,0:T(1,128)S(1)}, f32[1,4]{1,0:T(1,128)}, u32[]{:S(2)}) copy-start(f32[1,4]{1,0:T(1,128)} %param.10) | copy-start | bytes 52
  25.8 5.5 %collective-permute-start.7 = (bf16[24,3584]{1,0:T(8,128)(2,1)S(1)}, bf16[24,3584]{1,0:T(8,128)(2,1)S(1)}, u32[]{:S(2)}, u32[]{:S(2)}) collective-permute-start(bf16[24,3584]{1,0:T(8,128)(2,1)S(1)} %get-tuple-element.24), channel_id=1, source_target_pairs={{0,1},{1,0},{2,3},{3,2},{4,5},{5,4},{6,7},{7,6},{8,9},{9,8},{10,11... | collective-permute-start | bytes 516104 | tf_op jit(solution)/shard_map/ppermute | solution.py:81
  26.4 7.2 %collective-permute-start.8 = (bf16[24,3584]{1,0:T(8,128)(2,1)S(1)}, bf16[24,3584]{1,0:T(8,128)(2,1)S(1)}, u32[]{:S(2)}, u32[]{:S(2)}) collective-permute-start(bf16[24,3584]{1,0:T(8,128)(2,1)S(1)} %get-tuple-element.25), channel_id=1, source_target_pairs={{0,2},{1,3},{2,0},{3,1},{4,6},{5,7},{6,4},{7,5},{8,10},{9,11},{10,... | collective-permute-start | bytes 516104 | tf_op jit(solution)/shard_map/ppermute | solution.py:81
  26.9 6.7 %collective-permute-start.9 = (bf16[24,3584]{1,0:T(8,128)(2,1)S(1)}, bf16[24,3584]{1,0:T(8,128)(2,1)S(1)}, u32[]{:S(2)}, u32[]{:S(2)}) collective-permute-start(bf16[24,3584]{1,0:T(8,128)(2,1)S(1)} %get-tuple-element.26), channel_id=1, source_target_pairs={{0,3},{1,2},{2,1},{3,0},{4,7},{5,6},{6,5},{7,4},{8,11},{9,10},{10,... | collective-permute-start | bytes 516104 | tf_op jit(solution)/shard_map/ppermute | solution.py:81
  34.1 4.5 %collective-permute-start.10 = (bf16[4,7168]{1,0:T(4,128)(2,1)S(1)}, bf16[4,7168]{1,0:T(4,128)(2,1)S(1)}, u32[]{:S(2)}, u32[]{:S(2)}) collective-permute-start(bf16[4,7168]{1,0:T(4,128)(2,1)S(1)} %get-tuple-element.28), channel_id=1, source_target_pairs={{0,8},{4,12},{8,0},{12,4},{16,24},{20,28},{24,16},{28,20},{1,9},{5... | collective-permute-start | bytes 172040 | tf_op jit(solution)/shard_map/ppermute | solution.py:81
  34.1 5.1 %collective-permute-start.11 = (bf16[4,7168]{1,0:T(4,128)(2,1)S(1)}, bf16[4,7168]{1,0:T(4,128)(2,1)S(1)}, u32[]{:S(2)}, u32[]{:S(2)}) collective-permute-start(bf16[4,7168]{1,0:T(4,128)(2,1)S(1)} %get-tuple-element.29), channel_id=1, source_target_pairs={{0,16},{4,20},{8,24},{12,28},{16,0},{20,4},{24,8},{28,12},{1,17},{... | collective-permute-start | bytes 172040 | tf_op jit(solution)/shard_map/ppermute | solution.py:81
  35.8 6.0 %collective-permute-start.12 = (bf16[4,7168]{1,0:T(4,128)(2,1)S(1)}, bf16[4,7168]{1,0:T(4,128)(2,1)S(1)}, u32[]{:S(2)}, u32[]{:S(2)}) collective-permute-start(bf16[4,7168]{1,0:T(4,128)(2,1)S(1)} %get-tuple-element.30), channel_id=1, source_target_pairs={{0,24},{4,28},{8,16},{12,20},{16,8},{20,12},{24,0},{28,4},{1,25},{... | collective-permute-start | bytes 172040 | tf_op jit(solution)/shard_map/ppermute | solution.py:81

commit v9 on v8

--- a/solution.py
+++ b/solution.py
@@ -161,9 +161,18 @@
             jnp.float32
         )
     rows = stacked[...].astype(jnp.bfloat16)
-    gate = lax.dot_general(weights[0], rows, NT, preferred_element_type=jnp.float32)
-    up = lax.dot_general(weights[1], rows, NT, preferred_element_type=jnp.float32)
-    act = (gate * jax.nn.sigmoid(gate) * up).T
+    width = rows.shape[1]
+    step = width // 4 if width % 512 == 0 else width
+    gate, up = 0.0, 0.0
+    for start in range(0, width, step):
+        part = rows[:, start : start + step]
+        gate = gate + lax.dot_general(
+            part, weights[0, :, start : start + step], NT, preferred_element_type=jnp.float32
+        )
+        up = up + lax.dot_general(
+            part, weights[1, :, start : start + step], NT, preferred_element_type=jnp.float32
+        )
+    act = gate * jax.nn.sigmoid(gate) * up
     spare = lax.broadcasted_iota(jnp.int32, (act.shape[0], CODE), 0) == CAP
     out[:, :CODE] = jnp.where(spare, code_ref[0:1, :], act[:, :CODE]).astype(jnp.bfloat16)
     out[:, CODE:] = act[:, CODE:].astype(jnp.bfloat16)

time: 42.6 us -> 42.5 us (level)
  no operation moved by 1% of the time
where the time goes in v9:
time: 42.5 us; the launch traced here: 42.4 us
  starting transfers between devices  17 us (40%)
  waiting for transfers between devices  15.5 us (36%)
  Pallas kernels  8.98 us (21%)
  other arithmetic  0.71 us (2%)
    ppermute x13, starting transfers between devices, swap(): return lax.ppermute(value, axis, [(i, i ^ bits) for i in range(size)])  17 us
    ppermute x13, waiting for transfers between devices, swap(): return lax.ppermute(value, axis, [(i, i ^ bits) for i in range(size)])  15.5 us
    pallas_call x1, Pallas kernels, move_rows(): pl.pallas_call(functools.partial(activate_body, devices), out_shape=pltpu...  3.91 us
    pallas_call x1, Pallas kernels, move_rows(): pl.pallas_call(functools.partial(hold_body, chips, row_count), out_shape=...  1.52 us
    pallas_call x1, Pallas kernels, move_rows(): pl.pallas_call(functools.partial(prepare_body, shards), out_shape=[row_bl...  1.35 us
    pallas_call x1, Pallas kernels, move_rows(): pl.pallas_call(functools.partial(down_body, devices, chips), out_shape=[h...  1.03 us
  transfers between devices with their start and end apart: 13, of which 8 were waited for; matrix products, arithmetic and copies ran while one was open for 0% of the time, Pallas kernels for 18%

profile of v9, /device:TPU:0, one launch (start us, length us, event | category | flops | bytes accessed | tf_op | source)
XLA Modules:
  0.0 42.4 jit_solution(1932723747737398755)
XLA Ops:
  0.0 0.5 %collective-permute-start.6 = (bf16[128,7168]{1,0:T(8,128)(2,1)}, bf16[128,7168]{1,0:T(8,128)(2,1)S(1)}, u32[]{:S(2)}, u32[]{:S(2)}) collective-permute-start(bf16[128,7168]{1,0:T(8,128)(2,1)} %bitcast.10), channel_id=1, source_target_pairs={{0,4},{4,0},{8,12},{12,8},{16,20},{20,16},{24,28},{28,24},{1,5},{5... | collective-permute-start | bytes 5505032 | tf_op jit(solution)/shard_map/ppermute | solution.py:81
  0.5 0.0 slice-start
  0.5 0.0 slice-start.1
  0.5 0.0 slice-start.2
  0.5 0.0 slice-start.3
  0.5 1.4 %prepare.1 = (bf16[4,7168]{1,0:T(4,128)(2,1)S(1)}, bf16[4,7168]{1,0:T(4,128)(2,1)S(1)}, f32[8,128]{1,0:T(8,128)S(1)}) custom-call(s32[1,4]{1,0:T(1,128)} %bitcast.16, bf16[4,7168]{1,0:T(4,128)(2,1)} %bitcast.14, f32[1,7168]{1,0:T(1,128)} %bitcast.15), custom_call_target="tpu_custom_call" | custom-call | flops 10000000000 | bytes 20000000 | tf_op jit(solution)/shard_map/prepare/pallas_call | solution.py:293
  1.9 2.6 %collective-permute-start = (bf16[4,7168]{1,0:T(4,128)(2,1)S(1)}, bf16[4,7168]{1,0:T(4,128)(2,1)S(1)}, u32[]{:S(2)}, u32[]{:S(2)}) collective-permute-start(bf16[4,7168]{1,0:T(4,128)(2,1)S(1)} %get-tuple-element.19.refs_0_), channel_id=1, source_target_pairs={{0,1},{1,0},{2,3},{3,2},{4,5},{5,4},{6,7},{7,6},{8,9},{9,8},{10,11... | collective-permute-start | bytes 172040 | tf_op jit(solution)/shard_map/ppermute | solution.py:81
  4.4 1.5 %collective-permute-start.1 = (bf16[4,7168]{1,0:T(4,128)(2,1)S(1)}, bf16[4,7168]{1,0:T(4,128)(2,1)S(1)}, u32[]{:S(2)}, u32[]{:S(2)}) collective-permute-start(bf16[4,7168]{1,0:T(4,128)(2,1)S(1)} %get-tuple-element.20), channel_id=1, source_target_pairs={{0,2},{1,3},{2,0},{3,1},{4,6},{5,7},{6,4},{7,5},{8,10},{9,11},{10,... | collective-permute-start | bytes 172040 | tf_op jit(solution)/shard_map/ppermute | solution.py:81
  5.9 0.0 collective-permute-start.2
  6.0 1.0 %collective-permute-done.refs_1_ = bf16[4,7168]{1,0:T(4,128)(2,1)S(1)} collective-permute-done((bf16[4,7168]{1,0:T(4,128)(2,1)S(1)}, bf16[4,7168]{1,0:T(4,128)(2,1)S(1)}, u32[]{:S(2)}, u32[]{:S(2)}) %collective-permute-start) | collective-permute-done | bytes 57376 | tf_op jit(solution)/shard_map/ppermute | solution.py:81
  7.0 1.6 %collective-permute-done.1.refs_2_ = bf16[4,7168]{1,0:T(4,128)(2,1)S(1)} collective-permute-done((bf16[4,7168]{1,0:T(4,128)(2,1)S(1)}, bf16[4,7168]{1,0:T(4,128)(2,1)S(1)}, u32[]{:S(2)}, u32[]{:S(2)}) %collective-permute-start.1) | collective-permute-done | bytes 57376 | tf_op jit(solution)/shard_map/ppermute | solution.py:81
  8.6 2.4 %collective-permute-done.2.refs_3_ = bf16[4,7168]{1,0:T(4,128)(2,1)S(1)} collective-permute-done((bf16[4,7168]{1,0:T(4,128)(2,1)S(1)}, bf16[4,7168]{1,0:T(4,128)(2,1)S(1)}, u32[]{:S(2)}, u32[]{:S(2)}) %collective-permute-start.2) | collective-permute-done | bytes 57376 | tf_op jit(solution)/shard_map/ppermute | solution.py:81
  11.0 0.0 slice-done
  11.0 0.0 slice-done.1
  11.0 0.0 slice-done.2
  11.0 0.0 slice-done.3
  11.1 3.9 %activate.1.after.refs_0_ = bf16[16,512]{1,0:T(8,128)(2,1)S(1)} custom-call(bf16[2,512,7168]{2,1,0:T(8,128)(2,1)S(1)} %bitcast.9, f32[8,128]{1,0:T(8,128)S(1)} %get-tuple-element.18.code_ref.after, bf16[4,7168]{1,0:T(4,128)(2,1)S(1)} %get-tuple-element.19.refs_0_, bf16[4,7168]{1,0:T(4,128)(2,1)S(1)} %collective-permute-done.refs_1_, ...), custom_call_target="tpu_custom_call" | custom-call | tf_op jit(solution)/shard_map/activate/pallas_call | solution.py:322
  15.0 1.6 %collective-permute-start.3 = (bf16[16,512]{1,0:T(8,128)(2,1)S(1)}, bf16[16,512]{1,0:T(8,128)(2,1)S(1)}, u32[]{:S(2)}, u32[]{:S(2)}) collective-permute-start(bf16[16,512]{1,0:T(8,128)(2,1)S(1)} %activate.1.after.refs_0_), channel_id=1, source_target_pairs={{0,8},{4,12},{8,0},{12,4},{16,24},{20,28},{24,16},{28,20},{1,9},{5... | collective-permute-start | bytes 49160 | tf_op jit(solution)/shard_map/ppermute | solution.py:81
  16.5 2.6 %collective-permute-start.4 = (bf16[16,512]{1,0:T(8,128)(2,1)S(1)}, bf16[16,512]{1,0:T(8,128)(2,1)S(1)}, u32[]{:S(2)}, u32[]{:S(2)}) collective-permute-start(bf16[16,512]{1,0:T(8,128)(2,1)S(1)} %activate.1.after.refs_0_), channel_id=1, source_target_pairs={{0,16},{4,20},{8,24},{12,28},{16,0},{20,4},{24,8},{28,12},{1,17},{... | collective-permute-start | bytes 49160 | tf_op jit(solution)/shard_map/ppermute | solution.py:81
  19.1 0.2 collective-permute-start.5
  19.4 0.7 %flag.1.flags = f32[8,128]{1,0:T(8,128)S(1)} custom-call(s32[1,8]{1,0:T(1,128)} %bitcast.13, f32[8,128]{1,0:T(8,128)S(1)} %get-tuple-element.18.code_ref.after), custom_call_target="tpu_custom_call" | custom-call | tf_op jit(solution)/shard_map/flag/pallas_call | solution.py:310
  20.1 0.0 copy-start
  20.1 0.0 collective-permute-done.6.other
  20.1 1.5 %hold.1 = (bf16[256,7168]{1,0:T(8,128)(2,1)S(1)}, bf16[4,192,16]{2,1,0:T(8,128)(2,1)S(1)}) custom-call(bf16[128,7168]{1,0:T(8,128)(2,1)} %bitcast.11, bf16[128,7168]{1,0:T(8,128)(2,1)S(1)} %collective-permute-done.6.other, bf16[16,512]{1,0:T(8,128)(2,1)S(1)} %activate.1.after.refs_0_), custom_call_target="tpu_custom_call" | custom-call | tf_op jit(solution)/shard_map/hold/pallas_call | solution.py:332
  21.6 0.0 collective-permute-done.3.refs_1_
  21.6 0.0 collective-permute-done.4.refs_2_
  21.6 3.0 %collective-permute-done.5.refs_3_ = bf16[16,512]{1,0:T(8,128)(2,1)S(1)} collective-permute-done((bf16[16,512]{1,0:T(8,128)(2,1)S(1)}, bf16[16,512]{1,0:T(8,128)(2,1)S(1)}, u32[]{:S(2)}, u32[]{:S(2)}) %collective-permute-start.5) | collective-permute-done | bytes 16416 | tf_op jit(solution)/shard_map/ppermute | solution.py:81
  24.7 1.0 %down.1 = (bf16[24,3584]{1,0:T(8,128)(2,1)S(1)}, bf16[24,3584]{1,0:T(8,128)(2,1)S(1)}, bf16[24,3584]{1,0:T(8,128)(2,1)S(1)}, bf16[24,3584]{1,0:T(8,128)(2,1)S(1)}) custom-call(bf16[256,7168]{1,0:T(8,128)(2,1)S(1)} %get-tuple-element.21.down, f32[8,128]{1,0:T(8,128)S(1)} %flag.1.flags, bf16[4,192,16]{2,1,0:T(8,128)(2,1)S(1)} %get-tuple-element.22.placing, ...), custom_call_target="tpu_custom_call" | custom-call | tf_op jit(solution)/shard_map/down/pallas_call | solution.py:345
  25.7 0.6 %collective-permute-start.7 = (bf16[24,3584]{1,0:T(8,128)(2,1)S(1)}, bf16[24,3584]{1,0:T(8,128)(2,1)S(1)}, u32[]{:S(2)}, u32[]{:S(2)}) collective-permute-start(bf16[24,3584]{1,0:T(8,128)(2,1)S(1)} %get-tuple-element.24), channel_id=1, source_target_pairs={{0,1},{1,0},{2,3},{3,2},{4,5},{5,4},{6,7},{7,6},{8,9},{9,8},{10,11... | collective-permute-start | bytes 516104 | tf_op jit(solution)/shard_map/ppermute | solution.py:81
  26.3 0.5 %collective-permute-start.8 = (bf16[24,3584]{1,0:T(8,128)(2,1)S(1)}, bf16[24,3584]{1,0:T(8,128)(2,1)S(1)}, u32[]{:S(2)}, u32[]{:S(2)}) collective-permute-start(bf16[24,3584]{1,0:T(8,128)(2,1)S(1)} %get-tuple-element.25), channel_id=1, source_target_pairs={{0,2},{1,3},{2,0},{3,1},{4,6},{5,7},{6,4},{7,5},{8,10},{9,11},{10,... | collective-permute-start | bytes 516104 | tf_op jit(solution)/shard_map/ppermute | solution.py:81
  26.8 2.5 %collective-permute-start.9 = (bf16[24,3584]{1,0:T(8,128)(2,1)S(1)}, bf16[24,3584]{1,0:T(8,128)(2,1)S(1)}, u32[]{:S(2)}, u32[]{:S(2)}) collective-permute-start(bf16[24,3584]{1,0:T(8,128)(2,1)S(1)} %get-tuple-element.26), channel_id=1, source_target_pairs={{0,3},{1,2},{2,1},{3,0},{4,7},{5,6},{6,5},{7,4},{8,11},{9,10},{10,... | collective-permute-start | bytes 516104 | tf_op jit(solution)/shard_map/ppermute | solution.py:81
  29.3 0.1 place.1.placing
  29.4 1.8 %collective-permute-done.7.refs_1_ = bf16[24,3584]{1,0:T(8,128)(2,1)S(1)} collective-permute-done((bf16[24,3584]{1,0:T(8,128)(2,1)S(1)}, bf16[24,3584]{1,0:T(8,128)(2,1)S(1)}, u32[]{:S(2)}, u32[]{:S(2)}) %collective-permute-start.7) | collective-permute-done | bytes 172064 | tf_op jit(solution)/shard_map/ppermute | solution.py:81
  31.2 2.4 %collective-permute-done.8.refs_2_ = bf16[24,3584]{1,0:T(8,128)(2,1)S(1)} collective-permute-done((bf16[24,3584]{1,0:T(8,128)(2,1)S(1)}, bf16[24,3584]{1,0:T(8,128)(2,1)S(1)}, u32[]{:S(2)}, u32[]{:S(2)}) %collective-permute-start.8) | collective-permute-done | bytes 172064 | tf_op jit(solution)/shard_map/ppermute | solution.py:81
  33.6 0.0 collective-permute-done.9.refs_3_
  33.6 0.4 combine.1
  34.0 0.1 collective-permute-start.10
  34.0 1.6 %collective-permute-start.11 = (bf16[4,7168]{1,0:T(4,128)(2,1)S(1)}, bf16[4,7168]{1,0:T(4,128)(2,1)S(1)}, u32[]{:S(2)}, u32[]{:S(2)}) collective-permute-start(bf16[4,7168]{1,0:T(4,128)(2,1)S(1)} %get-tuple-element.29), channel_id=1, source_target_pairs={{0,16},{4,20},{8,24},{12,28},{16,0},{20,4},{24,8},{28,12},{1,17},{... | collective-permute-start | bytes 172040 | tf_op jit(solution)/shard_map/ppermute | solution.py:81
  35.7 2.7 %collective-permute-start.12 = (bf16[4,7168]{1,0:T(4,128)(2,1)S(1)}, bf16[4,7168]{1,0:T(4,128)(2,1)S(1)}, u32[]{:S(2)}, u32[]{:S(2)}) collective-permute-start(bf16[4,7168]{1,0:T(4,128)(2,1)S(1)} %get-tuple-element.30), channel_id=1, source_target_pairs={{0,24},{4,28},{8,16},{12,20},{16,8},{20,12},{24,0},{28,4},{1,25},{... | collective-permute-start | bytes 172040 | tf_op jit(solution)/shard_map/ppermute | solution.py:81
  38.4 0.0 collective-permute-done.10
  38.4 0.8 %collective-permute-done.11 = bf16[4,7168]{1,0:T(4,128)(2,1)S(1)} collective-permute-done((bf16[4,7168]{1,0:T(4,128)(2,1)S(1)}, bf16[4,7168]{1,0:T(4,128)(2,1)S(1)}, u32[]{:S(2)}, u32[]{:S(2)}) %collective-permute-start.11) | collective-permute-done | bytes 57376 | tf_op jit(solution)/shard_map/ppermute | solution.py:81
  39.2 2.5 %collective-permute-done.12 = bf16[4,7168]{1,0:T(4,128)(2,1)S(1)} collective-permute-done((bf16[4,7168]{1,0:T(4,128)(2,1)S(1)}, bf16[4,7168]{1,0:T(4,128)(2,1)S(1)}, u32[]{:S(2)}, u32[]{:S(2)}) %collective-permute-start.12) | collective-permute-done | bytes 57376 | tf_op jit(solution)/shard_map/ppermute | solution.py:81
  41.7 0.0 copy-done
  41.7 0.7 %fusion = bf16[1,4,7168]{2,1,0:T(4,128)(2,1)} fusion(bf16[4,7168]{1,0:T(4,128)(2,1)S(1)} %collective-permute-done.12, bf16[4,7168]{1,0:T(4,128)(2,1)S(1)} %collective-permute-done.11, bf16[4,7168]{1,0:T(4,128)(2,1)S(1)} %collective-permute-done.10, bf16[4,7168]{1,0:T(4,128)(2,1)S(1)} %get-tuple-element.27, f32[4]{0:T(128)S(1)} %bitcast.12), kind=kLoop, calls=%fused_computation.1 | loop fusion | flops 258048 | bytes 286736 | tf_op jit(solution)/shard_map/reshape | solution.py:375
  (1 shorter events, 0.0 us)
Async XLA Ops:
  0.0 20.1 %collective-permute-start.6 = (bf16[128,7168]{1,0:T(8,128)(2,1)}, bf16[128,7168]{1,0:T(8,128)(2,1)S(1)}, u32[]{:S(2)}, u32[]{:S(2)}) collective-permute-start(bf16[128,7168]{1,0:T(8,128)(2,1)} %bitcast.10), channel_id=1, source_target_pairs={{0,4},{4,0},{8,12},{12,8},{16,20},{20,16},{24,28},{28,24},{1,5},{5... | collective-permute-start | bytes 5505032 | tf_op jit(solution)/shard_map/ppermute | solution.py:81
  0.5 10.5 %slice-start = ((s8[14680064]{0:T(1024)(128)(4,1)}), s8[4194304]{0:T(1024)(128)(4,1)S(1)}, s32[]{:S(2)}) async-start(s8[14680064]{0:T(1024)(128)(4,1)} %bitcast.8), calls=%async_computation | async-start | bytes 8388608
  0.5 10.5 %slice-start.1 = ((s8[14680064]{0:T(1024)(128)(4,1)}), s8[4194304]{0:T(1024)(128)(4,1)S(1)}, s32[]{:S(2)}) async-start(s8[14680064]{0:T(1024)(128)(4,1)} %bitcast.8), calls=%async_computation.1 | async-start | bytes 8388608
  0.5 10.5 %slice-start.2 = ((s8[14680064]{0:T(1024)(128)(4,1)}), s8[4194304]{0:T(1024)(128)(4,1)S(1)}, s32[]{:S(2)}) async-start(s8[14680064]{0:T(1024)(128)(4,1)} %bitcast.8), calls=%async_computation.2 | async-start | bytes 8388608
  0.5 10.5 %slice-start.3 = ((s8[14680064]{0:T(1024)(128)(4,1)}), s8[2097152]{0:T(1024)(128)(4,1)S(1)}, s32[]{:S(2)}) async-start(s8[14680064]{0:T(1024)(128)(4,1)} %bitcast.8), calls=%async_computation.3 | async-start | bytes 4194304
  1.9 5.1 %collective-permute-start = (bf16[4,7168]{1,0:T(4,128)(2,1)S(1)}, bf16[4,7168]{1,0:T(4,128)(2,1)S(1)}, u32[]{:S(2)}, u32[]{:S(2)}) collective-permute-start(bf16[4,7168]{1,0:T(4,128)(2,1)S(1)} %get-tuple-element.19.refs_0_), channel_id=1, source_target_pairs={{0,1},{1,0},{2,3},{3,2},{4,5},{5,4},{6,7},{7,6},{8,9},{9,8},{10,11... | collective-permute-start | bytes 172040 | tf_op jit(solution)/shard_map/ppermute | solution.py:81
  4.4 4.2 %collective-permute-start.1 = (bf16[4,7168]{1,0:T(4,128)(2,1)S(1)}, bf16[4,7168]{1,0:T(4,128)(2,1)S(1)}, u32[]{:S(2)}, u32[]{:S(2)}) collective-permute-start(bf16[4,7168]{1,0:T(4,128)(2,1)S(1)} %get-tuple-element.20), channel_id=1, source_target_pairs={{0,2},{1,3},{2,0},{3,1},{4,6},{5,7},{6,4},{7,5},{8,10},{9,11},{10,... | collective-permute-start | bytes 172040 | tf_op jit(solution)/shard_map/ppermute | solution.py:81
  5.9 5.1 %collective-permute-start.2 = (bf16[4,7168]{1,0:T(4,128)(2,1)S(1)}, bf16[4,7168]{1,0:T(4,128)(2,1)S(1)}, u32[]{:S(2)}, u32[]{:S(2)}) collective-permute-start(bf16[4,7168]{1,0:T(4,128)(2,1)S(1)} %get-tuple-element.20), channel_id=1, source_target_pairs={{0,3},{1,2},{2,1},{3,0},{4,7},{5,6},{6,5},{7,4},{8,11},{9,10},{10,... | collective-permute-start | bytes 172040 | tf_op jit(solution)/shard_map/ppermute | solution.py:81
  15.0 6.7 %collective-permute-start.3 = (bf16[16,512]{1,0:T(8,128)(2,1)S(1)}, bf16[16,512]{1,0:T(8,128)(2,1)S(1)}, u32[]{:S(2)}, u32[]{:S(2)}) collective-permute-start(bf16[16,512]{1,0:T(8,128)(2,1)S(1)} %activate.1.after.refs_0_), channel_id=1, source_target_pairs={{0,8},{4,12},{8,0},{12,4},{16,24},{20,28},{24,16},{28,20},{1,9},{5... | collective-permute-start | bytes 49160 | tf_op jit(solution)/shard_map/ppermute | solution.py:81
  16.5 5.1 %collective-permute-start.4 = (bf16[16,512]{1,0:T(8,128)(2,1)S(1)}, bf16[16,512]{1,0:T(8,128)(2,1)S(1)}, u32[]{:S(2)}, u32[]{:S(2)}) collective-permute-start(bf16[16,512]{1,0:T(8,128)(2,1)S(1)} %activate.1.after.refs_0_), channel_id=1, source_target_pairs={{0,16},{4,20},{8,24},{12,28},{16,0},{20,4},{24,8},{28,12},{1,17},{... | collective-permute-start | bytes 49160 | tf_op jit(solution)/shard_map/ppermute | solution.py:81
  19.1 5.5 %collective-permute-start.5 = (bf16[16,512]{1,0:T(8,128)(2,1)S(1)}, bf16[16,512]{1,0:T(8,128)(2,1)S(1)}, u32[]{:S(2)}, u32[]{:S(2)}) collective-permute-start(bf16[16,512]{1,0:T(8,128)(2,1)S(1)} %activate.1.after.refs_0_), channel_id=1, source_target_pairs={{0,24},{4,28},{8,16},{12,20},{16,8},{20,12},{24,0},{28,4},{1,25},{... | collective-permute-start | bytes 49160 | tf_op jit(solution)/shard_map/ppermute | solution.py:81
  20.1 21.6 %copy-start = (f32[1,4]{1,0:T(1,128)S(1)}, f32[1,4]{1,0:T(1,128)}, u32[]{:S(2)}) copy-start(f32[1,4]{1,0:T(1,128)} %param.10) | copy-start | bytes 52
  25.7 5.5 %collective-permute-start.7 = (bf16[24,3584]{1,0:T(8,128)(2,1)S(1)}, bf16[24,3584]{1,0:T(8,128)(2,1)S(1)}, u32[]{:S(2)}, u32[]{:S(2)}) collective-permute-start(bf16[24,3584]{1,0:T(8,128)(2,1)S(1)} %get-tuple-element.24), channel_id=1, source_target_pairs={{0,1},{1,0},{2,3},{3,2},{4,5},{5,4},{6,7},{7,6},{8,9},{9,8},{10,11... | collective-permute-start | bytes 516104 | tf_op jit(solution)/shard_map/ppermute | solution.py:81
  26.3 7.2 %collective-permute-start.8 = (bf16[24,3584]{1,0:T(8,128)(2,1)S(1)}, bf16[24,3584]{1,0:T(8,128)(2,1)S(1)}, u32[]{:S(2)}, u32[]{:S(2)}) collective-permute-start(bf16[24,3584]{1,0:T(8,128)(2,1)S(1)} %get-tuple-element.25), channel_id=1, source_target_pairs={{0,2},{1,3},{2,0},{3,1},{4,6},{5,7},{6,4},{7,5},{8,10},{9,11},{10,... | collective-permute-start | bytes 516104 | tf_op jit(solution)/shard_map/ppermute | solution.py:81
  26.8 6.8 %collective-permute-start.9 = (bf16[24,3584]{1,0:T(8,128)(2,1)S(1)}, bf16[24,3584]{1,0:T(8,128)(2,1)S(1)}, u32[]{:S(2)}, u32[]{:S(2)}) collective-permute-start(bf16[24,3584]{1,0:T(8,128)(2,1)S(1)} %get-tuple-element.26), channel_id=1, source_target_pairs={{0,3},{1,2},{2,1},{3,0},{4,7},{5,6},{6,5},{7,4},{8,11},{9,10},{10,... | collective-permute-start | bytes 516104 | tf_op jit(solution)/shard_map/ppermute | solution.py:81
  34.0 4.5 %collective-permute-start.10 = (bf16[4,7168]{1,0:T(4,128)(2,1)S(1)}, bf16[4,7168]{1,0:T(4,128)(2,1)S(1)}, u32[]{:S(2)}, u32[]{:S(2)}) collective-permute-start(bf16[4,7168]{1,0:T(4,128)(2,1)S(1)} %get-tuple-element.28), channel_id=1, source_target_pairs={{0,8},{4,12},{8,0},{12,4},{16,24},{20,28},{24,16},{28,20},{1,9},{5... | collective-permute-start | bytes 172040 | tf_op jit(solution)/shard_map/ppermute | solution.py:81
  34.0 5.1 %collective-permute-start.11 = (bf16[4,7168]{1,0:T(4,128)(2,1)S(1)}, bf16[4,7168]{1,0:T(4,128)(2,1)S(1)}, u32[]{:S(2)}, u32[]{:S(2)}) collective-permute-start(bf16[4,7168]{1,0:T(4,128)(2,1)S(1)} %get-tuple-element.29), channel_id=1, source_target_pairs={{0,16},{4,20},{8,24},{12,28},{16,0},{20,4},{24,8},{28,12},{1,17},{... | collective-permute-start | bytes 172040 | tf_op jit(solution)/shard_map/ppermute | solution.py:81
  35.7 6.0 %collective-permute-start.12 = (bf16[4,7168]{1,0:T(4,128)(2,1)S(1)}, bf16[4,7168]{1,0:T(4,128)(2,1)S(1)}, u32[]{:S(2)}, u32[]{:S(2)}) collective-permute-start(bf16[4,7168]{1,0:T(4,128)(2,1)S(1)} %get-tuple-element.30), channel_id=1, source_target_pairs={{0,24},{4,28},{8,16},{12,20},{16,8},{20,12},{24,0},{28,4},{1,25},{... | collective-permute-start | bytes 172040 | tf_op jit(solution)/shard_map/ppermute | solution.py:81
